TPU v7x, 32 devices: a whole 2x2x4 slice. The times are simulated.
32 devices in a mesh: dp: 8 (over y, x, core), chan: 4 (over z).
Axes of the slice: x: 2, y: 2, z: 4, core: 2. Of those that a mesh axis runs over, the one named last changes fastest.
Arguments:
- activations: bfloat16 [64, 32, 32, 512], P('dp'), may hold values from -12 to 12
- out_grads: bfloat16 [64, 32, 32, 512], P('dp', None, None, 'chan'), may hold values from -4 to 4
- weight: float32 [512, 3, 3, 512], P('dp', None, None, 'chan'), may hold values from -6 to 6
- momentum: float32 [512, 3, 3, 512], P('dp', None, None, 'chan'), may hold values from -6 to 6
Outputs:
- new_weight: float32 [512, 3, 3, 512], P('dp', None, None, 'chan')
- new_momentum: float32 [512, 3, 3, 512], P('dp', None, None, 'chan')
All inputs are finite; a program needn't handle non-finite values.
Results may differ from a plain program's by a relative error of at most 0.0003.
Values sent between devices are 32-bit elements; how exact they have to be, the bound alone decides.
No kernel may reach another device: no remote copies, remote signals or barrier semaphores. Data moves between devices by JAX's collectives and lax.ppermute only.
A program may use at most 64 MiB of HBM per device.

v0:
```python
import functools

import jax
import jax.numpy as jnp
from jax import lax
from jax.experimental import pallas as pl
from jax.experimental.pallas import tpu as pltpu
from jax.sharding import PartitionSpec as P


f32, bf16 = jnp.float32, jnp.bfloat16
SM = pl.BlockSpec(memory_space=pltpu.SMEM)
VM = pl.BlockSpec(memory_space=pltpu.VMEM)
HB = pl.BlockSpec(memory_space=pltpu.HBM)
STEPS = 8


def emit(acc, turned, outs, sem, me, cols):
    rows = turned.shape[1] // len(outs)
    for j in range(3):
        turned[j] = acc[j * cols : (j + 1) * cols, :].T
    copies = []
    for k, out in enumerate(outs):
        first = pl.multiple_of(jnp.bitwise_xor(me, k) * rows, rows)
        copies.append(pltpu.make_async_copy(turned.at[:, pl.ds(first, rows), :], out, sem.at[k]))
    for copy in copies:
        copy.start()
    for copy in copies:
        copy.wait()


def first_kernel(parts, me_ref, g_hbm, a_hbm, *rest):
    outs = rest[:parts]
    av, gt, gv, acc, turned, asem, gsem, osem = rest[parts:]
    height, batch, width, cin = av.shape
    cols = gv.shape[3]
    flat = batch * width
    step = height // STEPS
    acopy = [pltpu.make_async_copy(a_hbm.at[:, h], av.at[h], asem.at[h]) for h in range(height)]
    gcopy = [pltpu.make_async_copy(g_hbm.at[:, i * step : (i + 1) * step], gv.at[:, i * step : (i + 1) * step], gsem.at[i]) for i in range(STEPS)]
    for i in range(STEPS):
        gcopy[i].start()
        for h in range(i * step, (i + 1) * step):
            acopy[h].start()
    gt[:, 0:flat] = jnp.zeros((3 * cols, flat), bf16)
    gt[:, (height + 1) * flat : (height + 2) * flat] = jnp.zeros((3 * cols, flat), bf16)
    column = lax.broadcasted_iota(jnp.int32, (cols, flat), 1) % width
    is_last, is_first = column == width - 1, column == 0

    def prepare(i):
        gcopy[i].wait()
        for h in range(i * step, (i + 1) * step):
            g = gv[:, h].reshape(flat, cols).astype(f32).T
            here = slice((h + 1) * flat, (h + 2) * flat)
            gt[0:cols, here] = jnp.where(is_last, 0.0, pltpu.roll(g, flat - 1, 1)).astype(bf16)
            gt[cols : 2 * cols, here] = g.astype(bf16)
            gt[2 * cols : 3 * cols, here] = jnp.where(is_first, 0.0, pltpu.roll(g, 1, 1)).astype(bf16)

    prepare(0)
    for i in range(STEPS):
        for h in range(i * step, (i + 1) * step):
            acopy[h].wait()
        if i + 1 < STEPS:
            prepare(i + 1)
        rhs = av[i * step : (i + 1) * step].reshape(step * flat, cin)
        term = jnp.dot(gt[:, (i * step + 1) * flat : ((i + 1) * step + 1) * flat], rhs, preferred_element_type=f32)
        acc[...] = term if i == 0 else acc[...] + term
    emit(acc, turned, outs, osem, me_ref[0], cols)


def next_kernel(shift, parts, me_ref, gt, av, *rest):
    outs = rest[:parts]
    acc, turned, osem = rest[parts:]
    height, batch, width, cin = av.shape
    flat = batch * width
    cols = gt.shape[0] // 3
    lhs = gt[:, (1 + shift) * flat : (1 + shift + height) * flat]
    acc[...] = jnp.dot(lhs, av[...].reshape(height * flat, cin), preferred_element_type=f32)
    emit(acc, turned, outs, osem, me_ref[0], cols)


def conv_first(a, g, me, parts):
    batch, height, width, cin = a.shape
    cols = g.shape[3]
    flat = batch * width
    res = pl.pallas_call(
        functools.partial(first_kernel, parts),
        out_shape=[jax.ShapeDtypeStruct((3, cin // parts, cols), f32)] * parts
        + [pltpu.VMEM((height, batch, width, cin), bf16), pltpu.VMEM((3 * cols, (height + 2) * flat), bf16)],
        in_specs=[SM, HB, HB],
        out_specs=[HB] * parts + [VM, VM],
        scratch_shapes=[
            pltpu.VMEM((batch, height, width, cols), bf16),
            pltpu.VMEM((3 * cols, cin), f32),
            pltpu.VMEM((3, cin, cols), f32),
            pltpu.SemaphoreType.DMA((height,)),
            pltpu.SemaphoreType.DMA((STEPS,)),
            pltpu.SemaphoreType.DMA((parts,)),
        ],
        compiler_params=pltpu.CompilerParams(vmem_limit_bytes=FIRST_VMEM),
        cost_estimate=pl.CostEstimate(flops=6 * cols * cin * height * flat, bytes_accessed=2 * (a.size + g.size), transcendentals=0),
        name="conv_first",
    )(me, g, a)
    return list(res[:parts]), res[parts], res[parts + 1]


def conv_next(av, gt, me, shift, parts):
    height, batch, width, cin = av.shape
    cols = gt.shape[0] // 3
    return list(pl.pallas_call(
        functools.partial(next_kernel, shift, parts),
        out_shape=[jax.ShapeDtypeStruct((3, cin // parts, cols), f32)] * parts,
        in_specs=[SM, VM, VM],
        out_specs=[HB] * parts,
        scratch_shapes=[pltpu.VMEM((3 * cols, cin), f32), pltpu.VMEM((3, cin, cols), f32), pltpu.SemaphoreType.DMA((parts,))],
        compiler_params=pltpu.CompilerParams(vmem_limit_bytes=NEXT_VMEM),
        cost_estimate=pl.CostEstimate(flops=6 * cols * cin * height * batch * width, bytes_accessed=12 * cin * cols, transcendentals=0),
        name="conv_next",
    )(me, gt, av))


def tile_dot(acc, gt, av, tiles, lo, hi, keep):
    _, batch, width, lanes = av.shape[1:]
    flat = batch * width
    rows = gt.shape[0]
    rhs = jnp.concatenate([av[q, lo:hi].reshape((hi - lo) * flat, lanes) for q in tiles], axis=1)
    for i in range(3):
        lhs = gt[:, (lo + 2 - i) * flat : (hi + 2 - i) * flat]
        term = jnp.dot(lhs, rhs, preferred_element_type=f32)
        here = slice(i * rows, (i + 1) * rows)
        acc[here, :] = acc[here, :] + term if keep else term


def tile_emit(acc, turned, outs, sem, me, cols):
    depth = turned.shape[1] // len(outs)
    for j in range(9):
        turned[j] = acc[j * cols : (j + 1) * cols, :].T
    copies = []
    for k, out in enumerate(outs):
        core = jnp.bitwise_xor(jnp.bitwise_and(me, 1), k % 2)
        first = pl.multiple_of((k // 2) * 2 * depth + core * depth, depth)
        copies.append(pltpu.make_async_copy(turned.at[:, pl.ds(first, depth), :], out, sem.at[k]))
    for copy in copies:
        copy.start()
    for copy in copies:
        copy.wait()


def near_kernel(bounds, me_ref, g_hbm, a_hbm, *rest):
    outs = rest[:4]
    av, gt, gv, acc, turned, asem, bsem, gsem, osem = rest[4:]
    _, height, batch, width, lanes = av.shape
    cols = gv.shape[3]
    flat = batch * width
    me = me_ref[0]
    chip = me // 2

    def fetch(q, h, sem):
        first = pl.multiple_of(jnp.bitwise_xor(chip, q) * lanes, lanes)
        return pltpu.make_async_copy(a_hbm.at[:, h, :, pl.ds(first, lanes)], av.at[q, h], sem)

    gcopy = pltpu.make_async_copy(g_hbm, gv, gsem.at[0])
    near = [[fetch(q, h, asem.at[q - 1, h]) for q in (1, 2)] for h in range(height)]
    far = [[fetch(q, h, bsem.at[q // 3, h]) for q in (3, 0)] for h in range(height)]
    gcopy.start()
    for pair in near + far:
        for copy in pair:
            copy.start()
    gt[:, 0:flat] = jnp.zeros((3 * cols, flat), bf16)
    gt[:, (height + 1) * flat : (height + 2) * flat] = jnp.zeros((3 * cols, flat), bf16)
    column = lax.broadcasted_iota(jnp.int32, (cols, flat), 1) % width
    is_last, is_first = column == width - 1, column == 0

    def prepare(lo, hi):
        for h in range(lo, hi):
            g = gv[:, h].reshape(flat, cols).astype(f32).T
            here = slice((h + 1) * flat, (h + 2) * flat)
            gt[0:cols, here] = jnp.where(is_last, 0.0, pltpu.roll(g, flat - 1, 1)).astype(bf16)
            gt[cols : 2 * cols, here] = g.astype(bf16)
            gt[2 * cols : 3 * cols, here] = jnp.where(is_first, 0.0, pltpu.roll(g, 1, 1)).astype(bf16)

    gcopy.wait()
    prepare(0, bounds[1] + 1)
    for i in range(len(bounds) - 1):
        lo, hi = bounds[i], bounds[i + 1]
        for h in range(lo, hi):
            for copy in near[h]:
                copy.wait()
        if i + 2 < len(bounds):
            prepare(hi + 1, min(bounds[i + 2] + 1, height))
        tile_dot(acc, gt, av, (1, 2), lo, hi, i > 0)
    tile_emit(acc, turned, outs, osem, me, cols)
    for pair in far:
        for copy in pair:
            copy.wait()


def far_kernel(me_ref, gt, av, *rest):
    outs = rest[:4]
    acc, turned, osem = rest[4:]
    tile_dot(acc, gt, av, (3, 0), 0, av.shape[1], False)
    tile_emit(acc, turned, outs, osem, me_ref[0], gt.shape[0] // 3)


def near_blocks(a, g, me):
    batch, height, width, cin = a.shape
    cols = g.shape[3]
    lanes, flat = cin // 4, batch * width
    block = jax.ShapeDtypeStruct((9, lanes // 2, cols), f32)
    res = pl.pallas_call(
        functools.partial(near_kernel, [0, height // 8, height // 2, height]),
        out_shape=[block] * 4 + [pltpu.VMEM((4, height, batch, width, lanes), bf16), pltpu.VMEM((3 * cols, (height + 2) * flat), bf16)],
        in_specs=[SM, HB, HB],
        out_specs=[HB] * 4 + [VM, VM],
        scratch_shapes=[
            pltpu.VMEM((batch, height, width, cols), bf16),
            pltpu.VMEM((9 * cols, 2 * lanes), f32),
            pltpu.VMEM((9, 2 * lanes, cols), f32),
            pltpu.SemaphoreType.DMA((2, height)),
            pltpu.SemaphoreType.DMA((2, height)),
            pltpu.SemaphoreType.DMA((1,)),
            pltpu.SemaphoreType.DMA((4,)),
        ],
        compiler_params=pltpu.CompilerParams(vmem_limit_bytes=NEAR_VMEM),
        cost_estimate=pl.CostEstimate(flops=36 * cols * lanes * height * flat, bytes_accessed=2 * (a.size + g.size), transcendentals=0),
        name="conv_near",
    )(me, g, a)
    return list(res[:4]), res[4], res[5]


def far_blocks(av, gt, me):
    _, height, batch, width, lanes = av.shape
    cols = gt.shape[0] // 3
    block = jax.ShapeDtypeStruct((9, lanes // 2, cols), f32)
    return list(pl.pallas_call(
        far_kernel,
        out_shape=[block] * 4,
        in_specs=[SM, VM, VM],
        out_specs=[HB] * 4,
        scratch_shapes=[pltpu.VMEM((9 * cols, 2 * lanes), f32), pltpu.VMEM((9, 2 * lanes, cols), f32), pltpu.SemaphoreType.DMA((4,))],
        compiler_params=pltpu.CompilerParams(vmem_limit_bytes=NEXT_VMEM),
        cost_estimate=pl.CostEstimate(flops=36 * cols * lanes * height * batch * width, bytes_accessed=72 * lanes * cols, transcendentals=0),
        name="conv_far",
    )(me, gt, av))


def gram_kernel(pairs, parts, devices, me_ref, *rest):
    blocks, out, rowsums = rest[:-2], rest[-2], rest[-1]
    chunks = len(blocks) // parts
    before = blocks[chunks * parts :]
    me = me_ref[0]
    taps, depth, cols = blocks[0].shape
    rowsums[...] = jnp.zeros_like(rowsums)
    for first in range(0, len(pairs), 18):
        some = pairs[first : first + 18]
        names = sorted({n for pair in some for n in pair})
        sums = [jnp.zeros((8, cols), f32) for _ in some]
        for c in range(chunks):
            def body(i, sums):
                tap, r = i // (depth // 8), i % (depth // 8)
                x = {k: blocks[c * parts + k][tap, pl.ds(pl.multiple_of(r * 8, 8), 8), :] for k in names}
                return [s + x[k] * x[l] for s, (k, l) in zip(sums, some)]

            sums = lax.fori_loop(0, taps * depth // 8, body, sums, unroll=4)
        for s, (k, l) in zip(sums, some):
            rowsums[k * parts + l : k * parts + l + 1, :] = jnp.sum(s, axis=0, keepdims=True)
    number = lax.broadcasted_iota(jnp.int32, (parts * parts, 128), 0)
    a, b = jnp.bitwise_xor(number // parts, me), jnp.bitwise_xor(number % parts, me)
    at = jnp.minimum(a, b) * parts + jnp.maximum(a, b)
    place = lax.broadcasted_iota(jnp.int32, (parts * parts, 128), 1)
    values = jnp.sum(rowsums[...], axis=1, keepdims=True)
    for r in range(out.shape[-2]):
        total = jnp.sum(jnp.where(at == place + r * 128, values, 0.0), axis=0, keepdims=True)
        for part in before:
            total = total + part[r : r + 1, :]
        for n in range(max(devices, 1)):
            if devices:
                out[n, r : r + 1, :] = total
            else:
                out[r : r + 1, :] = total


def gram(chunks, pairs, before, me, devices):
    parts = len(chunks[0])
    rows = -(-parts * parts // 128)
    shape = (devices, rows, 128) if devices else (rows, 128)
    flat = [b for chunk in chunks for b in chunk]
    return pl.pallas_call(
        functools.partial(gram_kernel, pairs, parts, devices),
        out_shape=jax.ShapeDtypeStruct(shape, f32),
        in_specs=[SM] + [VM] * (len(flat) + len(before)),
        out_specs=VM,
        scratch_shapes=[pltpu.VMEM((parts * parts, flat[0].shape[2]), f32)],
        compiler_params=pltpu.CompilerParams(vmem_limit_bytes=NEXT_VMEM),
        cost_estimate=pl.CostEstimate(flops=2 * flat[0].size * len(chunks) * len(pairs), bytes_accessed=4 * flat[0].size * len(flat), transcendentals=0),
        name="gram",
    )(me, *flat, *before)


def mixes_of(sums, parts):
    rows = sums.shape[0]
    place = lax.broadcasted_iota(jnp.int32, (rows, 128), 0) * 128 + lax.broadcasted_iota(jnp.int32, (rows, 128), 1)
    g = {}
    for a in range(parts):
        for b in range(a, parts):
            g[a, b] = g[b, a] = jnp.sum(jnp.where(place == a * parts + b, sums, 0.0), axis=(0, 1), keepdims=True)
    factors = [None] * parts
    count, width = parts, 1
    while count > 1:
        coef = []
        for k in range(count // 2):
            p, qa, qb = g[2 * k, 2 * k + 1], g[2 * k, 2 * k] + 1e-6, g[2 * k + 1, 2 * k + 1] + 1e-6
            coef += [1.0 - p / (2.0 * qa), 1.0 - p / (2.0 * qb)]
        for r in range(parts):
            c = coef[r // width]
            factors[r] = c if factors[r] is None else factors[r] * c
        count, width = count // 2, width * 2
        new = {}
        for k in range(count):
            for l in range(k, count):
                new[k, l] = new[l, k] = sum(coef[x] * coef[y] * g[x, y] for x in (2 * k, 2 * k + 1) for y in (2 * l, 2 * l + 1))
        g = new
    return factors


def final_kernel(parts, me_ref, sums, weight, momentum, *rest):
    blocks, (new_weight, new_momentum) = rest[:-2], rest[-2:]
    me = me_ref[0]
    total = jnp.sum(sums[...], axis=0)
    factors = mixes_of(total, parts)
    mine = []
    for k in range(parts):
        at = jnp.bitwise_xor(me, k)
        pick = factors[0]
        for r in range(1, parts):
            pick = jnp.where(at == r, factors[r], pick)
        mine.append(pick)
    taps = blocks[0].shape[0]
    for n in range(weight.shape[0]):
        value = 0.9 * momentum[n]
        for k in range(parts):
            value = value + mine[k] * blocks[n // taps * parts + k][n % taps]
        new_momentum[n] = value
        new_weight[n] = weight[n] - 0.1 * value


def finish(sums, weight, momentum, chunks, me):
    parts = len(chunks[0])
    depth, cols = weight.shape[0], weight.shape[3]
    w = jnp.transpose(weight, (1, 2, 0, 3)).reshape(9, depth, cols)
    m = jnp.transpose(momentum, (1, 2, 0, 3)).reshape(9, depth, cols)
    flat = [b for chunk in chunks for b in chunk]
    outs = pl.pallas_call(
        functools.partial(final_kernel, parts),
        out_shape=[jax.ShapeDtypeStruct(w.shape, f32)] * 2,
        in_specs=[SM] + [VM] * (3 + len(flat)),
        out_specs=[VM, VM],
        compiler_params=pltpu.CompilerParams(vmem_limit_bytes=NEXT_VMEM),
        cost_estimate=pl.CostEstimate(flops=2 * w.size * parts, bytes_accessed=4 * w.size * (parts + 4), transcendentals=0),
        name="final",
    )(me, sums, w, m, *flat)
    return tuple(jnp.transpose(x.reshape(3, 3, depth, cols), (2, 0, 1, 3)) for x in outs)


def upper_pairs(parts):
    return [(k, l) for k in range(parts) for l in range(k, parts)]


def send(block, k, parts):
    return lax.ppermute(block, "dp", [(r, r ^ k) for r in range(parts)])


def by_rows(activations, out_grads, me, parts):
    def exchange(blocks):
        return blocks[:1] + [send(blocks[k], k, parts) for k in range(1, parts)]

    middle, av, gt = conv_first(activations, out_grads, me, parts)
    middle = exchange(middle)
    lower = exchange(conv_next(av, gt, me, 1, parts))
    upper = exchange(conv_next(av, gt, me, -1, parts))
    return [lower, middle, upper], upper_pairs(parts), []


def by_chips(activations, out_grads, me, parts):
    near, av, gt = near_blocks(activations, out_grads, me)
    near = [send(near[k - 2], k, parts) for k in range(2, 6)]
    far = far_blocks(av, gt, me)
    far = [send(far[k], 6 + k, parts) for k in range(2)] + [far[2], send(far[3], 1, parts)]
    blocks = far[2:] + near
    early = [pair for pair in upper_pairs(parts) if pair[1] < 6]
    partial = gram([blocks + [blocks[0]] * 2], early, [], me, 0)
    blocks = blocks + far[:2]
    return [blocks], [pair for pair in upper_pairs(parts) if pair[1] >= 6], [partial]


def shards(activations, out_grads, weight, momentum):
    parts = lax.axis_size("dp")
    devices = parts * lax.axis_size("chan")
    me = lax.axis_index("dp").reshape(1).astype(jnp.int32)
    four = parts == 8 and activations.shape[3] % 512 == 0
    chunks, pairs, before = (by_chips if four else by_rows)(activations, out_grads, me, parts)
    sums = gram(chunks, pairs, before, me, devices)
    sums = lax.all_to_all(sums, ("dp", "chan"), split_axis=0, concat_axis=0, tiled=True)
    return finish(sums, weight, momentum, chunks, me)


FIRST_VMEM, NEXT_VMEM, NEAR_VMEM = 30 << 20, 30 << 20, 46 << 20


def solution(mesh):
    in_specs = (
        P("dp", None, None, None),
        P("dp", None, None, "chan"),
        P("dp", None, None, "chan"),
        P("dp", None, None, "chan"),
    )
    out_specs = (P("dp", None, None, "chan"), P("dp", None, None, "chan"))
    return jax.shard_map(shards, mesh=mesh, in_specs=in_specs, out_specs=out_specs, check_vma=False)
```

profile of v0, /device:TPU:0, one launch (start us, length us, event | category | flops | bytes accessed | tf_op | source)
XLA Modules:
  0.0 71.5 jit_solution(14516044194009847824)
XLA Ops:
  0.6 11.4 %conv_near.1 = (f32[9,64,128]{2,1,0:T(8,128)}, f32[9,64,128]{2,1,0:T(8,128)}, f32[9,64,128]{2,1,0:T(8,128)}, f32[9,64,128]{2,1,0:T(8,128)}, bf16[4,32,8,32,128]{...) custom-call(s32[1]{0:T(128)} %bitcast.me_ref, bf16[8,32,32,128]{3,2,1,0:T(8,128)(2,1)} %g_hbm.1, ...), custom_call_target="tpu_custom_call" | custom-call | flops 4831838208 | bytes 10485760 | tf_op jit(solution)/shard_map/conv_near/pallas_call | solution.py:210
  12.0 0.0 copy-start.2
  12.0 3.2 %copy-done.2 = bf16[4,32,8,32,128]{4,3,2,1,0:T(8,128)(2,1)} copy-done((bf16[4,32,8,32,128]{4,3,2,1,0:T(8,128)(2,1)}, bf16[4,32,8,32,128]{4,3,2,1,0:T(8,128)(2,1)S(1)}, u32[]{:S(2)}) %copy-start.2) | copy-done | bytes 8388632
  15.2 0.0 copy-start.3
  15.2 3.4 %copy-done.3 = bf16[4,32,8,32,128]{4,3,2,1,0:T(8,128)(2,1)S(1)} copy-done((bf16[4,32,8,32,128]{4,3,2,1,0:T(8,128)(2,1)S(1)}, bf16[4,32,8,32,128]{4,3,2,1,0:T(8,128)(2,1)}, u32[]{:S(2)}) %copy-start.3) | copy-done | bytes 8388632
  18.6 0.0 copy-start.7
  18.6 0.0 copy-start.6
  18.6 0.0 copy-start.5
  18.6 0.0 copy-start.4
  18.6 0.0 copy-start
  18.6 0.0 copy-start.1
  18.6 5.4 %conv_far.1 = (f32[9,64,128]{2,1,0:T(8,128)S(1)}, f32[9,64,128]{2,1,0:T(8,128)S(1)}, f32[9,64,128]{2,1,0:T(8,128)S(1)}, f32[9,64,128]{2,1,0:T(8,128)S(1)}) custom-call(s32[1]{0:T(128)} %bitcast.me_ref, bf16[384,8704]{1,0:T(8,128)(2,1)S(1)} %get-tuple-element.14.gt, bf16[4,32,8,32,128]{4,3,2,1,0:T(8,128)(2,1)S(1)} %copy-done.3), custom_call_target="tpu_custom_call" | custom-call | flops 4831838208 | bytes 1179648 | tf_op jit(solution)/shard_map/conv_far/pallas_call | solution.py:235
  24.0 0.6 collective-permute-start
  24.6 0.0 copy-done.7
  24.6 2.6 %collective-permute-start.1 = (f32[9,64,128]{2,1,0:T(8,128)S(1)}, f32[9,64,128]{2,1,0:T(8,128)S(1)}, u32[]{:S(2)}, u32[]{:S(2)}) collective-permute-start(f32[9,64,128]{2,1,0:T(8,128)S(1)} %copy-done.7), channel_id=1, source_target_pairs={{0,8},{4,12},{8,0},{12,4},{16,24},{20,28},{24,16},{28,20},{1,9},{5... | collective-permute-start | bytes 884744 | tf_op jit(solution)/shard_map/ppermute | solution.py:370
  27.1 0.0 copy-done.6
  27.1 0.1 collective-permute-start.2
  27.2 0.0 copy-done.5
  27.2 1.7 %collective-permute-start.3 = (f32[9,64,128]{2,1,0:T(8,128)S(1)}, f32[9,64,128]{2,1,0:T(8,128)S(1)}, u32[]{:S(2)}, u32[]{:S(2)}) collective-permute-start(f32[9,64,128]{2,1,0:T(8,128)S(1)} %copy-done.5), channel_id=1, source_target_pairs={{0,16},{4,20},{8,24},{12,28},{16,0},{20,4},{24,8},{28,12},{1,17},{... | collective-permute-start | bytes 884744 | tf_op jit(solution)/shard_map/ppermute | solution.py:370
  28.9 0.0 copy-done.4
  28.9 0.0 collective-permute-start.4
  29.0 0.0 collective-permute-done.rest_1_
  29.0 2.6 %collective-permute-start.5 = (f32[9,64,128]{2,1,0:T(8,128)S(1)}, f32[9,64,128]{2,1,0:T(8,128)S(1)}, u32[]{:S(2)}, u32[]{:S(2)}) collective-permute-start(f32[9,64,128]{2,1,0:T(8,128)S(1)} %get-tuple-element.22), channel_id=1, source_target_pairs={{0,24},{4,28},{8,16},{12,20},{16,8},{20,12},{24,0},{28,4},{1,25},{... | collective-permute-start | bytes 884744 | tf_op jit(solution)/shard_map/ppermute | solution.py:370
  31.6 3.4 %collective-permute-done.1.rest_2_ = f32[9,64,128]{2,1,0:T(8,128)S(1)} collective-permute-done((f32[9,64,128]{2,1,0:T(8,128)S(1)}, f32[9,64,128]{2,1,0:T(8,128)S(1)}, u32[]{:S(2)}, u32[]{:S(2)}) %collective-permute-start.1) | collective-permute-done | bytes 294944 | tf_op jit(solution)/shard_map/ppermute | solution.py:370
  35.0 1.6 %collective-permute-start.6 = (f32[9,64,128]{2,1,0:T(8,128)S(1)}, f32[9,64,128]{2,1,0:T(8,128)S(1)}, u32[]{:S(2)}, u32[]{:S(2)}) collective-permute-start(f32[9,64,128]{2,1,0:T(8,128)S(1)} %get-tuple-element.23), channel_id=1, source_target_pairs={{0,28},{4,24},{8,20},{12,16},{16,12},{20,8},{24,4},{28,0},{1,29},{... | collective-permute-start | bytes 884744 | tf_op jit(solution)/shard_map/ppermute | solution.py:370
  36.6 4.3 %collective-permute-done.2.rest_3_ = f32[9,64,128]{2,1,0:T(8,128)S(1)} collective-permute-done((f32[9,64,128]{2,1,0:T(8,128)S(1)}, f32[9,64,128]{2,1,0:T(8,128)S(1)}, u32[]{:S(2)}, u32[]{:S(2)}) %collective-permute-start.2) | collective-permute-done | bytes 294944 | tf_op jit(solution)/shard_map/ppermute | solution.py:370
  40.9 0.0 collective-permute-done.3.rest_4_
  40.9 13.8 %collective-permute-done.4.rest_5_ = f32[9,64,128]{2,1,0:T(8,128)S(1)} collective-permute-done((f32[9,64,128]{2,1,0:T(8,128)S(1)}, f32[9,64,128]{2,1,0:T(8,128)S(1)}, u32[]{:S(2)}, u32[]{:S(2)}) %collective-permute-start.4) | collective-permute-done | bytes 294944 | tf_op jit(solution)/shard_map/ppermute | solution.py:370
  54.7 1.4 %gram.2.rest_8_ = f32[1,128]{1,0:T(1,128)S(1)} custom-call(s32[1]{0:T(128)} %bitcast.me_ref, f32[9,64,128]{2,1,0:T(8,128)S(1)} %get-tuple-element.16.rest_0_.rest_6_.rest_7_, f32[9,64,128]{2,1,0:T(8,128)S(1)} %collective-permute-done.rest_1_, f32[9,64,128]{2,1,0:T(8,128)S(1)} %collective-permute-done.1.rest_2_, ...), custom_call_target="tpu_custom_call" | custom-call | flops 3096576 | bytes 2359296 | tf_op jit(solution)/shard_map/gram/pallas_call | solution.py:288
  56.1 0.0 collective-permute-done.5.rest_6_
  56.1 0.0 collective-permute-done.6.rest_7_
  56.1 0.9 %gram.3 = f32[32,1,128]{2,1,0:T(1,128)S(1)} custom-call(s32[1]{0:T(128)} %bitcast.me_ref, f32[9,64,128]{2,1,0:T(8,128)S(1)} %get-tuple-element.16.rest_0_.rest_6_.rest_7_, f32[9,64,128]{2,1,0:T(8,128)S(1)} %collective-permute-done.rest_1_, f32[9,64,128]{2,1,0:T(8,128)S(1)} %collective-permute-done.1.rest_2_, ...), custom_call_target="tpu_custom_call" | custom-call | flops 2211840 | bytes 2359296 | tf_op jit(solution)/shard_map/gram/pallas_call | solution.py:288
  57.0 13.2 %all_to_all.5.sums = f32[32,1,128]{2,1,0:T(1,128)S(1)} all-to-all(f32[32,1,128]{2,1,0:T(1,128)S(1)} %gram.3), channel_id=1, replica_groups=mesh['dp'=8,'chan'=4] {'dp','chan'}, dimensions={0} | all-to-all | bytes 32768 | tf_op jit(solution)/shard_map/all_to_all | solution.py:403
  70.2 0.0 copy-done
  70.2 0.0 copy-done.1
  70.2 1.3 %final.1 = (f32[9,64,128]{2,1,0:T(8,128)}, f32[9,64,128]{2,1,0:T(8,128)}) custom-call(s32[1]{0:T(128)} %bitcast.me_ref, f32[32,1,128]{2,1,0:T(1,128)S(1)} %all_to_all.5.sums, f32[9,64,128]{2,1,0:T(8,128)S(1)} %bitcast.13, f32[9,64,128]{2,1,0:T(8,128)S(1)} %bitcast.14, f32[9,64,128]{2,1,0:T(8,128)S(1)} %get-tuple-element.16.rest_0_.rest_6_.rest_7_, ...), custom_call_target="tpu_custom_call" | custom-call | flops 1179648 | bytes 3538944 | tf_op jit(solution)/shard_map/final/pallas_call | solution.py:353
Async XLA Ops:
  12.0 3.2 %copy-start.2 = (bf16[4,32,8,32,128]{4,3,2,1,0:T(8,128)(2,1)}, bf16[4,32,8,32,128]{4,3,2,1,0:T(8,128)(2,1)S(1)}, u32[]{:S(2)}) copy-start(bf16[4,32,8,32,128]{4,3,2,1,0:T(8,128)(2,1)S(1)} %get-tuple-element.15.av) | copy-start | bytes 25165828
  15.2 3.4 %copy-start.3 = (bf16[4,32,8,32,128]{4,3,2,1,0:T(8,128)(2,1)S(1)}, bf16[4,32,8,32,128]{4,3,2,1,0:T(8,128)(2,1)}, u32[]{:S(2)}) copy-start(bf16[4,32,8,32,128]{4,3,2,1,0:T(8,128)(2,1)} %copy-done.2) | copy-start | bytes 25165828
  18.6 6.0 %copy-start.7 = (f32[9,64,128]{2,1,0:T(8,128)S(1)}, f32[9,64,128]{2,1,0:T(8,128)}, u32[]{:S(2)}) copy-start(f32[9,64,128]{2,1,0:T(8,128)} %get-tuple-element.18) | copy-start | bytes 884740
  18.6 8.5 %copy-start.6 = (f32[9,64,128]{2,1,0:T(8,128)S(1)}, f32[9,64,128]{2,1,0:T(8,128)}, u32[]{:S(2)}) copy-start(f32[9,64,128]{2,1,0:T(8,128)} %get-tuple-element.19) | copy-start | bytes 884740
  18.6 8.6 %copy-start.5 = (f32[9,64,128]{2,1,0:T(8,128)S(1)}, f32[9,64,128]{2,1,0:T(8,128)}, u32[]{:S(2)}) copy-start(f32[9,64,128]{2,1,0:T(8,128)} %get-tuple-element.20) | copy-start | bytes 884740
  18.6 10.3 %copy-start.4 = (f32[9,64,128]{2,1,0:T(8,128)S(1)}, f32[9,64,128]{2,1,0:T(8,128)}, u32[]{:S(2)}) copy-start(f32[9,64,128]{2,1,0:T(8,128)} %get-tuple-element.21) | copy-start | bytes 884740
  18.6 51.6 %copy-start = (f32[64,3,3,128]{3,0,2,1:T(8,128)S(1)}, f32[64,3,3,128]{3,0,2,1:T(8,128)}, u32[]{:S(2)}) copy-start(f32[64,3,3,128]{3,0,2,1:T(8,128)} %param.6) | copy-start | bytes 884740
  18.6 51.6 %copy-start.1 = (f32[64,3,3,128]{3,0,2,1:T(8,128)S(1)}, f32[64,3,3,128]{3,0,2,1:T(8,128)}, u32[]{:S(2)}) copy-start(f32[64,3,3,128]{3,0,2,1:T(8,128)} %param.7) | copy-start | bytes 884740
  24.0 5.0 %collective-permute-start = (f32[9,64,128]{2,1,0:T(8,128)S(1)}, f32[9,64,128]{2,1,0:T(8,128)S(1)}, u32[]{:S(2)}, u32[]{:S(2)}) collective-permute-start(f32[9,64,128]{2,1,0:T(8,128)S(1)} %get-tuple-element.17), channel_id=1, source_target_pairs={{0,4},{4,0},{8,12},{12,8},{16,20},{20,16},{24,28},{28,24},{1,5},{5... | collective-permute-start | bytes 884744 | tf_op jit(solution)/shard_map/ppermute | solution.py:370
  24.6 10.4 %collective-permute-start.1 = (f32[9,64,128]{2,1,0:T(8,128)S(1)}, f32[9,64,128]{2,1,0:T(8,128)S(1)}, u32[]{:S(2)}, u32[]{:S(2)}) collective-permute-start(f32[9,64,128]{2,1,0:T(8,128)S(1)} %copy-done.7), channel_id=1, source_target_pairs={{0,8},{4,12},{8,0},{12,4},{16,24},{20,28},{24,16},{28,20},{1,9},{5... | collective-permute-start | bytes 884744 | tf_op jit(solution)/shard_map/ppermute | solution.py:370
  27.1 13.7 %collective-permute-start.2 = (f32[9,64,128]{2,1,0:T(8,128)S(1)}, f32[9,64,128]{2,1,0:T(8,128)S(1)}, u32[]{:S(2)}, u32[]{:S(2)}) collective-permute-start(f32[9,64,128]{2,1,0:T(8,128)S(1)} %copy-done.6), channel_id=1, source_target_pairs={{0,12},{4,8},{8,4},{12,0},{16,28},{20,24},{24,20},{28,16},{1,13},{... | collective-permute-start | bytes 884744 | tf_op jit(solution)/shard_map/ppermute | solution.py:370
  27.2 13.6 %collective-permute-start.3 = (f32[9,64,128]{2,1,0:T(8,128)S(1)}, f32[9,64,128]{2,1,0:T(8,128)S(1)}, u32[]{:S(2)}, u32[]{:S(2)}) collective-permute-start(f32[9,64,128]{2,1,0:T(8,128)S(1)} %copy-done.5), channel_id=1, source_target_pairs={{0,16},{4,20},{8,24},{12,28},{16,0},{20,4},{24,8},{28,12},{1,17},{... | collective-permute-start | bytes 884744 | tf_op jit(solution)/shard_map/ppermute | solution.py:370
  28.9 25.8 %collective-permute-start.4 = (f32[9,64,128]{2,1,0:T(8,128)S(1)}, f32[9,64,128]{2,1,0:T(8,128)S(1)}, u32[]{:S(2)}, u32[]{:S(2)}) collective-permute-start(f32[9,64,128]{2,1,0:T(8,128)S(1)} %copy-done.4), channel_id=1, source_target_pairs={{0,20},{4,16},{8,28},{12,24},{16,4},{20,0},{24,12},{28,8},{1,21},{... | collective-permute-start | bytes 884744 | tf_op jit(solution)/shard_map/ppermute | solution.py:370
  29.0 27.1 %collective-permute-start.5 = (f32[9,64,128]{2,1,0:T(8,128)S(1)}, f32[9,64,128]{2,1,0:T(8,128)S(1)}, u32[]{:S(2)}, u32[]{:S(2)}) collective-permute-start(f32[9,64,128]{2,1,0:T(8,128)S(1)} %get-tuple-element.22), channel_id=1, source_target_pairs={{0,24},{4,28},{8,16},{12,20},{16,8},{20,12},{24,0},{28,4},{1,25},{... | collective-permute-start | bytes 884744 | tf_op jit(solution)/shard_map/ppermute | solution.py:370
  35.0 21.1 %collective-permute-start.6 = (f32[9,64,128]{2,1,0:T(8,128)S(1)}, f32[9,64,128]{2,1,0:T(8,128)S(1)}, u32[]{:S(2)}, u32[]{:S(2)}) collective-permute-start(f32[9,64,128]{2,1,0:T(8,128)S(1)} %get-tuple-element.23), channel_id=1, source_target_pairs={{0,28},{4,24},{8,20},{12,16},{16,12},{20,8},{24,4},{28,0},{1,29},{... | collective-permute-start | bytes 884744 | tf_op jit(solution)/shard_map/ppermute | solution.py:370
where the time goes:
time: 71.7 us; the launch traced here: 71.5 us
  waiting for transfers between devices  21.5 us (30%)
  Pallas kernels  20.2 us (28%)
  blocking collectives  13.2 us (18%)
  starting transfers between devices  9.17 us (13%)
  local copies, waits for them, and re-layouts  6.63 us (9%)
    ppermute x7, waiting for transfers between devices, send(): return lax.ppermute(block, 'dp', [(r, r ^ k) for r in range(parts)])  21.5 us
    all_to_all x1, blocking collectives, shards(): lax.all_to_all(sums, ('dp', 'chan'), split_axis=0, concat_axis=0, tiled=T...  13.2 us
    pallas_call x1, Pallas kernels, near_blocks(): pl.pallas_call(functools.partial(near_kernel, [0, height // 8, height //...  11.4 us
    ppermute x7, starting transfers between devices, send(): return lax.ppermute(block, 'dp', [(r, r ^ k) for r in range(parts)])  9.17 us
    unnamed x16, local copies, waits for them, and re-layouts  6.63 us
    pallas_call x1, Pallas kernels, far_blocks(): pl.pallas_call(far_kernel, out_shape=[block] * 4, in_specs=[SM, VM, VM],...  5.36 us
    pallas_call x2, Pallas kernels, gram(): pl.pallas_call(functools.partial(gram_kernel, pairs, parts, devices), out...  2.26 us
  transfers between devices with their start and end apart: 7, of which 3 were waited for; matrix products, arithmetic and copies ran while one was open for 0% of the time, Pallas kernels for 2%

commit v1 on v0

--- a/solution.py
+++ b/solution.py
@@ -119,55 +119,43 @@
     )(me, gt, av))
 
 
-def tile_dot(acc, gt, av, tiles, lo, hi, keep):
-    _, batch, width, lanes = av.shape[1:]
-    flat = batch * width
-    rows = gt.shape[0]
-    rhs = jnp.concatenate([av[q, lo:hi].reshape((hi - lo) * flat, lanes) for q in tiles], axis=1)
-    for i in range(3):
-        lhs = gt[:, (lo + 2 - i) * flat : (hi + 2 - i) * flat]
-        term = jnp.dot(lhs, rhs, preferred_element_type=f32)
-        here = slice(i * rows, (i + 1) * rows)
-        acc[here, :] = acc[here, :] + term if keep else term
-
-
-def tile_emit(acc, turned, outs, sem, me, cols):
-    depth = turned.shape[1] // len(outs)
-    for j in range(9):
-        turned[j] = acc[j * cols : (j + 1) * cols, :].T
-    copies = []
-    for k, out in enumerate(outs):
-        core = jnp.bitwise_xor(jnp.bitwise_and(me, 1), k % 2)
-        first = pl.multiple_of((k // 2) * 2 * depth + core * depth, depth)
-        copies.append(pltpu.make_async_copy(turned.at[:, pl.ds(first, depth), :], out, sem.at[k]))
-    for copy in copies:
-        copy.start()
-    for copy in copies:
-        copy.wait()
+def tile_terms(gt, rhs, lo, hi, flat, i):
+    return jnp.dot(gt[:, (lo + 2 - i) * flat : (hi + 2 - i) * flat], rhs, preferred_element_type=f32)
+
+
+def tile_columns(av, chip, tiles, lo, hi):
+    _, batch, width, cin = av.shape
+    lanes = cin // 4
+    firsts = [pl.multiple_of(jnp.bitwise_xor(chip, q) * lanes, lanes) for q in tiles]
+    return jnp.concatenate([av[lo:hi, :, :, pl.ds(f, lanes)].reshape((hi - lo) * batch * width, lanes) for f in firsts], axis=1)
+
+
+def tile_store(value, i, outs, me, cols):
+    depth = outs[0].shape[1]
+    is_lower = jnp.bitwise_and(me, 1) == 0
+    for q in range(len(outs) // 2):
+        for j in range(3):
+            turned = value[j * cols : (j + 1) * cols, q * 2 * depth : (q + 1) * 2 * depth].T
+            lower, upper = turned[:depth], turned[depth:]
+            outs[2 * q][3 * i + j] = jnp.where(is_lower, lower, upper)
+            outs[2 * q + 1][3 * i + j] = jnp.where(is_lower, upper, lower)
 
 
 def near_kernel(bounds, me_ref, g_hbm, a_hbm, *rest):
     outs = rest[:4]
-    av, gt, gv, acc, turned, asem, bsem, gsem, osem = rest[4:]
-    _, height, batch, width, lanes = av.shape
+    av, gt, gv, acc, asem, gsem = rest[4:]
+    height, batch, width, _ = av.shape
     cols = gv.shape[3]
     flat = batch * width
+    rows = 3 * cols
     me = me_ref[0]
-    chip = me // 2
-
-    def fetch(q, h, sem):
-        first = pl.multiple_of(jnp.bitwise_xor(chip, q) * lanes, lanes)
-        return pltpu.make_async_copy(a_hbm.at[:, h, :, pl.ds(first, lanes)], av.at[q, h], sem)
-
-    gcopy = pltpu.make_async_copy(g_hbm, gv, gsem.at[0])
-    near = [[fetch(q, h, asem.at[q - 1, h]) for q in (1, 2)] for h in range(height)]
-    far = [[fetch(q, h, bsem.at[q // 3, h]) for q in (3, 0)] for h in range(height)]
-    gcopy.start()
-    for pair in near + far:
-        for copy in pair:
-            copy.start()
-    gt[:, 0:flat] = jnp.zeros((3 * cols, flat), bf16)
-    gt[:, (height + 1) * flat : (height + 2) * flat] = jnp.zeros((3 * cols, flat), bf16)
+    gends = [0] + [min(b + 1, height) for b in bounds[1:]]
+    gcopy = [pltpu.make_async_copy(g_hbm.at[:, h], gv.at[:, h], gsem.at[h]) for h in range(height)]
+    acopy = [pltpu.make_async_copy(a_hbm.at[:, h], av.at[h], asem.at[h]) for h in range(height)]
+    for copy in gcopy[: gends[1]] + acopy[: bounds[1]] + gcopy[gends[1] :] + acopy[bounds[1] :]:
+        copy.start()
+    gt[:, 0:flat] = jnp.zeros((rows, flat), bf16)
+    gt[:, (height + 1) * flat : (height + 2) * flat] = jnp.zeros((rows, flat), bf16)
     column = lax.broadcasted_iota(jnp.int32, (cols, flat), 1) % width
     is_last, is_first = column == width - 1, column == 0
 
@@ -179,27 +167,44 @@
             gt[cols : 2 * cols, here] = g.astype(bf16)
             gt[2 * cols : 3 * cols, here] = jnp.where(is_first, 0.0, pltpu.roll(g, 1, 1)).astype(bf16)
 
-    gcopy.wait()
-    prepare(0, bounds[1] + 1)
-    for i in range(len(bounds) - 1):
-        lo, hi = bounds[i], bounds[i + 1]
+    for h in range(gends[1]):
+        gcopy[h].wait()
+
+    @pl.when(me >= 0)
+    def _():
+        prepare(0, gends[1])
+
+    for n in range(len(bounds) - 1):
+        lo, hi = bounds[n], bounds[n + 1]
         for h in range(lo, hi):
-            for copy in near[h]:
-                copy.wait()
-        if i + 2 < len(bounds):
-            prepare(hi + 1, min(bounds[i + 2] + 1, height))
-        tile_dot(acc, gt, av, (1, 2), lo, hi, i > 0)
-    tile_emit(acc, turned, outs, osem, me, cols)
-    for pair in far:
-        for copy in pair:
-            copy.wait()
-
-
-def far_kernel(me_ref, gt, av, *rest):
-    outs = rest[:4]
-    acc, turned, osem = rest[4:]
-    tile_dot(acc, gt, av, (3, 0), 0, av.shape[1], False)
-    tile_emit(acc, turned, outs, osem, me_ref[0], gt.shape[0] // 3)
+            acopy[h].wait()
+        if n + 2 < len(bounds):
+            for h in range(gends[n + 1], gends[n + 2]):
+                gcopy[h].wait()
+
+        @pl.when(me >= 0)
+        def _(n=n, lo=lo, hi=hi):
+            is_end = n + 2 == len(bounds)
+            if not is_end:
+                prepare(gends[n + 1], gends[n + 2])
+            rhs = tile_columns(av, me // 2, (1, 2), lo, hi)
+            for i in range(3):
+                here = slice(i * rows, (i + 1) * rows)
+                term = tile_terms(gt, rhs, lo, hi, flat, i)
+                if n > 0:
+                    term = acc[here, :] + term
+                if is_end:
+                    tile_store(term, i, outs, me, cols)
+                else:
+                    acc[here, :] = term
+
+
+def far_kernel(me_ref, gt, av, *outs):
+    height, batch, width, _ = av.shape
+    me = me_ref[0]
+    rhs = tile_columns(av, me // 2, (3, 0), 0, height)
+    for i in range(3):
+        tile_store(tile_terms(gt, rhs, 0, height, batch * width, i), i, outs, me, gt.shape[0] // 3)
 
 
 def near_blocks(a, g, me):
@@ -208,18 +213,15 @@
     lanes, flat = cin // 4, batch * width
     block = jax.ShapeDtypeStruct((9, lanes // 2, cols), f32)
     res = pl.pallas_call(
-        functools.partial(near_kernel, [0, height // 8, height // 2, height]),
-        out_shape=[block] * 4 + [pltpu.VMEM((4, height, batch, width, lanes), bf16), pltpu.VMEM((3 * cols, (height + 2) * flat), bf16)],
+        functools.partial(near_kernel, [0, height // 8, height * 3 // 8, height * 11 // 16, height]),
+        out_shape=[block] * 4 + [pltpu.VMEM((height, batch, width, cin), bf16), pltpu.VMEM((3 * cols, (height + 2) * flat), bf16)],
         in_specs=[SM, HB, HB],
-        out_specs=[HB] * 4 + [VM, VM],
+        out_specs=[VM] * 6,
         scratch_shapes=[
             pltpu.VMEM((batch, height, width, cols), bf16),
             pltpu.VMEM((9 * cols, 2 * lanes), f32),
-            pltpu.VMEM((9, 2 * lanes, cols), f32),
-            pltpu.SemaphoreType.DMA((2, height)),
-            pltpu.SemaphoreType.DMA((2, height)),
-            pltpu.SemaphoreType.DMA((1,)),
-            pltpu.SemaphoreType.DMA((4,)),
+            pltpu.SemaphoreType.DMA((height,)),
+            pltpu.SemaphoreType.DMA((height,)),
         ],
         compiler_params=pltpu.CompilerParams(vmem_limit_bytes=NEAR_VMEM),
         cost_estimate=pl.CostEstimate(flops=36 * cols * lanes * height * flat, bytes_accessed=2 * (a.size + g.size), transcendentals=0),
@@ -229,15 +231,15 @@
 
 
 def far_blocks(av, gt, me):
-    _, height, batch, width, lanes = av.shape
+    height, batch, width, cin = av.shape
+    lanes = cin // 4
     cols = gt.shape[0] // 3
     block = jax.ShapeDtypeStruct((9, lanes // 2, cols), f32)
     return list(pl.pallas_call(
         far_kernel,
         out_shape=[block] * 4,
         in_specs=[SM, VM, VM],
-        out_specs=[HB] * 4,
-        scratch_shapes=[pltpu.VMEM((9 * cols, 2 * lanes), f32), pltpu.VMEM((9, 2 * lanes, cols), f32), pltpu.SemaphoreType.DMA((4,))],
+        out_specs=[VM] * 4,
         compiler_params=pltpu.CompilerParams(vmem_limit_bytes=NEXT_VMEM),
         cost_estimate=pl.CostEstimate(flops=36 * cols * lanes * height * batch * width, bytes_accessed=72 * lanes * cols, transcendentals=0),
         name="conv_far",
@@ -404,7 +406,7 @@
     return finish(sums, weight, momentum, chunks, me)
 
 
-FIRST_VMEM, NEXT_VMEM, NEAR_VMEM = 30 << 20, 30 << 20, 46 << 20
+FIRST_VMEM, NEXT_VMEM, NEAR_VMEM = 30 << 20, 30 << 20, 38 << 20
 
 
 def solution(mesh):

time: 71.7 us -> 62.3 us (0.87)
  local copies, waits for them, and re-layouts: 6.63 us -> 0.01 us
  Pallas kernels: 20.2 us -> 17.5 us
    unnamed x16 -> x4, local copies, waits for them, and re-layouts: 6.63 us -> 0.01 us
    pallas_call x1, Pallas kernels: 11.4 us -> 8.79 us  [near_blocks(): pl.pallas_call(functools.partial(near_kernel, [0, height // 8, height * 3...]
where the time goes in v1:
time: 62.3 us; the launch traced here: 62.1 us
  waiting for transfers between devices  21.4 us (34%)
  Pallas kernels  17.5 us (28%)
  blocking collectives  13.3 us (21%)
  starting transfers between devices  9.21 us (15%)
  between operations  0.68 us (1%)
    ppermute x7, waiting for transfers between devices, send(): return lax.ppermute(block, 'dp', [(r, r ^ k) for r in range(parts)])  21.4 us
    all_to_all x1, blocking collectives, shards(): lax.all_to_all(sums, ('dp', 'chan'), split_axis=0, concat_axis=0, tiled=T...  13.3 us
    ppermute x7, starting transfers between devices, send(): return lax.ppermute(block, 'dp', [(r, r ^ k) for r in range(parts)])  9.21 us
    pallas_call x1, Pallas kernels, near_blocks(): pl.pallas_call(functools.partial(near_kernel, [0, height // 8, height * 3...  8.79 us
    pallas_call x1, Pallas kernels, far_blocks(): pl.pallas_call(far_kernel, out_shape=[block] * 4, in_specs=[SM, VM, VM],...  5.22 us
    pallas_call x2, Pallas kernels, gram(): pl.pallas_call(functools.partial(gram_kernel, pairs, parts, devices), out...  2.26 us
    pallas_call x1, Pallas kernels, finish(): pl.pallas_call(functools.partial(final_kernel, parts), out_shape=[jax.Sha...  1.26 us
  transfers between devices with their start and end apart: 7, of which 3 were waited for; matrix products, arithmetic and copies ran while one was open for 0% of the time, Pallas kernels for 2%

profile of v1, /device:TPU:0, one launch (start us, length us, event | category | flops | bytes accessed | tf_op | source)
XLA Modules:
  0.0 62.1 jit_solution(15080778692570712204)
XLA Ops:
  0.6 8.8 %conv_near.1 = (f32[9,64,128]{2,1,0:T(8,128)S(1)}, f32[9,64,128]{2,1,0:T(8,128)S(1)}, f32[9,64,128]{2,1,0:T(8,128)S(1)}, f32[9,64,128]{2,1,0:T(8,128)S(1)}, bf16...) custom-call(s32[1]{0:T(128)} %bitcast.me_ref, bf16[8,32,32,128]{3,2,1,0:T(8,128)(2,1)} %g_hbm.1, ...), custom_call_target="tpu_custom_call" | custom-call | flops 4831838208 | bytes 10485760 | tf_op jit(solution)/shard_map/conv_near/pallas_call | solution.py:215
  9.4 0.0 copy-start
  9.4 0.0 copy-start.1
  9.5 5.2 %conv_far.1 = (f32[9,64,128]{2,1,0:T(8,128)S(1)}, f32[9,64,128]{2,1,0:T(8,128)S(1)}, f32[9,64,128]{2,1,0:T(8,128)S(1)}, f32[9,64,128]{2,1,0:T(8,128)S(1)}) custom-call(s32[1]{0:T(128)} %bitcast.me_ref, bf16[384,8704]{1,0:T(8,128)(2,1)S(1)} %get-tuple-element.14.gt, bf16[32,8,32,512]{3,2,1,0:T(8,128)(2,1)S(1)} %get-tuple-element.15.av), custom_call_target="tpu_custom_call" | custom-call | flops 4831838208 | bytes 1179648 | tf_op jit(solution)/shard_map/conv_far/pallas_call | solution.py:238
  14.7 0.6 collective-permute-start
  15.2 2.5 %collective-permute-start.1 = (f32[9,64,128]{2,1,0:T(8,128)S(1)}, f32[9,64,128]{2,1,0:T(8,128)S(1)}, u32[]{:S(2)}, u32[]{:S(2)}) collective-permute-start(f32[9,64,128]{2,1,0:T(8,128)S(1)} %get-tuple-element.18), channel_id=1, source_target_pairs={{0,8},{4,12},{8,0},{12,4},{16,24},{20,28},{24,16},{28,20},{1,9},{5... | collective-permute-start | bytes 884744 | tf_op jit(solution)/shard_map/ppermute | solution.py:372
  17.8 0.0 collective-permute-start.2
  17.8 1.8 %collective-permute-start.3 = (f32[9,64,128]{2,1,0:T(8,128)S(1)}, f32[9,64,128]{2,1,0:T(8,128)S(1)}, u32[]{:S(2)}, u32[]{:S(2)}) collective-permute-start(f32[9,64,128]{2,1,0:T(8,128)S(1)} %get-tuple-element.20), channel_id=1, source_target_pairs={{0,16},{4,20},{8,24},{12,28},{16,0},{20,4},{24,8},{28,12},{1,17},{... | collective-permute-start | bytes 884744 | tf_op jit(solution)/shard_map/ppermute | solution.py:372
  19.6 0.0 collective-permute-start.4
  19.6 0.0 collective-permute-done.rest_1_
  19.6 2.7 %collective-permute-start.5 = (f32[9,64,128]{2,1,0:T(8,128)S(1)}, f32[9,64,128]{2,1,0:T(8,128)S(1)}, u32[]{:S(2)}, u32[]{:S(2)}) collective-permute-start(f32[9,64,128]{2,1,0:T(8,128)S(1)} %get-tuple-element.22), channel_id=1, source_target_pairs={{0,24},{4,28},{8,16},{12,20},{16,8},{20,12},{24,0},{28,4},{1,25},{... | collective-permute-start | bytes 884744 | tf_op jit(solution)/shard_map/ppermute | solution.py:372
  22.3 3.4 %collective-permute-done.1.rest_2_ = f32[9,64,128]{2,1,0:T(8,128)S(1)} collective-permute-done((f32[9,64,128]{2,1,0:T(8,128)S(1)}, f32[9,64,128]{2,1,0:T(8,128)S(1)}, u32[]{:S(2)}, u32[]{:S(2)}) %collective-permute-start.1) | collective-permute-done | bytes 294944 | tf_op jit(solution)/shard_map/ppermute | solution.py:372
  25.6 1.6 %collective-permute-start.6 = (f32[9,64,128]{2,1,0:T(8,128)S(1)}, f32[9,64,128]{2,1,0:T(8,128)S(1)}, u32[]{:S(2)}, u32[]{:S(2)}) collective-permute-start(f32[9,64,128]{2,1,0:T(8,128)S(1)} %get-tuple-element.23), channel_id=1, source_target_pairs={{0,28},{4,24},{8,20},{12,16},{16,12},{20,8},{24,4},{28,0},{1,29},{... | collective-permute-start | bytes 884744 | tf_op jit(solution)/shard_map/ppermute | solution.py:372
  27.3 4.2 %collective-permute-done.2.rest_3_ = f32[9,64,128]{2,1,0:T(8,128)S(1)} collective-permute-done((f32[9,64,128]{2,1,0:T(8,128)S(1)}, f32[9,64,128]{2,1,0:T(8,128)S(1)}, u32[]{:S(2)}, u32[]{:S(2)}) %collective-permute-start.2) | collective-permute-done | bytes 294944 | tf_op jit(solution)/shard_map/ppermute | solution.py:372
  31.5 0.0 collective-permute-done.3.rest_4_
  31.5 13.8 %collective-permute-done.4.rest_5_ = f32[9,64,128]{2,1,0:T(8,128)S(1)} collective-permute-done((f32[9,64,128]{2,1,0:T(8,128)S(1)}, f32[9,64,128]{2,1,0:T(8,128)S(1)}, u32[]{:S(2)}, u32[]{:S(2)}) %collective-permute-start.4) | collective-permute-done | bytes 294944 | tf_op jit(solution)/shard_map/ppermute | solution.py:372
  45.3 1.4 %gram.2.rest_8_ = f32[1,128]{1,0:T(1,128)S(1)} custom-call(s32[1]{0:T(128)} %bitcast.me_ref, f32[9,64,128]{2,1,0:T(8,128)S(1)} %get-tuple-element.16.rest_0_.rest_6_.rest_7_, f32[9,64,128]{2,1,0:T(8,128)S(1)} %collective-permute-done.rest_1_, f32[9,64,128]{2,1,0:T(8,128)S(1)} %collective-permute-done.1.rest_2_, ...), custom_call_target="tpu_custom_call" | custom-call | flops 3096576 | bytes 2359296 | tf_op jit(solution)/shard_map/gram/pallas_call | solution.py:290
  46.7 0.0 collective-permute-done.5.rest_6_
  46.7 0.0 collective-permute-done.6.rest_7_
  46.7 0.9 %gram.3 = f32[32,1,128]{2,1,0:T(1,128)S(1)} custom-call(s32[1]{0:T(128)} %bitcast.me_ref, f32[9,64,128]{2,1,0:T(8,128)S(1)} %get-tuple-element.16.rest_0_.rest_6_.rest_7_, f32[9,64,128]{2,1,0:T(8,128)S(1)} %collective-permute-done.rest_1_, f32[9,64,128]{2,1,0:T(8,128)S(1)} %collective-permute-done.1.rest_2_, ...), custom_call_target="tpu_custom_call" | custom-call | flops 2211840 | bytes 2359296 | tf_op jit(solution)/shard_map/gram/pallas_call | solution.py:290
  47.6 13.3 %all_to_all.5.sums = f32[32,1,128]{2,1,0:T(1,128)S(1)} all-to-all(f32[32,1,128]{2,1,0:T(1,128)S(1)} %gram.3), channel_id=1, replica_groups=mesh['dp'=8,'chan'=4] {'dp','chan'}, dimensions={0} | all-to-all | bytes 32768 | tf_op jit(solution)/shard_map/all_to_all | solution.py:405
  60.9 0.0 copy-done
  60.9 0.0 copy-done.1
  60.9 1.3 %final.1 = (f32[9,64,128]{2,1,0:T(8,128)}, f32[9,64,128]{2,1,0:T(8,128)}) custom-call(s32[1]{0:T(128)} %bitcast.me_ref, f32[32,1,128]{2,1,0:T(1,128)S(1)} %all_to_all.5.sums, f32[9,64,128]{2,1,0:T(8,128)S(1)} %bitcast.13, f32[9,64,128]{2,1,0:T(8,128)S(1)} %bitcast.14, f32[9,64,128]{2,1,0:T(8,128)S(1)} %get-tuple-element.16.rest_0_.rest_6_.rest_7_, ...), custom_call_target="tpu_custom_call" | custom-call | flops 1179648 | bytes 3538944 | tf_op jit(solution)/shard_map/final/pallas_call | solution.py:355
Async XLA Ops:
  9.4 51.5 %copy-start = (f32[64,3,3,128]{3,0,2,1:T(8,128)S(1)}, f32[64,3,3,128]{3,0,2,1:T(8,128)}, u32[]{:S(2)}) copy-start(f32[64,3,3,128]{3,0,2,1:T(8,128)} %param.6) | copy-start | bytes 884740
  9.4 51.4 %copy-start.1 = (f32[64,3,3,128]{3,0,2,1:T(8,128)S(1)}, f32[64,3,3,128]{3,0,2,1:T(8,128)}, u32[]{:S(2)}) copy-start(f32[64,3,3,128]{3,0,2,1:T(8,128)} %param.7) | copy-start | bytes 884740
  14.7 4.9 %collective-permute-start = (f32[9,64,128]{2,1,0:T(8,128)S(1)}, f32[9,64,128]{2,1,0:T(8,128)S(1)}, u32[]{:S(2)}, u32[]{:S(2)}) collective-permute-start(f32[9,64,128]{2,1,0:T(8,128)S(1)} %get-tuple-element.17), channel_id=1, source_target_pairs={{0,4},{4,0},{8,12},{12,8},{16,20},{20,16},{24,28},{28,24},{1,5},{5... | collective-permute-start | bytes 884744 | tf_op jit(solution)/shard_map/ppermute | solution.py:372
  15.2 10.4 %collective-permute-start.1 = (f32[9,64,128]{2,1,0:T(8,128)S(1)}, f32[9,64,128]{2,1,0:T(8,128)S(1)}, u32[]{:S(2)}, u32[]{:S(2)}) collective-permute-start(f32[9,64,128]{2,1,0:T(8,128)S(1)} %get-tuple-element.18), channel_id=1, source_target_pairs={{0,8},{4,12},{8,0},{12,4},{16,24},{20,28},{24,16},{28,20},{1,9},{5... | collective-permute-start | bytes 884744 | tf_op jit(solution)/shard_map/ppermute | solution.py:372
  17.8 13.7 %collective-permute-start.2 = (f32[9,64,128]{2,1,0:T(8,128)S(1)}, f32[9,64,128]{2,1,0:T(8,128)S(1)}, u32[]{:S(2)}, u32[]{:S(2)}) collective-permute-start(f32[9,64,128]{2,1,0:T(8,128)S(1)} %get-tuple-element.19), channel_id=1, source_target_pairs={{0,12},{4,8},{8,4},{12,0},{16,28},{20,24},{24,20},{28,16},{1,13},{... | collective-permute-start | bytes 884744 | tf_op jit(solution)/shard_map/ppermute | solution.py:372
  17.8 13.7 %collective-permute-start.3 = (f32[9,64,128]{2,1,0:T(8,128)S(1)}, f32[9,64,128]{2,1,0:T(8,128)S(1)}, u32[]{:S(2)}, u32[]{:S(2)}) collective-permute-start(f32[9,64,128]{2,1,0:T(8,128)S(1)} %get-tuple-element.20), channel_id=1, source_target_pairs={{0,16},{4,20},{8,24},{12,28},{16,0},{20,4},{24,8},{28,12},{1,17},{... | collective-permute-start | bytes 884744 | tf_op jit(solution)/shard_map/ppermute | solution.py:372
  19.6 25.8 %collective-permute-start.4 = (f32[9,64,128]{2,1,0:T(8,128)S(1)}, f32[9,64,128]{2,1,0:T(8,128)S(1)}, u32[]{:S(2)}, u32[]{:S(2)}) collective-permute-start(f32[9,64,128]{2,1,0:T(8,128)S(1)} %get-tuple-element.21), channel_id=1, source_target_pairs={{0,20},{4,16},{8,28},{12,24},{16,4},{20,0},{24,12},{28,8},{1,21},{... | collective-permute-start | bytes 884744 | tf_op jit(solution)/shard_map/ppermute | solution.py:372
  19.6 27.1 %collective-permute-start.5 = (f32[9,64,128]{2,1,0:T(8,128)S(1)}, f32[9,64,128]{2,1,0:T(8,128)S(1)}, u32[]{:S(2)}, u32[]{:S(2)}) collective-permute-start(f32[9,64,128]{2,1,0:T(8,128)S(1)} %get-tuple-element.22), channel_id=1, source_target_pairs={{0,24},{4,28},{8,16},{12,20},{16,8},{20,12},{24,0},{28,4},{1,25},{... | collective-permute-start | bytes 884744 | tf_op jit(solution)/shard_map/ppermute | solution.py:372
  25.6 21.1 %collective-permute-start.6 = (f32[9,64,128]{2,1,0:T(8,128)S(1)}, f32[9,64,128]{2,1,0:T(8,128)S(1)}, u32[]{:S(2)}, u32[]{:S(2)}) collective-permute-start(f32[9,64,128]{2,1,0:T(8,128)S(1)} %get-tuple-element.23), channel_id=1, source_target_pairs={{0,28},{4,24},{8,20},{12,16},{16,12},{20,8},{24,4},{28,0},{1,29},{... | collective-permute-start | bytes 884744 | tf_op jit(solution)/shard_map/ppermute | solution.py:372

commit v2 on v1

--- a/solution.py
+++ b/solution.py
@@ -131,14 +131,15 @@
 
 
 def tile_store(value, i, outs, me, cols):
-    depth = outs[0].shape[1]
     is_lower = jnp.bitwise_and(me, 1) == 0
+    depth = outs[0].shape[0] // 9
     for q in range(len(outs) // 2):
         for j in range(3):
             turned = value[j * cols : (j + 1) * cols, q * 2 * depth : (q + 1) * 2 * depth].T
             lower, upper = turned[:depth], turned[depth:]
-            outs[2 * q][3 * i + j] = jnp.where(is_lower, lower, upper)
-            outs[2 * q + 1][3 * i + j] = jnp.where(is_lower, upper, lower)
+            here = slice((3 * i + j) * depth, (3 * i + j + 1) * depth)
+            outs[2 * q][here, :] = jnp.where(is_lower, lower, upper)
+            outs[2 * q + 1][here, :] = jnp.where(is_lower, upper, lower)
 
 
 def near_kernel(bounds, me_ref, g_hbm, a_hbm, *rest):
@@ -187,7 +188,7 @@
             is_end = n + 2 == len(bounds)
             if not is_end:
                 prepare(gends[n + 1], gends[n + 2])
-            rhs = tile_columns(av, me // 2, (1, 2), lo, hi)
+            rhs = tile_columns(av, me // 2, (1 + jnp.bitwise_and(me, 1), 2 - jnp.bitwise_and(me, 1)), lo, hi)
             for i in range(3):
                 here = slice(i * rows, (i + 1) * rows)
                 term = tile_terms(gt, rhs, lo, hi, flat, i)
@@ -211,7 +212,7 @@
     batch, height, width, cin = a.shape
     cols = g.shape[3]
     lanes, flat = cin // 4, batch * width
-    block = jax.ShapeDtypeStruct((9, lanes // 2, cols), f32)
+    block = jax.ShapeDtypeStruct((9 * (lanes // 2), cols), f32)
     res = pl.pallas_call(
         functools.partial(near_kernel, [0, height // 8, height * 3 // 8, height * 11 // 16, height]),
         out_shape=[block] * 4 + [pltpu.VMEM((height, batch, width, cin), bf16), pltpu.VMEM((3 * cols, (height + 2) * flat), bf16)],
@@ -234,7 +235,7 @@
     height, batch, width, cin = av.shape
     lanes = cin // 4
     cols = gt.shape[0] // 3
-    block = jax.ShapeDtypeStruct((9, lanes // 2, cols), f32)
+    block = jax.ShapeDtypeStruct((9 * (lanes // 2), cols), f32)
     return list(pl.pallas_call(
         far_kernel,
         out_shape=[block] * 4,
@@ -246,28 +247,30 @@
     )(me, gt, av))
 
 
-def gram_kernel(pairs, parts, devices, me_ref, *rest):
+def gram_kernel(pairs, parts, devices, ids, *rest):
     blocks, out, rowsums = rest[:-2], rest[-2], rest[-1]
     chunks = len(blocks) // parts
     before = blocks[chunks * parts :]
-    me = me_ref[0]
-    taps, depth, cols = blocks[0].shape
+    length, cols = blocks[0].shape
     rowsums[...] = jnp.zeros_like(rowsums)
-    for first in range(0, len(pairs), 18):
-        some = pairs[first : first + 18]
+    for first in range(0, len(pairs), 16):
+        some = pairs[first : first + 16]
         names = sorted({n for pair in some for n in pair})
         sums = [jnp.zeros((8, cols), f32) for _ in some]
         for c in range(chunks):
             def body(i, sums):
-                tap, r = i // (depth // 8), i % (depth // 8)
-                x = {k: blocks[c * parts + k][tap, pl.ds(pl.multiple_of(r * 8, 8), 8), :] for k in names}
+                here = pl.ds(pl.multiple_of(i * 8, 8), 8)
+                x = {k: blocks[c * parts + k][here, :] for k in names}
                 return [s + x[k] * x[l] for s, (k, l) in zip(sums, some)]
 
-            sums = lax.fori_loop(0, taps * depth // 8, body, sums, unroll=4)
+            sums = lax.fori_loop(0, length // 8, body, sums, unroll=8)
         for s, (k, l) in zip(sums, some):
             rowsums[k * parts + l : k * parts + l + 1, :] = jnp.sum(s, axis=0, keepdims=True)
     number = lax.broadcasted_iota(jnp.int32, (parts * parts, 128), 0)
-    a, b = jnp.bitwise_xor(number // parts, me), jnp.bitwise_xor(number % parts, me)
+    a, b = jnp.zeros_like(number), jnp.zeros_like(number)
+    for k in range(parts):
+        a = jnp.where(number // parts == k, ids[k], a)
+        b = jnp.where(number % parts == k, ids[k], b)
     at = jnp.minimum(a, b) * parts + jnp.maximum(a, b)
     place = lax.broadcasted_iota(jnp.int32, (parts * parts, 128), 1)
     values = jnp.sum(rowsums[...], axis=1, keepdims=True)
@@ -282,7 +285,7 @@
                 out[r : r + 1, :] = total
 
 
-def gram(chunks, pairs, before, me, devices):
+def gram(chunks, pairs, before, ids, devices):
     parts = len(chunks[0])
     rows = -(-parts * parts // 128)
     shape = (devices, rows, 128) if devices else (rows, 128)
@@ -292,11 +295,11 @@
         out_shape=jax.ShapeDtypeStruct(shape, f32),
         in_specs=[SM] + [VM] * (len(flat) + len(before)),
         out_specs=VM,
-        scratch_shapes=[pltpu.VMEM((parts * parts, flat[0].shape[2]), f32)],
+        scratch_shapes=[pltpu.VMEM((parts * parts, flat[0].shape[1]), f32)],
         compiler_params=pltpu.CompilerParams(vmem_limit_bytes=NEXT_VMEM),
         cost_estimate=pl.CostEstimate(flops=2 * flat[0].size * len(chunks) * len(pairs), bytes_accessed=4 * flat[0].size * len(flat), transcendentals=0),
         name="gram",
-    )(me, *flat, *before)
+    )(ids, *flat, *before)
 
 
 def mixes_of(sums, parts):
@@ -325,32 +328,30 @@
     return factors
 
 
-def final_kernel(parts, me_ref, sums, weight, momentum, *rest):
+def final_kernel(parts, ids, sums, weight, momentum, *rest):
     blocks, (new_weight, new_momentum) = rest[:-2], rest[-2:]
-    me = me_ref[0]
     total = jnp.sum(sums[...], axis=0)
     factors = mixes_of(total, parts)
     mine = []
     for k in range(parts):
-        at = jnp.bitwise_xor(me, k)
         pick = factors[0]
         for r in range(1, parts):
-            pick = jnp.where(at == r, factors[r], pick)
+            pick = jnp.where(ids[k] == r, factors[r], pick)
         mine.append(pick)
-    taps = blocks[0].shape[0]
-    for n in range(weight.shape[0]):
-        value = 0.9 * momentum[n]
+    length = blocks[0].shape[0]
+    for c in range(len(blocks) // parts):
+        here = slice(c * length, (c + 1) * length)
+        value = 0.9 * momentum[here, :]
         for k in range(parts):
-            value = value + mine[k] * blocks[n // taps * parts + k][n % taps]
-        new_momentum[n] = value
-        new_weight[n] = weight[n] - 0.1 * value
-
-
-def finish(sums, weight, momentum, chunks, me):
+            value = value + mine[k] * blocks[c * parts + k][...]
+        new_momentum[here, :] = value
+        new_weight[here, :] = weight[here, :] - 0.1 * value
+
+
+def finish(sums, weight, momentum, chunks, ids):
     parts = len(chunks[0])
     depth, cols = weight.shape[0], weight.shape[3]
-    w = jnp.transpose(weight, (1, 2, 0, 3)).reshape(9, depth, cols)
-    m = jnp.transpose(momentum, (1, 2, 0, 3)).reshape(9, depth, cols)
+    w, m = (jnp.transpose(x, (1, 2, 0, 3)).reshape(9 * depth, cols) for x in (weight, momentum))
     flat = [b for chunk in chunks for b in chunk]
     outs = pl.pallas_call(
         functools.partial(final_kernel, parts),
@@ -360,7 +361,7 @@
         compiler_params=pltpu.CompilerParams(vmem_limit_bytes=NEXT_VMEM),
         cost_estimate=pl.CostEstimate(flops=2 * w.size * parts, bytes_accessed=4 * w.size * (parts + 4), transcendentals=0),
         name="final",
-    )(me, sums, w, m, *flat)
+    )(ids, sums, w, m, *flat)
     return tuple(jnp.transpose(x.reshape(3, 3, depth, cols), (2, 0, 1, 3)) for x in outs)
 
 
@@ -368,31 +369,35 @@
     return [(k, l) for k in range(parts) for l in range(k, parts)]
 
 
-def send(block, k, parts):
-    return lax.ppermute(block, "dp", [(r, r ^ k) for r in range(parts)])
+def send(block, parts, flips):
+    return lax.ppermute(block, "dp", [(r, r ^ flips[r % 2]) for r in range(parts)])
 
 
 def by_rows(activations, out_grads, me, parts):
     def exchange(blocks):
-        return blocks[:1] + [send(blocks[k], k, parts) for k in range(1, parts)]
+        blocks = [b.reshape(-1, b.shape[2]) for b in blocks]
+        return blocks[:1] + [send(blocks[k], parts, (k, k)) for k in range(1, parts)]
 
     middle, av, gt = conv_first(activations, out_grads, me, parts)
     middle = exchange(middle)
     lower = exchange(conv_next(av, gt, me, 1, parts))
     upper = exchange(conv_next(av, gt, me, -1, parts))
-    return [lower, middle, upper], upper_pairs(parts), []
+    return [lower, middle, upper], upper_pairs(parts), [], jnp.bitwise_xor(me, jnp.arange(parts, dtype=jnp.int32))
 
 
 def by_chips(activations, out_grads, me, parts):
+    flips = [(2, 4), (3, 5), (4, 2), (5, 3)]
     near, av, gt = near_blocks(activations, out_grads, me)
-    near = [send(near[k - 2], k, parts) for k in range(2, 6)]
+    near = [send(block, parts, flip) for block, flip in zip(near, flips)]
     far = far_blocks(av, gt, me)
-    far = [send(far[k], 6 + k, parts) for k in range(2)] + [far[2], send(far[3], 1, parts)]
-    blocks = far[2:] + near
-    early = [pair for pair in upper_pairs(parts) if pair[1] < 6]
-    partial = gram([blocks + [blocks[0]] * 2], early, [], me, 0)
-    blocks = blocks + far[:2]
-    return [blocks], [pair for pair in upper_pairs(parts) if pair[1] >= 6], [partial]
+    far = [send(far[k], parts, (6 + k, 6 + k)) for k in range(2)] + [far[2], send(far[3], parts, (1, 1))]
+    even = jnp.array([0, 1, 2, 5, 4, 3, 6, 7], jnp.int32)
+    odd = jnp.array([0, 1, 4, 3, 2, 5, 6, 7], jnp.int32)
+    ids = jnp.bitwise_xor(me, jnp.where(me % 2 == 0, even, odd))
+    blocks = far[2:] + near + far[:2]
+    early = [pair for pair in upper_pairs(parts) if pair[1] < EARLY]
+    partial = gram([blocks[:EARLY] + [blocks[0]] * (parts - EARLY)], early, [], ids, 0)
+    return [blocks], [pair for pair in upper_pairs(parts) if pair[1] >= EARLY], [partial], ids
 
 
 def shards(activations, out_grads, weight, momentum):
@@ -400,12 +405,13 @@
     devices = parts * lax.axis_size("chan")
     me = lax.axis_index("dp").reshape(1).astype(jnp.int32)
     four = parts == 8 and activations.shape[3] % 512 == 0
-    chunks, pairs, before = (by_chips if four else by_rows)(activations, out_grads, me, parts)
-    sums = gram(chunks, pairs, before, me, devices)
+    chunks, pairs, before, ids = (by_chips if four else by_rows)(activations, out_grads, me, parts)
+    sums = gram(chunks, pairs, before, ids, devices)
     sums = lax.all_to_all(sums, ("dp", "chan"), split_axis=0, concat_axis=0, tiled=True)
-    return finish(sums, weight, momentum, chunks, me)
-
-
+    return finish(sums, weight, momentum, chunks, ids)
+
+
+EARLY = 4
 FIRST_VMEM, NEXT_VMEM, NEAR_VMEM = 30 << 20, 30 << 20, 38 << 20
 
 

time: 62.3 us -> 61.5 us (0.987)
  waiting for transfers between devices: 21.4 us -> 13.6 us
  starting transfers between devices: 9.21 us -> 15.5 us
    ppermute x7, waiting for transfers between devices: 21.4 us -> 13.6 us  [send(): lax.ppermute(block, 'dp', [(r, r ^ flips[r % 2]) for r in range(parts)])]
    ppermute x7, starting transfers between devices: 9.21 us -> 15.5 us  [send(): lax.ppermute(block, 'dp', [(r, r ^ flips[r % 2]) for r in range(parts)])]
    pallas_call x1, Pallas kernels: 1.26 us -> 1.95 us  [finish(): pl.pallas_call(functools.partial(final_kernel, parts), out_shape=[jax.Sha...]
  transfers between devices with their start and end apart: 7 -> 7, of which waited for: 3 -> 4; matrix products, arithmetic and copies ran while one was open for 0% -> 0% of each run, Pallas kernels for 2% -> 1%
where the time goes in v2:
time: 61.5 us; the launch traced here: 61.3 us
  Pallas kernels  18.1 us (29%)
  starting transfers between devices  15.5 us (25%)
  waiting for transfers between devices  13.6 us (22%)
  blocking collectives  13.4 us (22%)
  between operations  0.7 us (1%)
    ppermute x7, starting transfers between devices, send(): lax.ppermute(block, 'dp', [(r, r ^ flips[r % 2]) for r in range(parts)])  15.5 us
    ppermute x7, waiting for transfers between devices, send(): lax.ppermute(block, 'dp', [(r, r ^ flips[r % 2]) for r in range(parts)])  13.6 us
    all_to_all x1, blocking collectives, shards(): lax.all_to_all(sums, ('dp', 'chan'), split_axis=0, concat_axis=0, tiled=T...  13.4 us
    pallas_call x1, Pallas kernels, near_blocks(): pl.pallas_call(functools.partial(near_kernel, [0, height // 8, height * 3...  8.8 us
    pallas_call x1, Pallas kernels, far_blocks(): pl.pallas_call(far_kernel, out_shape=[block] * 4, in_specs=[SM, VM, VM],...  5.22 us
    pallas_call x2, Pallas kernels, gram(): pl.pallas_call(functools.partial(gram_kernel, pairs, parts, devices), out...  2.14 us
    pallas_call x1, Pallas kernels, finish(): pl.pallas_call(functools.partial(final_kernel, parts), out_shape=[jax.Sha...  1.95 us
  transfers between devices with their start and end apart: 7, of which 4 were waited for; matrix products, arithmetic and copies ran while one was open for 0% of the time, Pallas kernels for 1%

profile of v2, /device:TPU:0, one launch (start us, length us, event | category | flops | bytes accessed | tf_op | source)
XLA Modules:
  0.0 61.3 jit_solution(10242116046893669985)
XLA Ops:
  0.6 8.8 %conv_near.1 = (f32[576,128]{1,0:T(8,128)S(1)}, f32[576,128]{1,0:T(8,128)S(1)}, f32[576,128]{1,0:T(8,128)S(1)}, f32[576,128]{1,0:T(8,128)S(1)}, bf16[32,8,32,512...) custom-call(s32[1]{0:T(128)} %bitcast.me_ref, bf16[8,32,32,128]{3,2,1,0:T(8,128)(2,1)} %g_hbm.1, ...), custom_call_target="tpu_custom_call" | custom-call | flops 4831838208 | bytes 10485760 | tf_op jit(solution)/shard_map/conv_near/pallas_call | solution.py:216
  9.4 0.0 copy-start.2
  9.5 0.0 copy-start.3
  9.5 0.0 copy-start
  9.5 0.0 copy-start.1
  9.5 5.2 %conv_far.1 = (f32[576,128]{1,0:T(8,128)S(1)}, f32[576,128]{1,0:T(8,128)S(1)}, f32[576,128]{1,0:T(8,128)S(1)}, f32[576,128]{1,0:T(8,128)S(1)}) custom-call(s32[1]{0:T(128)} %bitcast.me_ref, bf16[384,8704]{1,0:T(8,128)(2,1)S(1)} %get-tuple-element.14.gt, bf16[32,8,32,512]{3,2,1,0:T(8,128)(2,1)S(1)} %get-tuple-element.15.av), custom_call_target="tpu_custom_call" | custom-call | flops 4831838208 | bytes 1179648 | tf_op jit(solution)/shard_map/conv_far/pallas_call | solution.py:239
  14.7 0.6 collective-permute-start
  15.3 2.5 %collective-permute-start.1 = (f32[576,128]{1,0:T(8,128)S(1)}, f32[576,128]{1,0:T(8,128)S(1)}, u32[]{:S(2)}, u32[]{:S(2)}) collective-permute-start(f32[576,128]{1,0:T(8,128)S(1)} %get-tuple-element.18), channel_id=1, source_target_pairs={{0,8},{4,20},{8,0},{12,28},{16,24},{20,4},{24,16},{28,12},{1,9},{5... | collective-permute-start | bytes 884744 | tf_op jit(solution)/shard_map/ppermute | solution.py:373
  17.8 1.5 %collective-permute-start.5 = (f32[576,128]{1,0:T(8,128)S(1)}, f32[576,128]{1,0:T(8,128)S(1)}, u32[]{:S(2)}, u32[]{:S(2)}) collective-permute-start(f32[576,128]{1,0:T(8,128)S(1)} %get-tuple-element.22), channel_id=1, source_target_pairs={{0,24},{4,28},{8,16},{12,20},{16,8},{20,12},{24,0},{28,4},{1,25},{... | collective-permute-start | bytes 884744 | tf_op jit(solution)/shard_map/ppermute | solution.py:373
  19.3 0.0 collective-permute-start.2
  19.3 2.7 %collective-permute-start.6 = (f32[576,128]{1,0:T(8,128)S(1)}, f32[576,128]{1,0:T(8,128)S(1)}, u32[]{:S(2)}, u32[]{:S(2)}) collective-permute-start(f32[576,128]{1,0:T(8,128)S(1)} %get-tuple-element.23), channel_id=1, source_target_pairs={{0,28},{4,24},{8,20},{12,16},{16,12},{20,8},{24,4},{28,0},{1,29},{... | collective-permute-start | bytes 884744 | tf_op jit(solution)/shard_map/ppermute | solution.py:373
  22.0 0.0 collective-permute-done.rest_1_
  22.0 0.5 collective-permute-start.3
  22.5 2.2 %collective-permute-done.1.rest_2_ = f32[576,128]{1,0:T(8,128)S(1)} collective-permute-done((f32[576,128]{1,0:T(8,128)S(1)}, f32[576,128]{1,0:T(8,128)S(1)}, u32[]{:S(2)}, u32[]{:S(2)}) %collective-permute-start.1) | collective-permute-done | bytes 294944 | tf_op jit(solution)/shard_map/ppermute | solution.py:373
  24.7 7.7 %collective-permute-start.4 = (f32[576,128]{1,0:T(8,128)S(1)}, f32[576,128]{1,0:T(8,128)S(1)}, u32[]{:S(2)}, u32[]{:S(2)}) collective-permute-start(f32[576,128]{1,0:T(8,128)S(1)} %get-tuple-element.21), channel_id=1, source_target_pairs={{0,20},{4,8},{8,28},{12,0},{16,4},{20,24},{24,12},{28,16},{1,21},{... | collective-permute-start | bytes 884744 | tf_op jit(solution)/shard_map/ppermute | solution.py:373
  32.4 0.0 copy-done.2
  32.4 0.0 copy-done.3
  32.4 4.8 %collective-permute-done.2.rest_3_ = f32[576,128]{1,0:T(8,128)S(1)} collective-permute-done((f32[576,128]{1,0:T(8,128)S(1)}, f32[576,128]{1,0:T(8,128)S(1)}, u32[]{:S(2)}, u32[]{:S(2)}) %collective-permute-start.2) | collective-permute-done | bytes 294944 | tf_op jit(solution)/shard_map/ppermute | solution.py:373
  37.2 0.9 %gram.2.rest_8_ = f32[1,128]{1,0:T(1,128)S(1)} custom-call(s32[8]{0:T(128)S(1)} %fusion.ids, f32[576,128]{1,0:T(8,128)S(1)} %get-tuple-element.16.rest_0_.rest_4_.rest_5_.rest_6_.rest_7_, f32[576,128]{1,0:T(8,128)S(1)} %collective-permute-done.rest_1_, f32[576,128]{1,0:T(8,128)S(1)} %collective-permute-done.1.rest_2_, ...), custom_call_target="tpu_custom_call" | custom-call | flops 1474560 | bytes 2359296 | tf_op jit(solution)/shard_map/gram/pallas_call | solution.py:293
  38.1 0.0 collective-permute-done.5.rest_6_
  38.1 5.4 %collective-permute-done.6.rest_7_ = f32[576,128]{1,0:T(8,128)S(1)} collective-permute-done((f32[576,128]{1,0:T(8,128)S(1)}, f32[576,128]{1,0:T(8,128)S(1)}, u32[]{:S(2)}, u32[]{:S(2)}) %collective-permute-start.6) | collective-permute-done | bytes 294944 | tf_op jit(solution)/shard_map/ppermute | solution.py:373
  43.6 0.0 collective-permute-done.3.rest_4_
  43.6 1.1 %collective-permute-done.4.rest_5_ = f32[576,128]{1,0:T(8,128)S(1)} collective-permute-done((f32[576,128]{1,0:T(8,128)S(1)}, f32[576,128]{1,0:T(8,128)S(1)}, u32[]{:S(2)}, u32[]{:S(2)}) %collective-permute-start.4) | collective-permute-done | bytes 294944 | tf_op jit(solution)/shard_map/ppermute | solution.py:373
  44.7 1.3 %gram.3 = f32[32,1,128]{2,1,0:T(1,128)S(1)} custom-call(s32[8]{0:T(128)S(1)} %fusion.ids, f32[576,128]{1,0:T(8,128)S(1)} %get-tuple-element.16.rest_0_.rest_4_.rest_5_.rest_6_.rest_7_, f32[576,128]{1,0:T(8,128)S(1)} %collective-permute-done.rest_1_, f32[576,128]{1,0:T(8,128)S(1)} %collective-permute-done.1.rest_2_, ...), custom_call_target="tpu_custom_call" | custom-call | flops 3833856 | bytes 2359296 | tf_op jit(solution)/shard_map/gram/pallas_call | solution.py:293
  45.9 13.4 %all_to_all.5.sums = f32[32,1,128]{2,1,0:T(1,128)S(1)} all-to-all(f32[32,1,128]{2,1,0:T(1,128)S(1)} %gram.3), channel_id=1, replica_groups=mesh['dp'=8,'chan'=4] {'dp','chan'}, dimensions={0} | all-to-all | bytes 32768 | tf_op jit(solution)/shard_map/all_to_all | solution.py:410
  59.3 0.0 copy-done
  59.3 0.0 copy-done.1
  59.3 1.9 %final.1 = (f32[576,128]{1,0:T(8,128)}, f32[576,128]{1,0:T(8,128)}) custom-call(s32[8]{0:T(128)S(1)} %fusion.ids, f32[32,1,128]{2,1,0:T(1,128)S(1)} %all_to_all.5.sums, f32[576,128]{1,0:T(8,128)S(1)} %bitcast.14, f32[576,128]{1,0:T(8,128)S(1)} %bitcast.15, f32[576,128]{1,0:T(8,128)S(1)} %get-tuple-element.16.rest_0_.rest_4_.rest_5_.rest_6_.rest_7_, ...), custom_call_target="tpu_custom_call" | custom-call | flops 1179648 | bytes 3538944 | tf_op jit(solution)/shard_map/final/pallas_call | solution.py:356
  (1 shorter events, 0.0 us)
Async XLA Ops:
  9.4 23.0 %copy-start.2 = (s32[8]{0:T(128)S(1)}, s32[8]{0:T(128)}, u32[]{:S(2)}) copy-start(s32[8]{0:T(128)} %constant.31.clone) | copy-start | bytes 100
  9.5 22.9 %copy-start.3 = (s32[8]{0:T(128)S(1)}, s32[8]{0:T(128)}, u32[]{:S(2)}) copy-start(s32[8]{0:T(128)} %constant.30.clone) | copy-start | bytes 100
  9.5 49.9 %copy-start = (f32[64,3,3,128]{3,0,2,1:T(8,128)S(1)}, f32[64,3,3,128]{3,0,2,1:T(8,128)}, u32[]{:S(2)}) copy-start(f32[64,3,3,128]{3,0,2,1:T(8,128)} %param.8) | copy-start | bytes 884740
  9.5 49.9 %copy-start.1 = (f32[64,3,3,128]{3,0,2,1:T(8,128)S(1)}, f32[64,3,3,128]{3,0,2,1:T(8,128)}, u32[]{:S(2)}) copy-start(f32[64,3,3,128]{3,0,2,1:T(8,128)} %param.9) | copy-start | bytes 884740
  14.7 7.3 %collective-permute-start = (f32[576,128]{1,0:T(8,128)S(1)}, f32[576,128]{1,0:T(8,128)S(1)}, u32[]{:S(2)}, u32[]{:S(2)}) collective-permute-start(f32[576,128]{1,0:T(8,128)S(1)} %get-tuple-element.17), channel_id=1, source_target_pairs={{0,4},{4,0},{8,12},{12,8},{16,20},{20,16},{24,28},{28,24},{1,5},{5... | collective-permute-start | bytes 884744 | tf_op jit(solution)/shard_map/ppermute | solution.py:373
  15.3 9.4 %collective-permute-start.1 = (f32[576,128]{1,0:T(8,128)S(1)}, f32[576,128]{1,0:T(8,128)S(1)}, u32[]{:S(2)}, u32[]{:S(2)}) collective-permute-start(f32[576,128]{1,0:T(8,128)S(1)} %get-tuple-element.18), channel_id=1, source_target_pairs={{0,8},{4,20},{8,0},{12,28},{16,24},{20,4},{24,16},{28,12},{1,9},{5... | collective-permute-start | bytes 884744 | tf_op jit(solution)/shard_map/ppermute | solution.py:373
  17.8 20.3 %collective-permute-start.5 = (f32[576,128]{1,0:T(8,128)S(1)}, f32[576,128]{1,0:T(8,128)S(1)}, u32[]{:S(2)}, u32[]{:S(2)}) collective-permute-start(f32[576,128]{1,0:T(8,128)S(1)} %get-tuple-element.22), channel_id=1, source_target_pairs={{0,24},{4,28},{8,16},{12,20},{16,8},{20,12},{24,0},{28,4},{1,25},{... | collective-permute-start | bytes 884744 | tf_op jit(solution)/shard_map/ppermute | solution.py:373
  19.3 18.0 %collective-permute-start.2 = (f32[576,128]{1,0:T(8,128)S(1)}, f32[576,128]{1,0:T(8,128)S(1)}, u32[]{:S(2)}, u32[]{:S(2)}) collective-permute-start(f32[576,128]{1,0:T(8,128)S(1)} %get-tuple-element.19), channel_id=1, source_target_pairs={{0,12},{4,16},{8,4},{12,24},{16,28},{20,0},{24,20},{28,8},{1,13},{... | collective-permute-start | bytes 884744 | tf_op jit(solution)/shard_map/ppermute | solution.py:373
  19.3 24.3 %collective-permute-start.6 = (f32[576,128]{1,0:T(8,128)S(1)}, f32[576,128]{1,0:T(8,128)S(1)}, u32[]{:S(2)}, u32[]{:S(2)}) collective-permute-start(f32[576,128]{1,0:T(8,128)S(1)} %get-tuple-element.23), channel_id=1, source_target_pairs={{0,28},{4,24},{8,20},{12,16},{16,12},{20,8},{24,4},{28,0},{1,29},{... | collective-permute-start | bytes 884744 | tf_op jit(solution)/shard_map/ppermute | solution.py:373
  22.0 21.6 %collective-permute-start.3 = (f32[576,128]{1,0:T(8,128)S(1)}, f32[576,128]{1,0:T(8,128)S(1)}, u32[]{:S(2)}, u32[]{:S(2)}) collective-permute-start(f32[576,128]{1,0:T(8,128)S(1)} %get-tuple-element.20), channel_id=1, source_target_pairs={{0,16},{4,12},{8,24},{12,4},{16,0},{20,28},{24,8},{28,20},{1,17},{... | collective-permute-start | bytes 884744 | tf_op jit(solution)/shard_map/ppermute | solution.py:373
  24.7 20.0 %collective-permute-start.4 = (f32[576,128]{1,0:T(8,128)S(1)}, f32[576,128]{1,0:T(8,128)S(1)}, u32[]{:S(2)}, u32[]{:S(2)}) collective-permute-start(f32[576,128]{1,0:T(8,128)S(1)} %get-tuple-element.21), channel_id=1, source_target_pairs={{0,20},{4,8},{8,28},{12,0},{16,4},{20,24},{24,12},{28,16},{1,21},{... | collective-permute-start | bytes 884744 | tf_op jit(solution)/shard_map/ppermute | solution.py:373

commit v3 on v2

--- a/solution.py
+++ b/solution.py
@@ -339,13 +339,16 @@
             pick = jnp.where(ids[k] == r, factors[r], pick)
         mine.append(pick)
     length = blocks[0].shape[0]
-    for c in range(len(blocks) // parts):
-        here = slice(c * length, (c + 1) * length)
-        value = 0.9 * momentum[here, :]
-        for k in range(parts):
-            value = value + mine[k] * blocks[c * parts + k][...]
-        new_momentum[here, :] = value
-        new_weight[here, :] = weight[here, :] - 0.1 * value
+    size = length // 3
+    for n in range(3 * (len(blocks) // parts)):
+        for r in range(0, size, 64):
+            end = min(r + 64, size)
+            here, there = slice(n * size + r, n * size + end), slice(n % 3 * size + r, n % 3 * size + end)
+            value = 0.9 * momentum[here, :]
+            for k in range(parts):
+                value = value + mine[k] * blocks[n // 3 * parts + k][there, :]
+            new_momentum[here, :] = value
+            new_weight[here, :] = weight[here, :] - 0.1 * value
 
 
 def finish(sums, weight, momentum, chunks, ids):
@@ -395,9 +398,12 @@
     odd = jnp.array([0, 1, 4, 3, 2, 5, 6, 7], jnp.int32)
     ids = jnp.bitwise_xor(me, jnp.where(me % 2 == 0, even, odd))
     blocks = far[2:] + near + far[:2]
-    early = [pair for pair in upper_pairs(parts) if pair[1] < EARLY]
-    partial = gram([blocks[:EARLY] + [blocks[0]] * (parts - EARLY)], early, [], ids, 0)
-    return [blocks], [pair for pair in upper_pairs(parts) if pair[1] >= EARLY], [partial], ids
+    partials, first = [], 0
+    for last in (parts - 2, parts - 1):
+        pairs = [pair for pair in upper_pairs(parts) if first <= pair[1] < last]
+        partials = [gram([blocks[:last] + [blocks[0]] * (parts - last)], pairs, partials, ids, 0)]
+        first = last
+    return [blocks], [pair for pair in upper_pairs(parts) if pair[1] >= first], partials, ids
 
 
 def shards(activations, out_grads, weight, momentum):
@@ -411,7 +417,6 @@
     return finish(sums, weight, momentum, chunks, ids)
 
 
-EARLY = 4
 FIRST_VMEM, NEXT_VMEM, NEAR_VMEM = 30 << 20, 30 << 20, 38 << 20
 
 

time: 61.5 us -> 60.9 us (level)
  waiting for transfers between devices: 13.6 us -> 19.1 us
  starting transfers between devices: 15.5 us -> 10.3 us
  blocking collectives: 13.4 us -> 11.9 us
    ppermute x7, waiting for transfers between devices: 13.6 us -> 19.1 us  [send(): lax.ppermute(block, 'dp', [(r, r ^ flips[r % 2]) for r in range(parts)])]
    ppermute x7, starting transfers between devices: 15.5 us -> 10.3 us  [send(): lax.ppermute(block, 'dp', [(r, r ^ flips[r % 2]) for r in range(parts)])]
    all_to_all x1, blocking collectives: 13.4 us -> 11.9 us  [shards(): lax.all_to_all(sums, ('dp', 'chan'), split_axis=0, concat_axis=0, tiled=T...]
    pallas_call x2 -> x3, Pallas kernels: 2.14 us -> 2.85 us  [gram(): pl.pallas_call(functools.partial(gram_kernel, pairs, parts, devices), out...]
  transfers between devices with their start and end apart: 7 -> 7, of which waited for: 4 -> 5; matrix products, arithmetic and copies ran while one was open for 0% -> 0% of each run, Pallas kernels for 1% -> 3%
where the time goes in v3:
time: 60.9 us; the launch traced here: 60.7 us
  waiting for transfers between devices  19.1 us (31%)
  Pallas kernels  18.7 us (31%)
  blocking collectives  11.9 us (20%)
  starting transfers between devices  10.3 us (17%)
  between operations  0.7 us (1%)
    ppermute x7, waiting for transfers between devices, send(): lax.ppermute(block, 'dp', [(r, r ^ flips[r % 2]) for r in range(parts)])  19.1 us
    all_to_all x1, blocking collectives, shards(): lax.all_to_all(sums, ('dp', 'chan'), split_axis=0, concat_axis=0, tiled=T...  11.9 us
    ppermute x7, starting transfers between devices, send(): lax.ppermute(block, 'dp', [(r, r ^ flips[r % 2]) for r in range(parts)])  10.3 us
    pallas_call x1, Pallas kernels, near_blocks(): pl.pallas_call(functools.partial(near_kernel, [0, height // 8, height * 3...  8.8 us
    pallas_call x1, Pallas kernels, far_blocks(): pl.pallas_call(far_kernel, out_shape=[block] * 4, in_specs=[SM, VM, VM],...  5.22 us
    pallas_call x3, Pallas kernels, gram(): pl.pallas_call(functools.partial(gram_kernel, pairs, parts, devices), out...  2.85 us
    pallas_call x1, Pallas kernels, finish(): pl.pallas_call(functools.partial(final_kernel, parts), out_shape=[jax.Sha...  1.79 us
  transfers between devices with their start and end apart: 7, of which 5 were waited for; matrix products, arithmetic and copies ran while one was open for 0% of the time, Pallas kernels for 3%

profile of v3, /device:TPU:0, one launch (start us, length us, event | category | flops | bytes accessed | tf_op | source)
XLA Modules:
  0.0 60.7 jit_solution(10526484223332168602)
XLA Ops:
  0.6 8.8 %conv_near.1 = (f32[576,128]{1,0:T(8,128)S(1)}, f32[576,128]{1,0:T(8,128)S(1)}, f32[576,128]{1,0:T(8,128)S(1)}, f32[576,128]{1,0:T(8,128)S(1)}, bf16[32,8,32,512...) custom-call(s32[1]{0:T(128)} %bitcast.me_ref, bf16[8,32,32,128]{3,2,1,0:T(8,128)(2,1)} %g_hbm.1, ...), custom_call_target="tpu_custom_call" | custom-call | flops 4831838208 | bytes 10485760 | tf_op jit(solution)/shard_map/conv_near/pallas_call | solution.py:216
  9.4 0.0 copy-start.2
  9.5 0.0 copy-start.3
  9.5 0.0 copy-start
  9.5 0.0 copy-start.1
  9.5 5.2 %conv_far.1 = (f32[576,128]{1,0:T(8,128)S(1)}, f32[576,128]{1,0:T(8,128)S(1)}, f32[576,128]{1,0:T(8,128)S(1)}, f32[576,128]{1,0:T(8,128)S(1)}) custom-call(s32[1]{0:T(128)} %bitcast.me_ref, bf16[384,8704]{1,0:T(8,128)(2,1)S(1)} %get-tuple-element.14.gt, bf16[32,8,32,512]{3,2,1,0:T(8,128)(2,1)S(1)} %get-tuple-element.15.av), custom_call_target="tpu_custom_call" | custom-call | flops 4831838208 | bytes 1179648 | tf_op jit(solution)/shard_map/conv_far/pallas_call | solution.py:239
  14.7 0.6 collective-permute-start
  15.3 2.5 %collective-permute-start.1 = (f32[576,128]{1,0:T(8,128)S(1)}, f32[576,128]{1,0:T(8,128)S(1)}, u32[]{:S(2)}, u32[]{:S(2)}) collective-permute-start(f32[576,128]{1,0:T(8,128)S(1)} %get-tuple-element.18), channel_id=1, source_target_pairs={{0,8},{4,20},{8,0},{12,28},{16,24},{20,4},{24,16},{28,12},{1,9},{5... | collective-permute-start | bytes 884744 | tf_op jit(solution)/shard_map/ppermute | solution.py:376
  17.8 1.3 %collective-permute-start.2 = (f32[576,128]{1,0:T(8,128)S(1)}, f32[576,128]{1,0:T(8,128)S(1)}, u32[]{:S(2)}, u32[]{:S(2)}) collective-permute-start(f32[576,128]{1,0:T(8,128)S(1)} %get-tuple-element.19), channel_id=1, source_target_pairs={{0,12},{4,16},{8,4},{12,24},{16,28},{20,0},{24,20},{28,8},{1,13},{... | collective-permute-start | bytes 884744 | tf_op jit(solution)/shard_map/ppermute | solution.py:376
  19.1 0.5 collective-permute-start.3
  19.6 0.0 collective-permute-start.4
  19.6 0.0 collective-permute-done.rest_1_
  19.6 2.7 %collective-permute-start.5 = (f32[576,128]{1,0:T(8,128)S(1)}, f32[576,128]{1,0:T(8,128)S(1)}, u32[]{:S(2)}, u32[]{:S(2)}) collective-permute-start(f32[576,128]{1,0:T(8,128)S(1)} %get-tuple-element.22), channel_id=1, source_target_pairs={{0,24},{4,28},{8,16},{12,20},{16,8},{20,12},{24,0},{28,4},{1,25},{... | collective-permute-start | bytes 884744 | tf_op jit(solution)/shard_map/ppermute | solution.py:376
  22.3 1.7 %collective-permute-done.1.rest_2_ = f32[576,128]{1,0:T(8,128)S(1)} collective-permute-done((f32[576,128]{1,0:T(8,128)S(1)}, f32[576,128]{1,0:T(8,128)S(1)}, u32[]{:S(2)}, u32[]{:S(2)}) %collective-permute-start.1) | collective-permute-done | bytes 294944 | tf_op jit(solution)/shard_map/ppermute | solution.py:376
  24.0 2.7 %collective-permute-start.6 = (f32[576,128]{1,0:T(8,128)S(1)}, f32[576,128]{1,0:T(8,128)S(1)}, u32[]{:S(2)}, u32[]{:S(2)}) collective-permute-start(f32[576,128]{1,0:T(8,128)S(1)} %get-tuple-element.23), channel_id=1, source_target_pairs={{0,28},{4,24},{8,20},{12,16},{16,12},{20,8},{24,4},{28,0},{1,29},{... | collective-permute-start | bytes 884744 | tf_op jit(solution)/shard_map/ppermute | solution.py:376
  26.7 0.0 copy-done.2
  26.7 0.0 copy-done.3
  26.8 3.6 %collective-permute-done.2.rest_3_ = f32[576,128]{1,0:T(8,128)S(1)} collective-permute-done((f32[576,128]{1,0:T(8,128)S(1)}, f32[576,128]{1,0:T(8,128)S(1)}, u32[]{:S(2)}, u32[]{:S(2)}) %collective-permute-start.2) | collective-permute-done | bytes 294944 | tf_op jit(solution)/shard_map/ppermute | solution.py:376
  30.3 0.0 collective-permute-done.3.rest_4_
  30.3 4.4 %collective-permute-done.4.rest_5_ = f32[576,128]{1,0:T(8,128)S(1)} collective-permute-done((f32[576,128]{1,0:T(8,128)S(1)}, f32[576,128]{1,0:T(8,128)S(1)}, u32[]{:S(2)}, u32[]{:S(2)}) %collective-permute-start.4) | collective-permute-done | bytes 294944 | tf_op jit(solution)/shard_map/ppermute | solution.py:376
  34.7 1.1 %gram.3.rest_8_ = f32[1,128]{1,0:T(1,128)S(1)} custom-call(s32[8]{0:T(128)S(1)} %fusion.ids, f32[576,128]{1,0:T(8,128)S(1)} %get-tuple-element.16.rest_0_.rest_6_.rest_7_, f32[576,128]{1,0:T(8,128)S(1)} %collective-permute-done.rest_1_, f32[576,128]{1,0:T(8,128)S(1)} %collective-permute-done.1.rest_2_, f32[576,128]{1,0:T(8,128)S(1)} %collective-permute-done.2.rest_3_, ...), custom_call_target="tpu_custom_call" | custom-call | flops 3096576 | bytes 2359296 | tf_op jit(solution)/shard_map/gram/pallas_call | solution.py:293
  35.8 2.8 %collective-permute-done.5.rest_6_ = f32[576,128]{1,0:T(8,128)S(1)} collective-permute-done((f32[576,128]{1,0:T(8,128)S(1)}, f32[576,128]{1,0:T(8,128)S(1)}, u32[]{:S(2)}, u32[]{:S(2)}) %collective-permute-start.5) | collective-permute-done | bytes 294944 | tf_op jit(solution)/shard_map/ppermute | solution.py:376
  38.6 0.8 %gram.4.rest_8_ = f32[1,128]{1,0:T(1,128)S(1)} custom-call(s32[8]{0:T(128)S(1)} %fusion.ids, f32[576,128]{1,0:T(8,128)S(1)} %get-tuple-element.16.rest_0_.rest_6_.rest_7_, f32[576,128]{1,0:T(8,128)S(1)} %collective-permute-done.rest_1_, f32[576,128]{1,0:T(8,128)S(1)} %collective-permute-done.1.rest_2_, f32[576,128]{1,0:T(8,128)S(1)} %collective-permute-done.2.rest_3_, ...), custom_call_target="tpu_custom_call" | custom-call | flops 1032192 | bytes 2359296 | tf_op jit(solution)/shard_map/gram/pallas_call | solution.py:293
  39.5 6.6 %collective-permute-done.6.rest_7_ = f32[576,128]{1,0:T(8,128)S(1)} collective-permute-done((f32[576,128]{1,0:T(8,128)S(1)}, f32[576,128]{1,0:T(8,128)S(1)}, u32[]{:S(2)}, u32[]{:S(2)}) %collective-permute-start.6) | collective-permute-done | bytes 294944 | tf_op jit(solution)/shard_map/ppermute | solution.py:376
  46.1 0.9 %gram.5 = f32[32,1,128]{2,1,0:T(1,128)S(1)} custom-call(s32[8]{0:T(128)S(1)} %fusion.ids, f32[576,128]{1,0:T(8,128)S(1)} %get-tuple-element.16.rest_0_.rest_6_.rest_7_, f32[576,128]{1,0:T(8,128)S(1)} %collective-permute-done.rest_1_, f32[576,128]{1,0:T(8,128)S(1)} %collective-permute-done.1.rest_2_, f32[576,128]{1,0:T(8,128)S(1)} %collective-permute-done.2.rest_3_, ...), custom_call_target="tpu_custom_call" | custom-call | flops 1179648 | bytes 2359296 | tf_op jit(solution)/shard_map/gram/pallas_call | solution.py:293
  47.0 11.9 %all_to_all.5.sums = f32[32,1,128]{2,1,0:T(1,128)S(1)} all-to-all(f32[32,1,128]{2,1,0:T(1,128)S(1)} %gram.5), channel_id=1, replica_groups=mesh['dp'=8,'chan'=4] {'dp','chan'}, dimensions={0} | all-to-all | bytes 32768 | tf_op jit(solution)/shard_map/all_to_all | solution.py:416
  58.9 0.0 copy-done
  58.9 0.0 copy-done.1
  58.9 1.8 %final.1 = (f32[576,128]{1,0:T(8,128)}, f32[576,128]{1,0:T(8,128)}) custom-call(s32[8]{0:T(128)S(1)} %fusion.ids, f32[32,1,128]{2,1,0:T(1,128)S(1)} %all_to_all.5.sums, f32[576,128]{1,0:T(8,128)S(1)} %bitcast.14, f32[576,128]{1,0:T(8,128)S(1)} %bitcast.15, f32[576,128]{1,0:T(8,128)S(1)} %get-tuple-element.16.rest_0_.rest_6_.rest_7_, ...), custom_call_target="tpu_custom_call" | custom-call | flops 1179648 | bytes 3538944 | tf_op jit(solution)/shard_map/final/pallas_call | solution.py:359
  (1 shorter events, 0.0 us)
Async XLA Ops:
  9.4 17.3 %copy-start.2 = (s32[8]{0:T(128)S(1)}, s32[8]{0:T(128)}, u32[]{:S(2)}) copy-start(s32[8]{0:T(128)} %constant.31.clone) | copy-start | bytes 100
  9.5 17.3 %copy-start.3 = (s32[8]{0:T(128)S(1)}, s32[8]{0:T(128)}, u32[]{:S(2)}) copy-start(s32[8]{0:T(128)} %constant.30.clone) | copy-start | bytes 100
  9.5 49.4 %copy-start = (f32[64,3,3,128]{3,0,2,1:T(8,128)S(1)}, f32[64,3,3,128]{3,0,2,1:T(8,128)}, u32[]{:S(2)}) copy-start(f32[64,3,3,128]{3,0,2,1:T(8,128)} %param.8) | copy-start | bytes 884740
  9.5 49.4 %copy-start.1 = (f32[64,3,3,128]{3,0,2,1:T(8,128)S(1)}, f32[64,3,3,128]{3,0,2,1:T(8,128)}, u32[]{:S(2)}) copy-start(f32[64,3,3,128]{3,0,2,1:T(8,128)} %param.9) | copy-start | bytes 884740
  14.7 4.9 %collective-permute-start = (f32[576,128]{1,0:T(8,128)S(1)}, f32[576,128]{1,0:T(8,128)S(1)}, u32[]{:S(2)}, u32[]{:S(2)}) collective-permute-start(f32[576,128]{1,0:T(8,128)S(1)} %get-tuple-element.17), channel_id=1, source_target_pairs={{0,4},{4,0},{8,12},{12,8},{16,20},{20,16},{24,28},{28,24},{1,5},{5... | collective-permute-start | bytes 884744 | tf_op jit(solution)/shard_map/ppermute | solution.py:376
  15.3 8.7 %collective-permute-start.1 = (f32[576,128]{1,0:T(8,128)S(1)}, f32[576,128]{1,0:T(8,128)S(1)}, u32[]{:S(2)}, u32[]{:S(2)}) collective-permute-start(f32[576,128]{1,0:T(8,128)S(1)} %get-tuple-element.18), channel_id=1, source_target_pairs={{0,8},{4,20},{8,0},{12,28},{16,24},{20,4},{24,16},{28,12},{1,9},{5... | collective-permute-start | bytes 884744 | tf_op jit(solution)/shard_map/ppermute | solution.py:376
  17.8 12.5 %collective-permute-start.2 = (f32[576,128]{1,0:T(8,128)S(1)}, f32[576,128]{1,0:T(8,128)S(1)}, u32[]{:S(2)}, u32[]{:S(2)}) collective-permute-start(f32[576,128]{1,0:T(8,128)S(1)} %get-tuple-element.19), channel_id=1, source_target_pairs={{0,12},{4,16},{8,4},{12,24},{16,28},{20,0},{24,20},{28,8},{1,13},{... | collective-permute-start | bytes 884744 | tf_op jit(solution)/shard_map/ppermute | solution.py:376
  19.1 11.2 %collective-permute-start.3 = (f32[576,128]{1,0:T(8,128)S(1)}, f32[576,128]{1,0:T(8,128)S(1)}, u32[]{:S(2)}, u32[]{:S(2)}) collective-permute-start(f32[576,128]{1,0:T(8,128)S(1)} %get-tuple-element.20), channel_id=1, source_target_pairs={{0,16},{4,12},{8,24},{12,4},{16,0},{20,28},{24,8},{28,20},{1,17},{... | collective-permute-start | bytes 884744 | tf_op jit(solution)/shard_map/ppermute | solution.py:376
  19.6 15.1 %collective-permute-start.4 = (f32[576,128]{1,0:T(8,128)S(1)}, f32[576,128]{1,0:T(8,128)S(1)}, u32[]{:S(2)}, u32[]{:S(2)}) collective-permute-start(f32[576,128]{1,0:T(8,128)S(1)} %get-tuple-element.21), channel_id=1, source_target_pairs={{0,20},{4,8},{8,28},{12,0},{16,4},{20,24},{24,12},{28,16},{1,21},{... | collective-permute-start | bytes 884744 | tf_op jit(solution)/shard_map/ppermute | solution.py:376
  19.6 19.1 %collective-permute-start.5 = (f32[576,128]{1,0:T(8,128)S(1)}, f32[576,128]{1,0:T(8,128)S(1)}, u32[]{:S(2)}, u32[]{:S(2)}) collective-permute-start(f32[576,128]{1,0:T(8,128)S(1)} %get-tuple-element.22), channel_id=1, source_target_pairs={{0,24},{4,28},{8,16},{12,20},{16,8},{20,12},{24,0},{28,4},{1,25},{... | collective-permute-start | bytes 884744 | tf_op jit(solution)/shard_map/ppermute | solution.py:376
  24.0 22.1 %collective-permute-start.6 = (f32[576,128]{1,0:T(8,128)S(1)}, f32[576,128]{1,0:T(8,128)S(1)}, u32[]{:S(2)}, u32[]{:S(2)}) collective-permute-start(f32[576,128]{1,0:T(8,128)S(1)} %get-tuple-element.23), channel_id=1, source_target_pairs={{0,28},{4,24},{8,20},{12,16},{16,12},{20,8},{24,4},{28,0},{1,29},{... | collective-permute-start | bytes 884744 | tf_op jit(solution)/shard_map/ppermute | solution.py:376

commit v4 on v2

--- a/solution.py
+++ b/solution.py
@@ -130,9 +130,10 @@
     return jnp.concatenate([av[lo:hi, :, :, pl.ds(f, lanes)].reshape((hi - lo) * batch * width, lanes) for f in firsts], axis=1)
 
 
-def tile_store(value, i, outs, me, cols):
+def tile_store(value, i, taps, outs, me, cols):
+    i = taps.index(i)
     is_lower = jnp.bitwise_and(me, 1) == 0
-    depth = outs[0].shape[0] // 9
+    depth = outs[0].shape[0] // (3 * len(taps))
     for q in range(len(outs) // 2):
         for j in range(3):
             turned = value[j * cols : (j + 1) * cols, q * 2 * depth : (q + 1) * 2 * depth].T
@@ -142,7 +143,7 @@
             outs[2 * q + 1][here, :] = jnp.where(is_lower, upper, lower)
 
 
-def near_kernel(bounds, me_ref, g_hbm, a_hbm, *rest):
+def near_kernel(bounds, taps, me_ref, g_hbm, a_hbm, *rest):
     outs = rest[:4]
     av, gt, gv, acc, asem, gsem = rest[4:]
     height, batch, width, _ = av.shape
@@ -189,90 +190,100 @@
             if not is_end:
                 prepare(gends[n + 1], gends[n + 2])
             rhs = tile_columns(av, me // 2, (1 + jnp.bitwise_and(me, 1), 2 - jnp.bitwise_and(me, 1)), lo, hi)
-            for i in range(3):
-                here = slice(i * rows, (i + 1) * rows)
+            for i in taps:
+                here = slice(taps.index(i) * rows, (taps.index(i) + 1) * rows)
                 term = tile_terms(gt, rhs, lo, hi, flat, i)
                 if n > 0:
                     term = acc[here, :] + term
                 if is_end:
-                    tile_store(term, i, outs, me, cols)
+                    tile_store(term, i, taps, outs, me, cols)
                 else:
                     acc[here, :] = term
 
 
-def far_kernel(me_ref, gt, av, *outs):
+def held_kernel(near, taps, me_ref, gt, av, *outs):
     height, batch, width, _ = av.shape
     me = me_ref[0]
-    rhs = tile_columns(av, me // 2, (3, 0), 0, height)
-    for i in range(3):
-        tile_store(tile_terms(gt, rhs, 0, height, batch * width, i), i, outs, me, gt.shape[0] // 3)
-
-
-def near_blocks(a, g, me):
+    core = jnp.bitwise_and(me, 1)
+    rhs = tile_columns(av, me // 2, (1 + core, 2 - core) if near else (3, 0), 0, height)
+    for i in taps:
+        tile_store(tile_terms(gt, rhs, 0, height, batch * width, i), i, taps, outs, me, gt.shape[0] // 3)
+
+
+def near_blocks(a, g, me, taps):
     batch, height, width, cin = a.shape
     cols = g.shape[3]
     lanes, flat = cin // 4, batch * width
-    block = jax.ShapeDtypeStruct((9 * (lanes // 2), cols), f32)
+    block = jax.ShapeDtypeStruct((3 * len(taps) * (lanes // 2), cols), f32)
     res = pl.pallas_call(
-        functools.partial(near_kernel, [0, height // 8, height * 3 // 8, height * 11 // 16, height]),
+        functools.partial(near_kernel, [0, height // 8, height * 3 // 8, height * 11 // 16, height], taps),
         out_shape=[block] * 4 + [pltpu.VMEM((height, batch, width, cin), bf16), pltpu.VMEM((3 * cols, (height + 2) * flat), bf16)],
         in_specs=[SM, HB, HB],
         out_specs=[VM] * 6,
         scratch_shapes=[
             pltpu.VMEM((batch, height, width, cols), bf16),
-            pltpu.VMEM((9 * cols, 2 * lanes), f32),
+            pltpu.VMEM((3 * len(taps) * cols, 2 * lanes), f32),
             pltpu.SemaphoreType.DMA((height,)),
             pltpu.SemaphoreType.DMA((height,)),
         ],
         compiler_params=pltpu.CompilerParams(vmem_limit_bytes=NEAR_VMEM),
-        cost_estimate=pl.CostEstimate(flops=36 * cols * lanes * height * flat, bytes_accessed=2 * (a.size + g.size), transcendentals=0),
+        cost_estimate=pl.CostEstimate(flops=12 * len(taps) * cols * lanes * height * flat, bytes_accessed=2 * (a.size + g.size), transcendentals=0),
         name="conv_near",
     )(me, g, a)
     return list(res[:4]), res[4], res[5]
 
 
-def far_blocks(av, gt, me):
+def held_blocks(av, gt, me, near, taps):
     height, batch, width, cin = av.shape
     lanes = cin // 4
     cols = gt.shape[0] // 3
-    block = jax.ShapeDtypeStruct((9 * (lanes // 2), cols), f32)
+    block = jax.ShapeDtypeStruct((3 * len(taps) * (lanes // 2), cols), f32)
     return list(pl.pallas_call(
-        far_kernel,
+        functools.partial(held_kernel, near, taps),
         out_shape=[block] * 4,
         in_specs=[SM, VM, VM],
         out_specs=[VM] * 4,
         compiler_params=pltpu.CompilerParams(vmem_limit_bytes=NEXT_VMEM),
-        cost_estimate=pl.CostEstimate(flops=36 * cols * lanes * height * batch * width, bytes_accessed=72 * lanes * cols, transcendentals=0),
-        name="conv_far",
+        cost_estimate=pl.CostEstimate(flops=12 * len(taps) * cols * lanes * height * batch * width, bytes_accessed=24 * len(taps) * lanes * cols, transcendentals=0),
+        name="conv_near_rest" if near else "conv_far",
     )(me, gt, av))
 
 
-def gram_kernel(pairs, parts, devices, ids, *rest):
-    blocks, out, rowsums = rest[:-2], rest[-2], rest[-1]
-    chunks = len(blocks) // parts
-    before = blocks[chunks * parts :]
-    length, cols = blocks[0].shape
+def replica_of(me, flips, k):
+    even, odd = flips[k]
+    return jnp.bitwise_xor(me, even + jnp.bitwise_and(me, 1) * (odd - even))
+
+
+def gram_kernel(jobs, pieces, flips, devices, me_ref, *rest):
+    parts = len(pieces)
+    count = 1 + max(n for piece in pieces for _, _, n in piece)
+    arrays, before, (out, rowsums) = rest[:count], rest[count:-2], rest[-2:]
+    me = me_ref[0]
+    cols = arrays[0].shape[1]
     rowsums[...] = jnp.zeros_like(rowsums)
-    for first in range(0, len(pairs), 16):
-        some = pairs[first : first + 16]
-        names = sorted({n for pair in some for n in pair})
-        sums = [jnp.zeros((8, cols), f32) for _ in some]
-        for c in range(chunks):
+    size = rowsums.shape[0]
+    number = lax.broadcasted_iota(jnp.int32, (size, 128), 0)
+    at = jnp.full((size, 128), -1, jnp.int32)
+    row = 0
+    for lo, hi, pairs in jobs:
+        for first in range(0, len(pairs), 16):
+            some = pairs[first : first + 16]
+            held = {}
+            for k in sorted({n for pair in some for n in pair}):
+                ((start, _, n),) = [p for p in pieces[k] if p[0] <= lo and hi <= p[1]]
+                held[k] = (arrays[n], lo - start)
+
             def body(i, sums):
-                here = pl.ds(pl.multiple_of(i * 8, 8), 8)
-                x = {k: blocks[c * parts + k][here, :] for k in names}
+                x = {k: ref[pl.ds(pl.multiple_of(i * 8, 8) + skip, 8), :] for k, (ref, skip) in held.items()}
                 return [s + x[k] * x[l] for s, (k, l) in zip(sums, some)]
 
-            sums = lax.fori_loop(0, length // 8, body, sums, unroll=8)
-        for s, (k, l) in zip(sums, some):
-            rowsums[k * parts + l : k * parts + l + 1, :] = jnp.sum(s, axis=0, keepdims=True)
-    number = lax.broadcasted_iota(jnp.int32, (parts * parts, 128), 0)
-    a, b = jnp.zeros_like(number), jnp.zeros_like(number)
-    for k in range(parts):
-        a = jnp.where(number // parts == k, ids[k], a)
-        b = jnp.where(number % parts == k, ids[k], b)
-    at = jnp.minimum(a, b) * parts + jnp.maximum(a, b)
-    place = lax.broadcasted_iota(jnp.int32, (parts * parts, 128), 1)
+            sums = lax.fori_loop(0, (hi - lo) // 8, body, [jnp.zeros((8, cols), f32) for _ in some], unroll=8)
+            for s, (k, l) in zip(sums, some):
+                rowsums[row : row + 1, :] = jnp.sum(s, axis=0, keepdims=True)
+                a, b = replica_of(me, flips, k), replica_of(me, flips, l)
+                at = jnp.where(number == row, jnp.minimum(a, b) * parts + jnp.maximum(a, b), at)
+                row += 1
+    place = lax.broadcasted_iota(jnp.int32, (size, 128), 1)
     values = jnp.sum(rowsums[...], axis=1, keepdims=True)
     for r in range(out.shape[-2]):
         total = jnp.sum(jnp.where(at == place + r * 128, values, 0.0), axis=0, keepdims=True)
@@ -285,21 +296,25 @@
                 out[r : r + 1, :] = total
 
 
-def gram(chunks, pairs, before, ids, devices):
-    parts = len(chunks[0])
+def gram(jobs, pieces, arrays, before, me, flips, devices):
+    parts = len(pieces)
+    names = [{n for pair in pairs for n in pair} for _, _, pairs in jobs]
+    used = sorted({n for k in range(parts) for lo, hi, n in pieces[k] for (jlo, jhi, _), ks in zip(jobs, names) if k in ks and lo <= jlo and jhi <= hi})
+    near = [[(lo, hi, used.index(n)) for lo, hi, n in piece if n in used] for piece in pieces]
     rows = -(-parts * parts // 128)
     shape = (devices, rows, 128) if devices else (rows, 128)
-    flat = [b for chunk in chunks for b in chunk]
+    size = -(-sum(len(pairs) for _, _, pairs in jobs) // 8) * 8
+    flat = [arrays[n] for n in used]
     return pl.pallas_call(
-        functools.partial(gram_kernel, pairs, parts, devices),
+        functools.partial(gram_kernel, jobs, near, flips, devices),
         out_shape=jax.ShapeDtypeStruct(shape, f32),
         in_specs=[SM] + [VM] * (len(flat) + len(before)),
         out_specs=VM,
-        scratch_shapes=[pltpu.VMEM((parts * parts, flat[0].shape[1]), f32)],
+        scratch_shapes=[pltpu.VMEM((size, flat[0].shape[1]), f32)],
         compiler_params=pltpu.CompilerParams(vmem_limit_bytes=NEXT_VMEM),
-        cost_estimate=pl.CostEstimate(flops=2 * flat[0].size * len(chunks) * len(pairs), bytes_accessed=4 * flat[0].size * len(flat), transcendentals=0),
+        cost_estimate=pl.CostEstimate(flops=2 * 128 * sum((hi - lo) * len(pairs) for lo, hi, pairs in jobs), bytes_accessed=sum(4 * x.size for x in flat), transcendentals=0),
         name="gram",
-    )(ids, *flat, *before)
+    )(me, *flat, *before)
 
 
 def mixes_of(sums, parts):
@@ -328,40 +343,40 @@
     return factors
 
 
-def final_kernel(parts, ids, sums, weight, momentum, *rest):
-    blocks, (new_weight, new_momentum) = rest[:-2], rest[-2:]
-    total = jnp.sum(sums[...], axis=0)
-    factors = mixes_of(total, parts)
+def final_kernel(pieces, flips, me_ref, sums, weight, momentum, *rest):
+    arrays, (new_weight, new_momentum) = rest[:-2], rest[-2:]
+    parts = len(pieces)
+    me = me_ref[0]
+    factors = mixes_of(jnp.sum(sums[...], axis=0), parts)
     mine = []
     for k in range(parts):
-        pick = factors[0]
+        pick, replica = factors[0], replica_of(me, flips, k)
         for r in range(1, parts):
-            pick = jnp.where(ids[k] == r, factors[r], pick)
+            pick = jnp.where(replica == r, factors[r], pick)
         mine.append(pick)
-    length = blocks[0].shape[0]
-    for c in range(len(blocks) // parts):
-        here = slice(c * length, (c + 1) * length)
+    step = weight.shape[0] // 9
+    for first in range(0, weight.shape[0], step):
+        here = slice(first, first + step)
         value = 0.9 * momentum[here, :]
         for k in range(parts):
-            value = value + mine[k] * blocks[c * parts + k][...]
+            ((lo, n),) = [(lo, n) for lo, hi, n in pieces[k] if lo <= first < hi]
+            value = value + mine[k] * arrays[n][first - lo : first - lo + step, :]
         new_momentum[here, :] = value
         new_weight[here, :] = weight[here, :] - 0.1 * value
 
 
-def finish(sums, weight, momentum, chunks, ids):
-    parts = len(chunks[0])
+def finish(sums, weight, momentum, pieces, arrays, me, flips):
     depth, cols = weight.shape[0], weight.shape[3]
     w, m = (jnp.transpose(x, (1, 2, 0, 3)).reshape(9 * depth, cols) for x in (weight, momentum))
-    flat = [b for chunk in chunks for b in chunk]
     outs = pl.pallas_call(
-        functools.partial(final_kernel, parts),
+        functools.partial(final_kernel, pieces, flips),
         out_shape=[jax.ShapeDtypeStruct(w.shape, f32)] * 2,
-        in_specs=[SM] + [VM] * (3 + len(flat)),
+        in_specs=[SM] + [VM] * (3 + len(arrays)),
         out_specs=[VM, VM],
         compiler_params=pltpu.CompilerParams(vmem_limit_bytes=NEXT_VMEM),
-        cost_estimate=pl.CostEstimate(flops=2 * w.size * parts, bytes_accessed=4 * w.size * (parts + 4), transcendentals=0),
+        cost_estimate=pl.CostEstimate(flops=2 * w.size * len(pieces), bytes_accessed=4 * w.size * (len(pieces) + 4), transcendentals=0),
         name="final",
-    )(ids, sums, w, m, *flat)
+    )(me, sums, w, m, *arrays)
     return tuple(jnp.transpose(x.reshape(3, 3, depth, cols), (2, 0, 1, 3)) for x in outs)
 
 
@@ -373,7 +388,7 @@
     return lax.ppermute(block, "dp", [(r, r ^ flips[r % 2]) for r in range(parts)])
 
 
-def by_rows(activations, out_grads, me, parts):
+def by_rows(activations, out_grads, me, parts, devices):
     def exchange(blocks):
         blocks = [b.reshape(-1, b.shape[2]) for b in blocks]
         return blocks[:1] + [send(blocks[k], parts, (k, k)) for k in range(1, parts)]
@@ -382,22 +397,36 @@
     middle = exchange(middle)
     lower = exchange(conv_next(av, gt, me, 1, parts))
     upper = exchange(conv_next(av, gt, me, -1, parts))
-    return [lower, middle, upper], upper_pairs(parts), [], jnp.bitwise_xor(me, jnp.arange(parts, dtype=jnp.int32))
-
-
-def by_chips(activations, out_grads, me, parts):
-    flips = [(2, 4), (3, 5), (4, 2), (5, 3)]
-    near, av, gt = near_blocks(activations, out_grads, me)
-    near = [send(block, parts, flip) for block, flip in zip(near, flips)]
-    far = far_blocks(av, gt, me)
-    far = [send(far[k], parts, (6 + k, 6 + k)) for k in range(2)] + [far[2], send(far[3], parts, (1, 1))]
-    even = jnp.array([0, 1, 2, 5, 4, 3, 6, 7], jnp.int32)
-    odd = jnp.array([0, 1, 4, 3, 2, 5, 6, 7], jnp.int32)
-    ids = jnp.bitwise_xor(me, jnp.where(me % 2 == 0, even, odd))
-    blocks = far[2:] + near + far[:2]
-    early = [pair for pair in upper_pairs(parts) if pair[1] < EARLY]
-    partial = gram([blocks[:EARLY] + [blocks[0]] * (parts - EARLY)], early, [], ids, 0)
-    return [blocks], [pair for pair in upper_pairs(parts) if pair[1] >= EARLY], [partial], ids
+    size = middle[0].shape[0]
+    pieces = [[(i * size, (i + 1) * size, i * parts + k) for i in range(3)] for k in range(parts)]
+    arrays, flips, partial = lower + middle + upper, [(k, k) for k in range(parts)], []
+    for i in (1, 0, 2):
+        job = (i * size, (i + 1) * size, upper_pairs(parts))
+        partial = [gram([job], pieces, arrays, partial, me, flips, devices if i == 2 else 0)]
+    return partial[0], pieces, arrays, flips
+
+
+def by_chips(activations, out_grads, me, parts, devices):
+    targets = [(2, 4), (3, 5), (4, 2), (5, 3)]
+    near, av, gt = near_blocks(activations, out_grads, me, (0, 1))
+    near = [send(block, parts, t) for block, t in zip(near, targets)]
+    far = held_blocks(av, gt, me, False, (0, 1, 2))
+    own = [far[2], send(far[3], parts, (1, 1))]
+    far = [send(far[k], parts, (6 + k, 6 + k)) for k in range(2)]
+    rest = held_blocks(av, gt, me, True, (2,))
+    rest = [send(block, parts, t) for block, t in zip(rest, targets)]
+    flips = [(0, 0), (1, 1), (2, 4), (5, 3), (4, 2), (3, 5), (6, 6), (7, 7)]
+    arrays = own + near + far + rest
+    split, whole = near[0].shape[0], own[0].shape[0]
+    pieces = [[(0, whole, k)] if k < 2 or k > 5 else [(0, split, k), (split, whole, k + 6)] for k in range(parts)]
+
+    def pairs(low, high):
+        return [pair for pair in upper_pairs(parts) if low <= pair[1] < high]
+
+    sums = gram([(0, split, pairs(0, 6))], pieces, arrays, [], me, flips, 0)
+    sums = gram([(split, whole, pairs(0, 7)), (0, split, pairs(6, 7))], pieces, arrays, [sums], me, flips, 0)
+    sums = gram([(0, split, pairs(7, 8)), (split, whole, pairs(7, 8))], pieces, arrays, [sums], me, flips, devices)
+    return sums, pieces, arrays, flips
 
 
 def shards(activations, out_grads, weight, momentum):
@@ -405,13 +434,11 @@
     devices = parts * lax.axis_size("chan")
     me = lax.axis_index("dp").reshape(1).astype(jnp.int32)
     four = parts == 8 and activations.shape[3] % 512 == 0
-    chunks, pairs, before, ids = (by_chips if four else by_rows)(activations, out_grads, me, parts)
-    sums = gram(chunks, pairs, before, ids, devices)
+    sums, pieces, arrays, flips = (by_chips if four else by_rows)(activations, out_grads, me, parts, devices)
     sums = lax.all_to_all(sums, ("dp", "chan"), split_axis=0, concat_axis=0, tiled=True)
-    return finish(sums, weight, momentum, chunks, ids)
-
-
-EARLY = 4
+    return finish(sums, weight, momentum, pieces, arrays, me, flips)
+
+
 FIRST_VMEM, NEXT_VMEM, NEAR_VMEM = 30 << 20, 30 << 20, 38 << 20
 
 

time: 61.5 us -> 60.7 us (0.987)
  waiting for transfers between devices: 13.6 us -> 17.8 us
  starting transfers between devices: 15.5 us -> 11.8 us
  Pallas kernels: 18.1 us -> 17 us
    ppermute x7 -> x11, waiting for transfers between devices: 13.6 us -> 17.8 us  [send(): lax.ppermute(block, 'dp', [(r, r ^ flips[r % 2]) for r in range(parts)])]
    ppermute x7 -> x11, starting transfers between devices: 15.5 us -> 11.8 us  [send(): lax.ppermute(block, 'dp', [(r, r ^ flips[r % 2]) for r in range(parts)])]
    pallas_call x1, Pallas kernels: 8.8 us -> 7.33 us  [near_blocks(): pl.pallas_call(functools.partial(near_kernel, [0, height // 8, height * 3...]
    pallas_call x4 -> x6, Pallas kernels: 9.31 us -> 9.67 us  [the longest x2 7.13 us: held_blocks(): pl.pallas_call(functools.partial(held_kernel, near, taps), out_shape=[blo...]
  transfers between devices with their start and end apart: 7 -> 11, of which waited for: 4 -> 3; matrix products, arithmetic and copies ran while one was open for 0% -> 0% of each run, Pallas kernels for 1% -> 13%
where the time goes in v4:
time: 60.7 us; the launch traced here: 60.5 us
  waiting for transfers between devices  17.8 us (29%)
  Pallas kernels  17 us (28%)
  blocking collectives  13.2 us (22%)
  starting transfers between devices  11.8 us (19%)
  between operations  0.69 us (1%)
    ppermute x11, waiting for transfers between devices, send(): lax.ppermute(block, 'dp', [(r, r ^ flips[r % 2]) for r in range(parts)])  17.8 us
    all_to_all x1, blocking collectives, shards(): lax.all_to_all(sums, ('dp', 'chan'), split_axis=0, concat_axis=0, tiled=T...  13.2 us
    ppermute x11, starting transfers between devices, send(): lax.ppermute(block, 'dp', [(r, r ^ flips[r % 2]) for r in range(parts)])  11.8 us
    pallas_call x1, Pallas kernels, near_blocks(): pl.pallas_call(functools.partial(near_kernel, [0, height // 8, height * 3...  7.33 us
    pallas_call x2, Pallas kernels, held_blocks(): pl.pallas_call(functools.partial(held_kernel, near, taps), out_shape=[blo...  7.13 us
    pallas_call x3, Pallas kernels, gram(): pl.pallas_call(functools.partial(gram_kernel, jobs, near, flips, devices)...  1.28 us
    pallas_call x1, Pallas kernels, finish(): pl.pallas_call(functools.partial(final_kernel, pieces, flips), out_shape=...  1.26 us
  transfers between devices with their start and end apart: 11, of which 3 were waited for; matrix products, arithmetic and copies ran while one was open for 0% of the time, Pallas kernels for 13%

profile of v4, /device:TPU:0, one launch (start us, length us, event | category | flops | bytes accessed | tf_op | source)
XLA Modules:
  0.0 60.5 jit_solution(9857836524386594920)
XLA Ops:
  0.6 7.3 %conv_near.1 = (f32[384,128]{1,0:T(8,128)S(1)}, f32[384,128]{1,0:T(8,128)S(1)}, f32[384,128]{1,0:T(8,128)S(1)}, f32[384,128]{1,0:T(8,128)S(1)}, bf16[32,8,32,512...) custom-call(s32[1]{0:T(128)} %bitcast.me_ref, bf16[8,32,32,128]{3,2,1,0:T(8,128)(2,1)} %g_hbm.1, ...), custom_call_target="tpu_custom_call" | custom-call | flops 3221225472 | bytes 10485760 | tf_op jit(solution)/shard_map/conv_near/pallas_call | solution.py:218
  8.0 3.0 %collective-permute-start.1 = (f32[384,128]{1,0:T(8,128)S(1)}, f32[384,128]{1,0:T(8,128)S(1)}, u32[]{:S(2)}, u32[]{:S(2)}) collective-permute-start(f32[384,128]{1,0:T(8,128)S(1)} %get-tuple-element.22), channel_id=1, source_target_pairs={{0,8},{4,20},{8,0},{12,28},{16,24},{20,4},{24,16},{28,12},{1,9},{5... | collective-permute-start | bytes 589832 | tf_op jit(solution)/shard_map/ppermute | solution.py:388
  11.0 0.7 %collective-permute-start.2 = (f32[384,128]{1,0:T(8,128)S(1)}, f32[384,128]{1,0:T(8,128)S(1)}, u32[]{:S(2)}, u32[]{:S(2)}) collective-permute-start(f32[384,128]{1,0:T(8,128)S(1)} %get-tuple-element.23), channel_id=1, source_target_pairs={{0,12},{4,16},{8,4},{12,24},{16,28},{20,0},{24,20},{28,8},{1,13},{... | collective-permute-start | bytes 589832 | tf_op jit(solution)/shard_map/ppermute | solution.py:388
  11.7 1.9 %conv_near_rest.1 = (f32[192,128]{1,0:T(8,128)S(1)}, f32[192,128]{1,0:T(8,128)S(1)}, f32[192,128]{1,0:T(8,128)S(1)}, f32[192,128]{1,0:T(8,128)S(1)}) custom-call(s32[1]{0:T(128)} %bitcast.me_ref, bf16[384,8704]{1,0:T(8,128)(2,1)S(1)} %get-tuple-element.18.gt, bf16[32,8,32,512]{3,2,1,0:T(8,128)(2,1)S(1)} %get-tuple-element.19.av), custom_call_target="tpu_custom_call" | custom-call | flops 1610612736 | bytes 393216 | tf_op jit(solution)/shard_map/conv_near_rest/pallas_call | solution.py:241
  13.6 0.0 copy-start
  13.6 0.0 copy-start.1
  13.6 0.6 collective-permute-start.7
  14.2 5.2 %conv_far.1 = (f32[576,128]{1,0:T(8,128)S(1)}, f32[576,128]{1,0:T(8,128)S(1)}, f32[576,128]{1,0:T(8,128)S(1)}, f32[576,128]{1,0:T(8,128)S(1)}) custom-call(s32[1]{0:T(128)} %bitcast.me_ref, bf16[384,8704]{1,0:T(8,128)(2,1)S(1)} %get-tuple-element.18.gt, bf16[32,8,32,512]{3,2,1,0:T(8,128)(2,1)S(1)} %get-tuple-element.19.av), custom_call_target="tpu_custom_call" | custom-call | flops 4831838208 | bytes 1179648 | tf_op jit(solution)/shard_map/conv_far/pallas_call | solution.py:241
  19.4 0.7 %collective-permute-start = (f32[576,128]{1,0:T(8,128)S(1)}, f32[576,128]{1,0:T(8,128)S(1)}, u32[]{:S(2)}, u32[]{:S(2)}) collective-permute-start(f32[576,128]{1,0:T(8,128)S(1)} %get-tuple-element.21), channel_id=1, source_target_pairs={{0,4},{4,0},{8,12},{12,8},{16,20},{20,16},{24,28},{28,24},{1,5},{5... | collective-permute-start | bytes 884744 | tf_op jit(solution)/shard_map/ppermute | solution.py:388
  20.1 1.6 %collective-permute-start.3 = (f32[384,128]{1,0:T(8,128)S(1)}, f32[384,128]{1,0:T(8,128)S(1)}, u32[]{:S(2)}, u32[]{:S(2)}) collective-permute-start(f32[384,128]{1,0:T(8,128)S(1)} %get-tuple-element.24), channel_id=1, source_target_pairs={{0,16},{4,12},{8,24},{12,4},{16,0},{20,28},{24,8},{28,20},{1,17},{... | collective-permute-start | bytes 589832 | tf_op jit(solution)/shard_map/ppermute | solution.py:388
  21.7 0.0 collective-permute-done.7.rest_7_.rest_8_
  21.7 0.0 collective-permute-start.4
  21.7 0.0 collective-permute-done.1.rest_2_
  21.7 1.3 %collective-permute-start.5 = (f32[576,128]{1,0:T(8,128)S(1)}, f32[576,128]{1,0:T(8,128)S(1)}, u32[]{:S(2)}, u32[]{:S(2)}) collective-permute-start(f32[576,128]{1,0:T(8,128)S(1)} %get-tuple-element.26), channel_id=1, source_target_pairs={{0,24},{4,28},{8,16},{12,20},{16,8},{20,12},{24,0},{28,4},{1,25},{... | collective-permute-start | bytes 884744 | tf_op jit(solution)/shard_map/ppermute | solution.py:388
  23.0 0.0 collective-permute-done.2.rest_3_
  23.0 1.5 %collective-permute-start.6 = (f32[576,128]{1,0:T(8,128)S(1)}, f32[576,128]{1,0:T(8,128)S(1)}, u32[]{:S(2)}, u32[]{:S(2)}) collective-permute-start(f32[576,128]{1,0:T(8,128)S(1)} %get-tuple-element.27), channel_id=1, source_target_pairs={{0,28},{4,24},{8,20},{12,16},{16,12},{20,8},{24,4},{28,0},{1,29},{... | collective-permute-start | bytes 884744 | tf_op jit(solution)/shard_map/ppermute | solution.py:388
  24.6 1.2 %collective-permute-done.3.rest_4_ = f32[384,128]{1,0:T(8,128)S(1)} collective-permute-done((f32[384,128]{1,0:T(8,128)S(1)}, f32[384,128]{1,0:T(8,128)S(1)}, u32[]{:S(2)}, u32[]{:S(2)}) %collective-permute-start.3) | collective-permute-done | bytes 196640 | tf_op jit(solution)/shard_map/ppermute | solution.py:388
  25.8 0.2 collective-permute-start.8
  26.0 14.6 %collective-permute-done.4.rest_5_ = f32[384,128]{1,0:T(8,128)S(1)} collective-permute-done((f32[384,128]{1,0:T(8,128)S(1)}, f32[384,128]{1,0:T(8,128)S(1)}, u32[]{:S(2)}, u32[]{:S(2)}) %collective-permute-start.4) | collective-permute-done | bytes 196640 | tf_op jit(solution)/shard_map/ppermute | solution.py:388
  40.6 0.0 collective-permute-start.9
  40.6 0.0 collective-permute-done.rest_1_
  40.6 2.2 %collective-permute-start.10 = (f32[192,128]{1,0:T(8,128)S(1)}, f32[192,128]{1,0:T(8,128)S(1)}, u32[]{:S(2)}, u32[]{:S(2)}) collective-permute-start(f32[192,128]{1,0:T(8,128)S(1)} %get-tuple-element.31), channel_id=1, source_target_pairs={{0,20},{4,8},{8,28},{12,0},{16,4},{20,24},{24,12},{28,16},{1,21},{... | collective-permute-start | bytes 294920 | tf_op jit(solution)/shard_map/ppermute | solution.py:388
  42.8 0.4 gram.3.rest_11_
  43.2 0.0 collective-permute-done.8.rest_8_.rest_9_
  43.2 2.0 %collective-permute-done.9.rest_9_.rest_10_ = f32[192,128]{1,0:T(8,128)S(1)} collective-permute-done((f32[192,128]{1,0:T(8,128)S(1)}, f32[192,128]{1,0:T(8,128)S(1)}, u32[]{:S(2)}, u32[]{:S(2)}) %collective-permute-start.9) | collective-permute-done | bytes 98336 | tf_op jit(solution)/shard_map/ppermute | solution.py:388
  45.2 0.0 collective-permute-done.10.rest_10_.rest_11_
  45.2 0.0 collective-permute-done.5.rest_6_
  45.2 0.5 gram.4.rest_12_
  45.7 0.0 collective-permute-done.6.rest_7_
  45.7 0.3 gram.5
  46.0 13.2 %all_to_all.5.sums = f32[32,1,128]{2,1,0:T(1,128)S(1)} all-to-all(f32[32,1,128]{2,1,0:T(1,128)S(1)} %gram.5), channel_id=1, replica_groups=mesh['dp'=8,'chan'=4] {'dp','chan'}, dimensions={0} | all-to-all | bytes 32768 | tf_op jit(solution)/shard_map/all_to_all | solution.py:438
  59.2 0.0 copy-done
  59.2 0.0 copy-done.1
  59.3 1.3 %final.1 = (f32[576,128]{1,0:T(8,128)}, f32[576,128]{1,0:T(8,128)}) custom-call(s32[1]{0:T(128)} %bitcast.me_ref, f32[32,1,128]{2,1,0:T(1,128)S(1)} %all_to_all.5.sums, f32[576,128]{1,0:T(8,128)S(1)} %bitcast.13, f32[576,128]{1,0:T(8,128)S(1)} %bitcast.14, f32[576,128]{1,0:T(8,128)S(1)} %get-tuple-element.20.rest_0_, ...), custom_call_target="tpu_custom_call" | custom-call | flops 1179648 | bytes 3538944 | tf_op jit(solution)/shard_map/final/pallas_call | solution.py:371
Async XLA Ops:
  8.0 13.8 %collective-permute-start.1 = (f32[384,128]{1,0:T(8,128)S(1)}, f32[384,128]{1,0:T(8,128)S(1)}, u32[]{:S(2)}, u32[]{:S(2)}) collective-permute-start(f32[384,128]{1,0:T(8,128)S(1)} %get-tuple-element.22), channel_id=1, source_target_pairs={{0,8},{4,20},{8,0},{12,28},{16,24},{20,4},{24,16},{28,12},{1,9},{5... | collective-permute-start | bytes 589832 | tf_op jit(solution)/shard_map/ppermute | solution.py:388
  11.0 12.0 %collective-permute-start.2 = (f32[384,128]{1,0:T(8,128)S(1)}, f32[384,128]{1,0:T(8,128)S(1)}, u32[]{:S(2)}, u32[]{:S(2)}) collective-permute-start(f32[384,128]{1,0:T(8,128)S(1)} %get-tuple-element.23), channel_id=1, source_target_pairs={{0,12},{4,16},{8,4},{12,24},{16,28},{20,0},{24,20},{28,8},{1,13},{... | collective-permute-start | bytes 589832 | tf_op jit(solution)/shard_map/ppermute | solution.py:388
  13.6 45.6 %copy-start = (f32[64,3,3,128]{3,0,2,1:T(8,128)S(1)}, f32[64,3,3,128]{3,0,2,1:T(8,128)}, u32[]{:S(2)}) copy-start(f32[64,3,3,128]{3,0,2,1:T(8,128)} %param.6) | copy-start | bytes 884740
  13.6 45.6 %copy-start.1 = (f32[64,3,3,128]{3,0,2,1:T(8,128)S(1)}, f32[64,3,3,128]{3,0,2,1:T(8,128)}, u32[]{:S(2)}) copy-start(f32[64,3,3,128]{3,0,2,1:T(8,128)} %param.7) | copy-start | bytes 884740
  13.6 8.1 %collective-permute-start.7 = (f32[192,128]{1,0:T(8,128)S(1)}, f32[192,128]{1,0:T(8,128)S(1)}, u32[]{:S(2)}, u32[]{:S(2)}) collective-permute-start(f32[192,128]{1,0:T(8,128)S(1)} %get-tuple-element.28), channel_id=1, source_target_pairs={{0,8},{4,20},{8,0},{12,28},{16,24},{20,4},{24,16},{28,12},{1,9},{5... | collective-permute-start | bytes 294920 | tf_op jit(solution)/shard_map/ppermute | solution.py:388
  19.4 21.2 %collective-permute-start = (f32[576,128]{1,0:T(8,128)S(1)}, f32[576,128]{1,0:T(8,128)S(1)}, u32[]{:S(2)}, u32[]{:S(2)}) collective-permute-start(f32[576,128]{1,0:T(8,128)S(1)} %get-tuple-element.21), channel_id=1, source_target_pairs={{0,4},{4,0},{8,12},{12,8},{16,20},{20,16},{24,28},{28,24},{1,5},{5... | collective-permute-start | bytes 884744 | tf_op jit(solution)/shard_map/ppermute | solution.py:388
  20.1 5.7 %collective-permute-start.3 = (f32[384,128]{1,0:T(8,128)S(1)}, f32[384,128]{1,0:T(8,128)S(1)}, u32[]{:S(2)}, u32[]{:S(2)}) collective-permute-start(f32[384,128]{1,0:T(8,128)S(1)} %get-tuple-element.24), channel_id=1, source_target_pairs={{0,16},{4,12},{8,24},{12,4},{16,0},{20,28},{24,8},{28,20},{1,17},{... | collective-permute-start | bytes 589832 | tf_op jit(solution)/shard_map/ppermute | solution.py:388
  21.7 18.9 %collective-permute-start.4 = (f32[384,128]{1,0:T(8,128)S(1)}, f32[384,128]{1,0:T(8,128)S(1)}, u32[]{:S(2)}, u32[]{:S(2)}) collective-permute-start(f32[384,128]{1,0:T(8,128)S(1)} %get-tuple-element.25), channel_id=1, source_target_pairs={{0,20},{4,8},{8,28},{12,0},{16,4},{20,24},{24,12},{28,16},{1,21},{... | collective-permute-start | bytes 589832 | tf_op jit(solution)/shard_map/ppermute | solution.py:388
  21.7 23.5 %collective-permute-start.5 = (f32[576,128]{1,0:T(8,128)S(1)}, f32[576,128]{1,0:T(8,128)S(1)}, u32[]{:S(2)}, u32[]{:S(2)}) collective-permute-start(f32[576,128]{1,0:T(8,128)S(1)} %get-tuple-element.26), channel_id=1, source_target_pairs={{0,24},{4,28},{8,16},{12,20},{16,8},{20,12},{24,0},{28,4},{1,25},{... | collective-permute-start | bytes 884744 | tf_op jit(solution)/shard_map/ppermute | solution.py:388
  23.0 22.7 %collective-permute-start.6 = (f32[576,128]{1,0:T(8,128)S(1)}, f32[576,128]{1,0:T(8,128)S(1)}, u32[]{:S(2)}, u32[]{:S(2)}) collective-permute-start(f32[576,128]{1,0:T(8,128)S(1)} %get-tuple-element.27), channel_id=1, source_target_pairs={{0,28},{4,24},{8,20},{12,16},{16,12},{20,8},{24,4},{28,0},{1,29},{... | collective-permute-start | bytes 884744 | tf_op jit(solution)/shard_map/ppermute | solution.py:388
  25.8 17.4 %collective-permute-start.8 = (f32[192,128]{1,0:T(8,128)S(1)}, f32[192,128]{1,0:T(8,128)S(1)}, u32[]{:S(2)}, u32[]{:S(2)}) collective-permute-start(f32[192,128]{1,0:T(8,128)S(1)} %get-tuple-element.29), channel_id=1, source_target_pairs={{0,12},{4,16},{8,4},{12,24},{16,28},{20,0},{24,20},{28,8},{1,13},{... | collective-permute-start | bytes 294920 | tf_op jit(solution)/shard_map/ppermute | solution.py:388
  40.6 4.6 %collective-permute-start.9 = (f32[192,128]{1,0:T(8,128)S(1)}, f32[192,128]{1,0:T(8,128)S(1)}, u32[]{:S(2)}, u32[]{:S(2)}) collective-permute-start(f32[192,128]{1,0:T(8,128)S(1)} %get-tuple-element.30), channel_id=1, source_target_pairs={{0,16},{4,12},{8,24},{12,4},{16,0},{20,28},{24,8},{28,20},{1,17},{... | collective-permute-start | bytes 294920 | tf_op jit(solution)/shard_map/ppermute | solution.py:388
  40.6 4.6 %collective-permute-start.10 = (f32[192,128]{1,0:T(8,128)S(1)}, f32[192,128]{1,0:T(8,128)S(1)}, u32[]{:S(2)}, u32[]{:S(2)}) collective-permute-start(f32[192,128]{1,0:T(8,128)S(1)} %get-tuple-element.31), channel_id=1, source_target_pairs={{0,20},{4,8},{8,28},{12,0},{16,4},{20,24},{24,12},{28,16},{1,21},{... | collective-permute-start | bytes 294920 | tf_op jit(solution)/shard_map/ppermute | solution.py:388

commit v5 on v4

--- a/solution.py
+++ b/solution.py
@@ -154,7 +154,12 @@
     gends = [0] + [min(b + 1, height) for b in bounds[1:]]
     gcopy = [pltpu.make_async_copy(g_hbm.at[:, h], gv.at[:, h], gsem.at[h]) for h in range(height)]
     acopy = [pltpu.make_async_copy(a_hbm.at[:, h], av.at[h], asem.at[h]) for h in range(height)]
-    for copy in gcopy[: gends[1]] + acopy[: bounds[1]] + gcopy[gends[1] :] + acopy[bounds[1] :]:
+    order = gcopy[: gends[1]]
+    for n in range(len(bounds) - 1):
+        order += acopy[bounds[n] : bounds[n + 1]]
+        if n + 2 < len(bounds):
+            order += gcopy[gends[n + 1] : gends[n + 2]]
+    for copy in order:
         copy.start()
     gt[:, 0:flat] = jnp.zeros((rows, flat), bf16)
     gt[:, (height + 1) * flat : (height + 2) * flat] = jnp.zeros((rows, flat), bf16)
@@ -216,7 +221,7 @@
     lanes, flat = cin // 4, batch * width
     block = jax.ShapeDtypeStruct((3 * len(taps) * (lanes // 2), cols), f32)
     res = pl.pallas_call(
-        functools.partial(near_kernel, [0, height // 8, height * 3 // 8, height * 11 // 16, height], taps),
+        functools.partial(near_kernel, [height * n // 32 for n in (0, 3, 8, 14, 20, 26, 32)], taps),
         out_shape=[block] * 4 + [pltpu.VMEM((height, batch, width, cin), bf16), pltpu.VMEM((3 * cols, (height + 2) * flat), bf16)],
         in_specs=[SM, HB, HB],
         out_specs=[VM] * 6,
@@ -408,24 +413,34 @@
 
 def by_chips(activations, out_grads, me, parts, devices):
     targets = [(2, 4), (3, 5), (4, 2), (5, 3)]
+
+    def near_out(blocks):
+        return [send(block, parts, t) for block, t in zip(blocks, targets)]
+
+    def far_out(blocks):
+        far = [send(blocks[k], parts, (6 + k, 6 + k)) for k in range(2)]
+        return [blocks[2], send(blocks[3], parts, (1, 1))], far
+
     near, av, gt = near_blocks(activations, out_grads, me, (0, 1))
-    near = [send(block, parts, t) for block, t in zip(near, targets)]
-    far = held_blocks(av, gt, me, False, (0, 1, 2))
-    own = [far[2], send(far[3], parts, (1, 1))]
-    far = [send(far[k], parts, (6 + k, 6 + k)) for k in range(2)]
+    near = near_out(near)
+    far = held_blocks(av, gt, me, False, (0, 1))
+    own, far = far_out(far)
     rest = held_blocks(av, gt, me, True, (2,))
-    rest = [send(block, parts, t) for block, t in zip(rest, targets)]
+    rest = near_out(rest)
+    tail = held_blocks(av, gt, me, False, (2,))
+    tail_own, tail = far_out(tail)
     flips = [(0, 0), (1, 1), (2, 4), (5, 3), (4, 2), (3, 5), (6, 6), (7, 7)]
-    arrays = own + near + far + rest
-    split, whole = near[0].shape[0], own[0].shape[0]
-    pieces = [[(0, whole, k)] if k < 2 or k > 5 else [(0, split, k), (split, whole, k + 6)] for k in range(parts)]
+    arrays = own + near + far + tail_own + rest + tail
+    split = near[0].shape[0]
+    whole = split + rest[0].shape[0]
+    pieces = [[(0, split, k), (split, whole, parts + k)] for k in range(parts)]
 
     def pairs(low, high):
         return [pair for pair in upper_pairs(parts) if low <= pair[1] < high]
 
     sums = gram([(0, split, pairs(0, 6))], pieces, arrays, [], me, flips, 0)
-    sums = gram([(split, whole, pairs(0, 7)), (0, split, pairs(6, 7))], pieces, arrays, [sums], me, flips, 0)
-    sums = gram([(0, split, pairs(7, 8)), (split, whole, pairs(7, 8))], pieces, arrays, [sums], me, flips, devices)
+    sums = gram([(0, split, pairs(6, 8))], pieces, arrays, [sums], me, flips, 0)
+    sums = gram([(split, whole, pairs(0, 8))], pieces, arrays, [sums], me, flips, devices)
     return sums, pieces, arrays, flips
 
 

time: 60.7 us -> 54.8 us (0.903)
  waiting for transfers between devices: 17.8 us -> 9.37 us
  starting transfers between devices: 11.8 us -> 15.7 us
  blocking collectives: 13.2 us -> 11.9 us
    ppermute x11 -> x14, waiting for transfers between devices: 17.8 us -> 9.37 us  [send(): lax.ppermute(block, 'dp', [(r, r ^ flips[r % 2]) for r in range(parts)])]
    ppermute x11 -> x14, starting transfers between devices: 11.8 us -> 15.7 us  [send(): lax.ppermute(block, 'dp', [(r, r ^ flips[r % 2]) for r in range(parts)])]
    all_to_all x1, blocking collectives: 13.2 us -> 11.9 us  [shards(): lax.all_to_all(sums, ('dp', 'chan'), split_axis=0, concat_axis=0, tiled=T...]
    pallas_call x2 -> x3, Pallas kernels: 7.13 us -> 7.39 us  [held_blocks(): pl.pallas_call(functools.partial(held_kernel, near, taps), out_shape=[blo...]
  transfers between devices with their start and end apart: 11 -> 14, of which waited for: 3 -> 7; matrix products, arithmetic and copies ran while one was open for 0% -> 0% of each run, Pallas kernels for 13% -> 15%
where the time goes in v5:
time: 54.8 us; the launch traced here: 54.6 us
  Pallas kernels  16.9 us (31%)
  starting transfers between devices  15.7 us (29%)
  blocking collectives  11.9 us (22%)
  waiting for transfers between devices  9.37 us (17%)
  between operations  0.69 us (1%)
    ppermute x14, starting transfers between devices, send(): lax.ppermute(block, 'dp', [(r, r ^ flips[r % 2]) for r in range(parts)])  15.7 us
    all_to_all x1, blocking collectives, shards(): lax.all_to_all(sums, ('dp', 'chan'), split_axis=0, concat_axis=0, tiled=T...  11.9 us
    ppermute x14, waiting for transfers between devices, send(): lax.ppermute(block, 'dp', [(r, r ^ flips[r % 2]) for r in range(parts)])  9.37 us
    pallas_call x3, Pallas kernels, held_blocks(): pl.pallas_call(functools.partial(held_kernel, near, taps), out_shape=[blo...  7.39 us
    pallas_call x1, Pallas kernels, near_blocks(): pl.pallas_call(functools.partial(near_kernel, [height * n // 32 for n in...  7 us
    pallas_call x1, Pallas kernels, finish(): pl.pallas_call(functools.partial(final_kernel, pieces, flips), out_shape=...  1.26 us
    pallas_call x3, Pallas kernels, gram(): pl.pallas_call(functools.partial(gram_kernel, jobs, near, flips, devices)...  1.23 us
  transfers between devices with their start and end apart: 14, of which 7 were waited for; matrix products, arithmetic and copies ran while one was open for 0% of the time, Pallas kernels for 15%

profile of v5, /device:TPU:0, one launch (start us, length us, event | category | flops | bytes accessed | tf_op | source)
XLA Modules:
  0.0 54.6 jit_solution(9763903450379571655)
XLA Ops:
  0.6 7.0 %conv_near.1 = (f32[384,128]{1,0:T(8,128)S(1)}, f32[384,128]{1,0:T(8,128)S(1)}, f32[384,128]{1,0:T(8,128)S(1)}, f32[384,128]{1,0:T(8,128)S(1)}, bf16[32,8,32,512...) custom-call(s32[1]{0:T(128)} %bitcast.me_ref, bf16[8,32,32,128]{3,2,1,0:T(8,128)(2,1)} %g_hbm.1, ...), custom_call_target="tpu_custom_call" | custom-call | flops 3221225472 | bytes 10485760 | tf_op jit(solution)/shard_map/conv_near/pallas_call | solution.py:223
  7.6 3.0 %collective-permute-start.8 = (f32[384,128]{1,0:T(8,128)S(1)}, f32[384,128]{1,0:T(8,128)S(1)}, u32[]{:S(2)}, u32[]{:S(2)}) collective-permute-start(f32[384,128]{1,0:T(8,128)S(1)} %get-tuple-element.34), channel_id=1, source_target_pairs={{0,8},{4,20},{8,0},{12,28},{16,24},{20,4},{24,16},{28,12},{1,9},{5... | collective-permute-start | bytes 589832 | tf_op jit(solution)/shard_map/ppermute | solution.py:393
  10.7 0.7 %collective-permute-start.9 = (f32[384,128]{1,0:T(8,128)S(1)}, f32[384,128]{1,0:T(8,128)S(1)}, u32[]{:S(2)}, u32[]{:S(2)}) collective-permute-start(f32[384,128]{1,0:T(8,128)S(1)} %get-tuple-element.35), channel_id=1, source_target_pairs={{0,12},{4,16},{8,4},{12,24},{16,28},{20,0},{24,20},{28,8},{1,13},{... | collective-permute-start | bytes 589832 | tf_op jit(solution)/shard_map/ppermute | solution.py:393
  11.4 0.9 %collective-permute-start.10 = (f32[384,128]{1,0:T(8,128)S(1)}, f32[384,128]{1,0:T(8,128)S(1)}, u32[]{:S(2)}, u32[]{:S(2)}) collective-permute-start(f32[384,128]{1,0:T(8,128)S(1)} %get-tuple-element.36), channel_id=1, source_target_pairs={{0,16},{4,12},{8,24},{12,4},{16,0},{20,28},{24,8},{28,20},{1,17},{... | collective-permute-start | bytes 589832 | tf_op jit(solution)/shard_map/ppermute | solution.py:393
  12.2 1.9 %conv_near_rest.1 = (f32[192,128]{1,0:T(8,128)S(1)}, f32[192,128]{1,0:T(8,128)S(1)}, f32[192,128]{1,0:T(8,128)S(1)}, f32[192,128]{1,0:T(8,128)S(1)}) custom-call(s32[1]{0:T(128)} %bitcast.me_ref, bf16[384,8704]{1,0:T(8,128)(2,1)S(1)} %get-tuple-element.22.gt, bf16[32,8,32,512]{3,2,1,0:T(8,128)(2,1)S(1)} %get-tuple-element.23.av), custom_call_target="tpu_custom_call" | custom-call | flops 1610612736 | bytes 393216 | tf_op jit(solution)/shard_map/conv_near_rest/pallas_call | solution.py:246
  14.2 0.5 %collective-permute-start.1 = (f32[192,128]{1,0:T(8,128)S(1)}, f32[192,128]{1,0:T(8,128)S(1)}, u32[]{:S(2)}, u32[]{:S(2)}) collective-permute-start(f32[192,128]{1,0:T(8,128)S(1)} %get-tuple-element.26), channel_id=1, source_target_pairs={{0,8},{4,20},{8,0},{12,28},{16,24},{20,4},{24,16},{28,12},{1,9},{5... | collective-permute-start | bytes 294920 | tf_op jit(solution)/shard_map/ppermute | solution.py:393
  14.7 1.2 %collective-permute-start.2 = (f32[192,128]{1,0:T(8,128)S(1)}, f32[192,128]{1,0:T(8,128)S(1)}, u32[]{:S(2)}, u32[]{:S(2)}) collective-permute-start(f32[192,128]{1,0:T(8,128)S(1)} %get-tuple-element.27), channel_id=1, source_target_pairs={{0,12},{4,16},{8,4},{12,24},{16,28},{20,0},{24,20},{28,8},{1,13},{... | collective-permute-start | bytes 294920 | tf_op jit(solution)/shard_map/ppermute | solution.py:393
  15.9 3.6 %conv_far.3 = (f32[384,128]{1,0:T(8,128)S(1)}, f32[384,128]{1,0:T(8,128)S(1)}, f32[384,128]{1,0:T(8,128)S(1)}, f32[384,128]{1,0:T(8,128)S(1)}) custom-call(s32[1]{0:T(128)} %bitcast.me_ref, bf16[384,8704]{1,0:T(8,128)(2,1)S(1)} %get-tuple-element.22.gt, bf16[32,8,32,512]{3,2,1,0:T(8,128)(2,1)S(1)} %get-tuple-element.23.av), custom_call_target="tpu_custom_call" | custom-call | flops 3221225472 | bytes 786432 | tf_op jit(solution)/shard_map/conv_far/pallas_call | solution.py:246
  19.5 0.1 collective-permute-done.1.rest_2_.rest_10_
  19.6 0.5 collective-permute-start.11
  20.1 0.1 collective-permute-done.2.rest_3_.rest_11_
  20.2 1.5 %collective-permute-start.7 = (f32[384,128]{1,0:T(8,128)S(1)}, f32[384,128]{1,0:T(8,128)S(1)}, u32[]{:S(2)}, u32[]{:S(2)}) collective-permute-start(f32[384,128]{1,0:T(8,128)S(1)} %get-tuple-element.33), channel_id=1, source_target_pairs={{0,4},{4,0},{8,12},{12,8},{16,20},{20,16},{24,28},{28,24},{1,5},{5... | collective-permute-start | bytes 589832 | tf_op jit(solution)/shard_map/ppermute | solution.py:393
  21.7 0.0 collective-permute-done.8.rest_2_
  21.7 1.6 %collective-permute-start.12 = (f32[384,128]{1,0:T(8,128)S(1)}, f32[384,128]{1,0:T(8,128)S(1)}, u32[]{:S(2)}, u32[]{:S(2)}) collective-permute-start(f32[384,128]{1,0:T(8,128)S(1)} %get-tuple-element.38), channel_id=1, source_target_pairs={{0,24},{4,28},{8,16},{12,20},{16,8},{20,12},{24,0},{28,4},{1,25},{... | collective-permute-start | bytes 589832 | tf_op jit(solution)/shard_map/ppermute | solution.py:393
  23.4 0.0 collective-permute-done.9.rest_3_
  23.4 0.0 copy-start
  23.4 0.0 copy-start.1
  23.4 0.7 %collective-permute-start.13 = (f32[384,128]{1,0:T(8,128)S(1)}, f32[384,128]{1,0:T(8,128)S(1)}, u32[]{:S(2)}, u32[]{:S(2)}) collective-permute-start(f32[384,128]{1,0:T(8,128)S(1)} %get-tuple-element.39), channel_id=1, source_target_pairs={{0,28},{4,24},{8,20},{12,16},{16,12},{20,8},{24,4},{28,0},{1,29},{... | collective-permute-start | bytes 589832 | tf_op jit(solution)/shard_map/ppermute | solution.py:393
  24.0 1.9 %conv_far.2 = (f32[192,128]{1,0:T(8,128)S(1)}, f32[192,128]{1,0:T(8,128)S(1)}, f32[192,128]{1,0:T(8,128)S(1)}, f32[192,128]{1,0:T(8,128)S(1)}) custom-call(s32[1]{0:T(128)} %bitcast.me_ref, bf16[384,8704]{1,0:T(8,128)(2,1)S(1)} %get-tuple-element.22.gt, bf16[32,8,32,512]{3,2,1,0:T(8,128)(2,1)S(1)} %get-tuple-element.23.av), custom_call_target="tpu_custom_call" | custom-call | flops 1610612736 | bytes 393216 | tf_op jit(solution)/shard_map/conv_far/pallas_call | solution.py:246
  26.0 0.0 collective-permute-done.10.rest_4_
  26.0 1.5 %collective-permute-start.3 = (f32[192,128]{1,0:T(8,128)S(1)}, f32[192,128]{1,0:T(8,128)S(1)}, u32[]{:S(2)}, u32[]{:S(2)}) collective-permute-start(f32[192,128]{1,0:T(8,128)S(1)} %get-tuple-element.28), channel_id=1, source_target_pairs={{0,16},{4,12},{8,24},{12,4},{16,0},{20,28},{24,8},{28,20},{1,17},{... | collective-permute-start | bytes 294920 | tf_op jit(solution)/shard_map/ppermute | solution.py:393
  27.5 0.0 collective-permute-done.11.rest_5_
  27.5 0.8 %collective-permute-start.4 = (f32[192,128]{1,0:T(8,128)S(1)}, f32[192,128]{1,0:T(8,128)S(1)}, u32[]{:S(2)}, u32[]{:S(2)}) collective-permute-start(f32[192,128]{1,0:T(8,128)S(1)} %get-tuple-element.29), channel_id=1, source_target_pairs={{0,20},{4,8},{8,28},{12,0},{16,4},{20,24},{24,12},{28,16},{1,21},{... | collective-permute-start | bytes 294920 | tf_op jit(solution)/shard_map/ppermute | solution.py:393
  28.3 0.0 collective-permute-done.7.rest_1_
  28.3 0.0 collective-permute-start
  28.3 2.2 %collective-permute-done.12.rest_6_ = f32[384,128]{1,0:T(8,128)S(1)} collective-permute-done((f32[384,128]{1,0:T(8,128)S(1)}, f32[384,128]{1,0:T(8,128)S(1)}, u32[]{:S(2)}, u32[]{:S(2)}) %collective-permute-start.12) | collective-permute-done | bytes 196640 | tf_op jit(solution)/shard_map/ppermute | solution.py:393
  30.5 1.7 %collective-permute-start.5 = (f32[192,128]{1,0:T(8,128)S(1)}, f32[192,128]{1,0:T(8,128)S(1)}, u32[]{:S(2)}, u32[]{:S(2)}) collective-permute-start(f32[192,128]{1,0:T(8,128)S(1)} %get-tuple-element.30), channel_id=1, source_target_pairs={{0,24},{4,28},{8,16},{12,20},{16,8},{20,12},{24,0},{28,4},{1,25},{... | collective-permute-start | bytes 294920 | tf_op jit(solution)/shard_map/ppermute | solution.py:393
  32.1 2.5 %collective-permute-done.13.rest_7_ = f32[384,128]{1,0:T(8,128)S(1)} collective-permute-done((f32[384,128]{1,0:T(8,128)S(1)}, f32[384,128]{1,0:T(8,128)S(1)}, u32[]{:S(2)}, u32[]{:S(2)}) %collective-permute-start.13) | collective-permute-done | bytes 196640 | tf_op jit(solution)/shard_map/ppermute | solution.py:393
  34.7 1.1 %collective-permute-start.6 = (f32[192,128]{1,0:T(8,128)S(1)}, f32[192,128]{1,0:T(8,128)S(1)}, u32[]{:S(2)}, u32[]{:S(2)}) collective-permute-start(f32[192,128]{1,0:T(8,128)S(1)} %get-tuple-element.31), channel_id=1, source_target_pairs={{0,28},{4,24},{8,20},{12,16},{16,12},{20,8},{24,4},{28,0},{1,29},{... | collective-permute-start | bytes 294920 | tf_op jit(solution)/shard_map/ppermute | solution.py:393
  35.7 0.4 gram.3.rest_8_
  36.2 0.3 gram.4.rest_8_
  36.5 0.0 collective-permute-done.3.rest_4_.rest_12_
  36.5 0.3 collective-permute-done.4.rest_5_.rest_13_
  36.8 0.0 collective-permute-done.rest_1_.rest_9_
  36.8 0.3 collective-permute-done.5.rest_6_.rest_14_
  37.1 3.9 %collective-permute-done.6.rest_7_.rest_15_ = f32[192,128]{1,0:T(8,128)S(1)} collective-permute-done((f32[192,128]{1,0:T(8,128)S(1)}, f32[192,128]{1,0:T(8,128)S(1)}, u32[]{:S(2)}, u32[]{:S(2)}) %collective-permute-start.6) | collective-permute-done | bytes 98336 | tf_op jit(solution)/shard_map/ppermute | solution.py:393
  41.0 0.4 gram.5
  41.4 11.9 %all_to_all.5.sums = f32[32,1,128]{2,1,0:T(1,128)S(1)} all-to-all(f32[32,1,128]{2,1,0:T(1,128)S(1)} %gram.5), channel_id=1, replica_groups=mesh['dp'=8,'chan'=4] {'dp','chan'}, dimensions={0} | all-to-all | bytes 32768 | tf_op jit(solution)/shard_map/all_to_all | solution.py:453
  53.3 0.0 copy-done
  53.3 0.0 copy-done.1
  53.3 1.3 %final.1 = (f32[576,128]{1,0:T(8,128)}, f32[576,128]{1,0:T(8,128)}) custom-call(s32[1]{0:T(128)} %bitcast.me_ref, f32[32,1,128]{2,1,0:T(1,128)S(1)} %all_to_all.5.sums, f32[576,128]{1,0:T(8,128)S(1)} %bitcast.13, f32[576,128]{1,0:T(8,128)S(1)} %bitcast.14, f32[384,128]{1,0:T(8,128)S(1)} %get-tuple-element.32.rest_0_, ...), custom_call_target="tpu_custom_call" | custom-call | flops 1179648 | bytes 3538944 | tf_op jit(solution)/shard_map/final/pallas_call | solution.py:376
Async XLA Ops:
  7.6 14.1 %collective-permute-start.8 = (f32[384,128]{1,0:T(8,128)S(1)}, f32[384,128]{1,0:T(8,128)S(1)}, u32[]{:S(2)}, u32[]{:S(2)}) collective-permute-start(f32[384,128]{1,0:T(8,128)S(1)} %get-tuple-element.34), channel_id=1, source_target_pairs={{0,8},{4,20},{8,0},{12,28},{16,24},{20,4},{24,16},{28,12},{1,9},{5... | collective-permute-start | bytes 589832 | tf_op jit(solution)/shard_map/ppermute | solution.py:393
  10.7 12.7 %collective-permute-start.9 = (f32[384,128]{1,0:T(8,128)S(1)}, f32[384,128]{1,0:T(8,128)S(1)}, u32[]{:S(2)}, u32[]{:S(2)}) collective-permute-start(f32[384,128]{1,0:T(8,128)S(1)} %get-tuple-element.35), channel_id=1, source_target_pairs={{0,12},{4,16},{8,4},{12,24},{16,28},{20,0},{24,20},{28,8},{1,13},{... | collective-permute-start | bytes 589832 | tf_op jit(solution)/shard_map/ppermute | solution.py:393
  11.4 14.6 %collective-permute-start.10 = (f32[384,128]{1,0:T(8,128)S(1)}, f32[384,128]{1,0:T(8,128)S(1)}, u32[]{:S(2)}, u32[]{:S(2)}) collective-permute-start(f32[384,128]{1,0:T(8,128)S(1)} %get-tuple-element.36), channel_id=1, source_target_pairs={{0,16},{4,12},{8,24},{12,4},{16,0},{20,28},{24,8},{28,20},{1,17},{... | collective-permute-start | bytes 589832 | tf_op jit(solution)/shard_map/ppermute | solution.py:393
  14.2 5.4 %collective-permute-start.1 = (f32[192,128]{1,0:T(8,128)S(1)}, f32[192,128]{1,0:T(8,128)S(1)}, u32[]{:S(2)}, u32[]{:S(2)}) collective-permute-start(f32[192,128]{1,0:T(8,128)S(1)} %get-tuple-element.26), channel_id=1, source_target_pairs={{0,8},{4,20},{8,0},{12,28},{16,24},{20,4},{24,16},{28,12},{1,9},{5... | collective-permute-start | bytes 294920 | tf_op jit(solution)/shard_map/ppermute | solution.py:393
  14.7 5.5 %collective-permute-start.2 = (f32[192,128]{1,0:T(8,128)S(1)}, f32[192,128]{1,0:T(8,128)S(1)}, u32[]{:S(2)}, u32[]{:S(2)}) collective-permute-start(f32[192,128]{1,0:T(8,128)S(1)} %get-tuple-element.27), channel_id=1, source_target_pairs={{0,12},{4,16},{8,4},{12,24},{16,28},{20,0},{24,20},{28,8},{1,13},{... | collective-permute-start | bytes 294920 | tf_op jit(solution)/shard_map/ppermute | solution.py:393
  19.6 7.9 %collective-permute-start.11 = (f32[384,128]{1,0:T(8,128)S(1)}, f32[384,128]{1,0:T(8,128)S(1)}, u32[]{:S(2)}, u32[]{:S(2)}) collective-permute-start(f32[384,128]{1,0:T(8,128)S(1)} %get-tuple-element.37), channel_id=1, source_target_pairs={{0,20},{4,8},{8,28},{12,0},{16,4},{20,24},{24,12},{28,16},{1,21},{... | collective-permute-start | bytes 589832 | tf_op jit(solution)/shard_map/ppermute | solution.py:393
  20.2 8.1 %collective-permute-start.7 = (f32[384,128]{1,0:T(8,128)S(1)}, f32[384,128]{1,0:T(8,128)S(1)}, u32[]{:S(2)}, u32[]{:S(2)}) collective-permute-start(f32[384,128]{1,0:T(8,128)S(1)} %get-tuple-element.33), channel_id=1, source_target_pairs={{0,4},{4,0},{8,12},{12,8},{16,20},{20,16},{24,28},{28,24},{1,5},{5... | collective-permute-start | bytes 589832 | tf_op jit(solution)/shard_map/ppermute | solution.py:393
  21.7 8.8 %collective-permute-start.12 = (f32[384,128]{1,0:T(8,128)S(1)}, f32[384,128]{1,0:T(8,128)S(1)}, u32[]{:S(2)}, u32[]{:S(2)}) collective-permute-start(f32[384,128]{1,0:T(8,128)S(1)} %get-tuple-element.38), channel_id=1, source_target_pairs={{0,24},{4,28},{8,16},{12,20},{16,8},{20,12},{24,0},{28,4},{1,25},{... | collective-permute-start | bytes 589832 | tf_op jit(solution)/shard_map/ppermute | solution.py:393
  23.4 30.0 %copy-start = (f32[64,3,3,128]{3,0,2,1:T(8,128)S(1)}, f32[64,3,3,128]{3,0,2,1:T(8,128)}, u32[]{:S(2)}) copy-start(f32[64,3,3,128]{3,0,2,1:T(8,128)} %param.6) | copy-start | bytes 884740
  23.4 30.0 %copy-start.1 = (f32[64,3,3,128]{3,0,2,1:T(8,128)S(1)}, f32[64,3,3,128]{3,0,2,1:T(8,128)}, u32[]{:S(2)}) copy-start(f32[64,3,3,128]{3,0,2,1:T(8,128)} %param.7) | copy-start | bytes 884740
  23.4 11.3 %collective-permute-start.13 = (f32[384,128]{1,0:T(8,128)S(1)}, f32[384,128]{1,0:T(8,128)S(1)}, u32[]{:S(2)}, u32[]{:S(2)}) collective-permute-start(f32[384,128]{1,0:T(8,128)S(1)} %get-tuple-element.39), channel_id=1, source_target_pairs={{0,28},{4,24},{8,20},{12,16},{16,12},{20,8},{24,4},{28,0},{1,29},{... | collective-permute-start | bytes 589832 | tf_op jit(solution)/shard_map/ppermute | solution.py:393
  26.0 10.6 %collective-permute-start.3 = (f32[192,128]{1,0:T(8,128)S(1)}, f32[192,128]{1,0:T(8,128)S(1)}, u32[]{:S(2)}, u32[]{:S(2)}) collective-permute-start(f32[192,128]{1,0:T(8,128)S(1)} %get-tuple-element.28), channel_id=1, source_target_pairs={{0,16},{4,12},{8,24},{12,4},{16,0},{20,28},{24,8},{28,20},{1,17},{... | collective-permute-start | bytes 294920 | tf_op jit(solution)/shard_map/ppermute | solution.py:393
  27.5 9.3 %collective-permute-start.4 = (f32[192,128]{1,0:T(8,128)S(1)}, f32[192,128]{1,0:T(8,128)S(1)}, u32[]{:S(2)}, u32[]{:S(2)}) collective-permute-start(f32[192,128]{1,0:T(8,128)S(1)} %get-tuple-element.29), channel_id=1, source_target_pairs={{0,20},{4,8},{8,28},{12,0},{16,4},{20,24},{24,12},{28,16},{1,21},{... | collective-permute-start | bytes 294920 | tf_op jit(solution)/shard_map/ppermute | solution.py:393
  28.3 8.5 %collective-permute-start = (f32[192,128]{1,0:T(8,128)S(1)}, f32[192,128]{1,0:T(8,128)S(1)}, u32[]{:S(2)}, u32[]{:S(2)}) collective-permute-start(f32[192,128]{1,0:T(8,128)S(1)} %get-tuple-element.25), channel_id=1, source_target_pairs={{0,4},{4,0},{8,12},{12,8},{16,20},{20,16},{24,28},{28,24},{1,5},{5... | collective-permute-start | bytes 294920 | tf_op jit(solution)/shard_map/ppermute | solution.py:393
  30.5 6.6 %collective-permute-start.5 = (f32[192,128]{1,0:T(8,128)S(1)}, f32[192,128]{1,0:T(8,128)S(1)}, u32[]{:S(2)}, u32[]{:S(2)}) collective-permute-start(f32[192,128]{1,0:T(8,128)S(1)} %get-tuple-element.30), channel_id=1, source_target_pairs={{0,24},{4,28},{8,16},{12,20},{16,8},{20,12},{24,0},{28,4},{1,25},{... | collective-permute-start | bytes 294920 | tf_op jit(solution)/shard_map/ppermute | solution.py:393
  34.7 6.3 %collective-permute-start.6 = (f32[192,128]{1,0:T(8,128)S(1)}, f32[192,128]{1,0:T(8,128)S(1)}, u32[]{:S(2)}, u32[]{:S(2)}) collective-permute-start(f32[192,128]{1,0:T(8,128)S(1)} %get-tuple-element.31), channel_id=1, source_target_pairs={{0,28},{4,24},{8,20},{12,16},{16,12},{20,8},{24,4},{28,0},{1,29},{... | collective-permute-start | bytes 294920 | tf_op jit(solution)/shard_map/ppermute | solution.py:393

commit v6 on v5

--- a/solution.py
+++ b/solution.py
@@ -168,11 +168,11 @@
 
     def prepare(lo, hi):
         for h in range(lo, hi):
-            g = gv[:, h].reshape(flat, cols).astype(f32).T
+            g = gv[:, h].reshape(flat, cols).T
             here = slice((h + 1) * flat, (h + 2) * flat)
-            gt[0:cols, here] = jnp.where(is_last, 0.0, pltpu.roll(g, flat - 1, 1)).astype(bf16)
-            gt[cols : 2 * cols, here] = g.astype(bf16)
-            gt[2 * cols : 3 * cols, here] = jnp.where(is_first, 0.0, pltpu.roll(g, 1, 1)).astype(bf16)
+            gt[0:cols, here] = jnp.where(is_last, jnp.zeros_like(g), pltpu.roll(g, flat - 1, 1))
+            gt[cols : 2 * cols, here] = g
+            gt[2 * cols : 3 * cols, here] = jnp.where(is_first, jnp.zeros_like(g), pltpu.roll(g, 1, 1))
 
     for h in range(gends[1]):
         gcopy[h].wait()
@@ -349,8 +349,9 @@
 
 
 def final_kernel(pieces, flips, me_ref, sums, weight, momentum, *rest):
-    arrays, (new_weight, new_momentum) = rest[:-2], rest[-2:]
+    arrays, (weight_out, momentum_out, new_weight, new_momentum, sem) = rest[:-5], rest[-5:]
     parts = len(pieces)
+    copies = []
     me = me_ref[0]
     factors = mixes_of(jnp.sum(sums[...], axis=0), parts)
     mine = []
@@ -368,6 +369,13 @@
             value = value + mine[k] * arrays[n][first - lo : first - lo + step, :]
         new_momentum[here, :] = value
         new_weight[here, :] = weight[here, :] - 0.1 * value
+        if (first // step) % 3 == 2:
+            third = slice(first - 2 * step, first + step)
+            for held, out in ((new_weight, weight_out), (new_momentum, momentum_out)):
+                copies.append(pltpu.make_async_copy(held.at[third], out.at[third], sem.at[len(copies)]))
+                copies[-1].start()
+    for copy in copies:
+        copy.wait()
 
 
 def finish(sums, weight, momentum, pieces, arrays, me, flips):
@@ -377,7 +385,8 @@
         functools.partial(final_kernel, pieces, flips),
         out_shape=[jax.ShapeDtypeStruct(w.shape, f32)] * 2,
         in_specs=[SM] + [VM] * (3 + len(arrays)),
-        out_specs=[VM, VM],
+        out_specs=[HB, HB],
+        scratch_shapes=[pltpu.VMEM(w.shape, f32), pltpu.VMEM(w.shape, f32), pltpu.SemaphoreType.DMA((6,))],
         compiler_params=pltpu.CompilerParams(vmem_limit_bytes=NEXT_VMEM),
         cost_estimate=pl.CostEstimate(flops=2 * w.size * len(pieces), bytes_accessed=4 * w.size * (len(pieces) + 4), transcendentals=0),
         name="final",
@@ -440,7 +449,8 @@
 
     sums = gram([(0, split, pairs(0, 6))], pieces, arrays, [], me, flips, 0)
     sums = gram([(0, split, pairs(6, 8))], pieces, arrays, [sums], me, flips, 0)
-    sums = gram([(split, whole, pairs(0, 8))], pieces, arrays, [sums], me, flips, devices)
+    sums = gram([(split, whole, pairs(0, 7))], pieces, arrays, [sums], me, flips, 0)
+    sums = gram([(split, whole, pairs(7, 8))], pieces, arrays, [sums], me, flips, devices)
     return sums, pieces, arrays, flips
 
 

time: 54.8 us -> 54.3 us (level)
    pallas_call x3 -> x4, Pallas kernels: 1.23 us -> 1.3 us  [gram(): pl.pallas_call(functools.partial(gram_kernel, jobs, near, flips, devices)...]
  transfers between devices with their start and end apart: 14 -> 14, of which waited for: 7 -> 7; matrix products, arithmetic and copies ran while one was open for 0% -> 0% of each run, Pallas kernels for 15% -> 16%
where the time goes in v6:
time: 54.3 us; the launch traced here: 54.1 us
  Pallas kernels  16.8 us (31%)
  starting transfers between devices  15.7 us (29%)
  blocking collectives  11.9 us (22%)
  waiting for transfers between devices  9.01 us (17%)
  between operations  0.69 us (1%)
    ppermute x14, starting transfers between devices, send(): lax.ppermute(block, 'dp', [(r, r ^ flips[r % 2]) for r in range(parts)])  15.7 us
    all_to_all x1, blocking collectives, shards(): lax.all_to_all(sums, ('dp', 'chan'), split_axis=0, concat_axis=0, tiled=T...  11.9 us
    ppermute x14, waiting for transfers between devices, send(): lax.ppermute(block, 'dp', [(r, r ^ flips[r % 2]) for r in range(parts)])  9.01 us
    pallas_call x3, Pallas kernels, held_blocks(): pl.pallas_call(functools.partial(held_kernel, near, taps), out_shape=[blo...  7.39 us
    pallas_call x1, Pallas kernels, near_blocks(): pl.pallas_call(functools.partial(near_kernel, [height * n // 32 for n in...  6.91 us
    pallas_call x4, Pallas kernels, gram(): pl.pallas_call(functools.partial(gram_kernel, jobs, near, flips, devices)...  1.3 us
    pallas_call x1, Pallas kernels, finish(): pl.pallas_call(functools.partial(final_kernel, pieces, flips), out_shape=...  1.18 us
  transfers between devices with their start and end apart: 14, of which 7 were waited for; matrix products, arithmetic and copies ran while one was open for 0% of the time, Pallas kernels for 16%

profile of v6, /device:TPU:0, one launch (start us, length us, event | category | flops | bytes accessed | tf_op | source)
XLA Modules:
  0.0 54.1 jit_solution(9585743161666491387)
XLA Ops:
  0.6 6.9 %conv_near.1 = (f32[384,128]{1,0:T(8,128)S(1)}, f32[384,128]{1,0:T(8,128)S(1)}, f32[384,128]{1,0:T(8,128)S(1)}, f32[384,128]{1,0:T(8,128)S(1)}, bf16[32,8,32,512...) custom-call(s32[1]{0:T(128)} %bitcast.me_ref, bf16[8,32,32,128]{3,2,1,0:T(8,128)(2,1)} %g_hbm.1, ...), custom_call_target="tpu_custom_call" | custom-call | flops 3221225472 | bytes 10485760 | tf_op jit(solution)/shard_map/conv_near/pallas_call | solution.py:223
  7.5 3.0 %collective-permute-start.8 = (f32[384,128]{1,0:T(8,128)S(1)}, f32[384,128]{1,0:T(8,128)S(1)}, u32[]{:S(2)}, u32[]{:S(2)}) collective-permute-start(f32[384,128]{1,0:T(8,128)S(1)} %get-tuple-element.34), channel_id=1, source_target_pairs={{0,8},{4,20},{8,0},{12,28},{16,24},{20,4},{24,16},{28,12},{1,9},{5... | collective-permute-start | bytes 589832 | tf_op jit(solution)/shard_map/ppermute | solution.py:402
  10.6 0.7 %collective-permute-start.9 = (f32[384,128]{1,0:T(8,128)S(1)}, f32[384,128]{1,0:T(8,128)S(1)}, u32[]{:S(2)}, u32[]{:S(2)}) collective-permute-start(f32[384,128]{1,0:T(8,128)S(1)} %get-tuple-element.35), channel_id=1, source_target_pairs={{0,12},{4,16},{8,4},{12,24},{16,28},{20,0},{24,20},{28,8},{1,13},{... | collective-permute-start | bytes 589832 | tf_op jit(solution)/shard_map/ppermute | solution.py:402
  11.3 0.9 %collective-permute-start.10 = (f32[384,128]{1,0:T(8,128)S(1)}, f32[384,128]{1,0:T(8,128)S(1)}, u32[]{:S(2)}, u32[]{:S(2)}) collective-permute-start(f32[384,128]{1,0:T(8,128)S(1)} %get-tuple-element.36), channel_id=1, source_target_pairs={{0,16},{4,12},{8,24},{12,4},{16,0},{20,28},{24,8},{28,20},{1,17},{... | collective-permute-start | bytes 589832 | tf_op jit(solution)/shard_map/ppermute | solution.py:402
  12.1 1.9 %conv_near_rest.1 = (f32[192,128]{1,0:T(8,128)S(1)}, f32[192,128]{1,0:T(8,128)S(1)}, f32[192,128]{1,0:T(8,128)S(1)}, f32[192,128]{1,0:T(8,128)S(1)}) custom-call(s32[1]{0:T(128)} %bitcast.me_ref, bf16[384,8704]{1,0:T(8,128)(2,1)S(1)} %get-tuple-element.22.gt, bf16[32,8,32,512]{3,2,1,0:T(8,128)(2,1)S(1)} %get-tuple-element.23.av), custom_call_target="tpu_custom_call" | custom-call | flops 1610612736 | bytes 393216 | tf_op jit(solution)/shard_map/conv_near_rest/pallas_call | solution.py:246
  14.1 0.6 %collective-permute-start.1 = (f32[192,128]{1,0:T(8,128)S(1)}, f32[192,128]{1,0:T(8,128)S(1)}, u32[]{:S(2)}, u32[]{:S(2)}) collective-permute-start(f32[192,128]{1,0:T(8,128)S(1)} %get-tuple-element.26), channel_id=1, source_target_pairs={{0,8},{4,20},{8,0},{12,28},{16,24},{20,4},{24,16},{28,12},{1,9},{5... | collective-permute-start | bytes 294920 | tf_op jit(solution)/shard_map/ppermute | solution.py:402
  14.6 1.2 %collective-permute-start.2 = (f32[192,128]{1,0:T(8,128)S(1)}, f32[192,128]{1,0:T(8,128)S(1)}, u32[]{:S(2)}, u32[]{:S(2)}) collective-permute-start(f32[192,128]{1,0:T(8,128)S(1)} %get-tuple-element.27), channel_id=1, source_target_pairs={{0,12},{4,16},{8,4},{12,24},{16,28},{20,0},{24,20},{28,8},{1,13},{... | collective-permute-start | bytes 294920 | tf_op jit(solution)/shard_map/ppermute | solution.py:402
  15.8 3.6 %conv_far.3 = (f32[384,128]{1,0:T(8,128)S(1)}, f32[384,128]{1,0:T(8,128)S(1)}, f32[384,128]{1,0:T(8,128)S(1)}, f32[384,128]{1,0:T(8,128)S(1)}) custom-call(s32[1]{0:T(128)} %bitcast.me_ref, bf16[384,8704]{1,0:T(8,128)(2,1)S(1)} %get-tuple-element.22.gt, bf16[32,8,32,512]{3,2,1,0:T(8,128)(2,1)S(1)} %get-tuple-element.23.av), custom_call_target="tpu_custom_call" | custom-call | flops 3221225472 | bytes 786432 | tf_op jit(solution)/shard_map/conv_far/pallas_call | solution.py:246
  19.4 0.1 collective-permute-done.1.rest_2_.rest_10_
  19.5 0.5 collective-permute-start.11
  20.0 0.1 collective-permute-done.2.rest_3_.rest_11_
  20.1 1.5 %collective-permute-start.7 = (f32[384,128]{1,0:T(8,128)S(1)}, f32[384,128]{1,0:T(8,128)S(1)}, u32[]{:S(2)}, u32[]{:S(2)}) collective-permute-start(f32[384,128]{1,0:T(8,128)S(1)} %get-tuple-element.33), channel_id=1, source_target_pairs={{0,4},{4,0},{8,12},{12,8},{16,20},{20,16},{24,28},{28,24},{1,5},{5... | collective-permute-start | bytes 589832 | tf_op jit(solution)/shard_map/ppermute | solution.py:402
  21.6 0.0 collective-permute-done.8.rest_2_
  21.6 1.6 %collective-permute-start.12 = (f32[384,128]{1,0:T(8,128)S(1)}, f32[384,128]{1,0:T(8,128)S(1)}, u32[]{:S(2)}, u32[]{:S(2)}) collective-permute-start(f32[384,128]{1,0:T(8,128)S(1)} %get-tuple-element.38), channel_id=1, source_target_pairs={{0,24},{4,28},{8,16},{12,20},{16,8},{20,12},{24,0},{28,4},{1,25},{... | collective-permute-start | bytes 589832 | tf_op jit(solution)/shard_map/ppermute | solution.py:402
  23.3 0.0 collective-permute-done.9.rest_3_
  23.3 0.0 copy-start
  23.3 0.0 copy-start.1
  23.3 0.7 %collective-permute-start.13 = (f32[384,128]{1,0:T(8,128)S(1)}, f32[384,128]{1,0:T(8,128)S(1)}, u32[]{:S(2)}, u32[]{:S(2)}) collective-permute-start(f32[384,128]{1,0:T(8,128)S(1)} %get-tuple-element.39), channel_id=1, source_target_pairs={{0,28},{4,24},{8,20},{12,16},{16,12},{20,8},{24,4},{28,0},{1,29},{... | collective-permute-start | bytes 589832 | tf_op jit(solution)/shard_map/ppermute | solution.py:402
  24.0 1.9 %conv_far.2 = (f32[192,128]{1,0:T(8,128)S(1)}, f32[192,128]{1,0:T(8,128)S(1)}, f32[192,128]{1,0:T(8,128)S(1)}, f32[192,128]{1,0:T(8,128)S(1)}) custom-call(s32[1]{0:T(128)} %bitcast.me_ref, bf16[384,8704]{1,0:T(8,128)(2,1)S(1)} %get-tuple-element.22.gt, bf16[32,8,32,512]{3,2,1,0:T(8,128)(2,1)S(1)} %get-tuple-element.23.av), custom_call_target="tpu_custom_call" | custom-call | flops 1610612736 | bytes 393216 | tf_op jit(solution)/shard_map/conv_far/pallas_call | solution.py:246
  25.9 0.0 collective-permute-done.10.rest_4_
  25.9 1.5 %collective-permute-start.3 = (f32[192,128]{1,0:T(8,128)S(1)}, f32[192,128]{1,0:T(8,128)S(1)}, u32[]{:S(2)}, u32[]{:S(2)}) collective-permute-start(f32[192,128]{1,0:T(8,128)S(1)} %get-tuple-element.28), channel_id=1, source_target_pairs={{0,16},{4,12},{8,24},{12,4},{16,0},{20,28},{24,8},{28,20},{1,17},{... | collective-permute-start | bytes 294920 | tf_op jit(solution)/shard_map/ppermute | solution.py:402
  27.4 0.0 collective-permute-done.11.rest_5_
  27.4 0.8 %collective-permute-start.4 = (f32[192,128]{1,0:T(8,128)S(1)}, f32[192,128]{1,0:T(8,128)S(1)}, u32[]{:S(2)}, u32[]{:S(2)}) collective-permute-start(f32[192,128]{1,0:T(8,128)S(1)} %get-tuple-element.29), channel_id=1, source_target_pairs={{0,20},{4,8},{8,28},{12,0},{16,4},{20,24},{24,12},{28,16},{1,21},{... | collective-permute-start | bytes 294920 | tf_op jit(solution)/shard_map/ppermute | solution.py:402
  28.2 0.0 collective-permute-done.7.rest_1_
  28.2 0.0 collective-permute-start
  28.2 2.2 %collective-permute-done.12.rest_6_ = f32[384,128]{1,0:T(8,128)S(1)} collective-permute-done((f32[384,128]{1,0:T(8,128)S(1)}, f32[384,128]{1,0:T(8,128)S(1)}, u32[]{:S(2)}, u32[]{:S(2)}) %collective-permute-start.12) | collective-permute-done | bytes 196640 | tf_op jit(solution)/shard_map/ppermute | solution.py:402
  30.4 1.7 %collective-permute-start.5 = (f32[192,128]{1,0:T(8,128)S(1)}, f32[192,128]{1,0:T(8,128)S(1)}, u32[]{:S(2)}, u32[]{:S(2)}) collective-permute-start(f32[192,128]{1,0:T(8,128)S(1)} %get-tuple-element.30), channel_id=1, source_target_pairs={{0,24},{4,28},{8,16},{12,20},{16,8},{20,12},{24,0},{28,4},{1,25},{... | collective-permute-start | bytes 294920 | tf_op jit(solution)/shard_map/ppermute | solution.py:402
  32.0 2.5 %collective-permute-done.13.rest_7_ = f32[384,128]{1,0:T(8,128)S(1)} collective-permute-done((f32[384,128]{1,0:T(8,128)S(1)}, f32[384,128]{1,0:T(8,128)S(1)}, u32[]{:S(2)}, u32[]{:S(2)}) %collective-permute-start.13) | collective-permute-done | bytes 196640 | tf_op jit(solution)/shard_map/ppermute | solution.py:402
  34.6 1.1 %collective-permute-start.6 = (f32[192,128]{1,0:T(8,128)S(1)}, f32[192,128]{1,0:T(8,128)S(1)}, u32[]{:S(2)}, u32[]{:S(2)}) collective-permute-start(f32[192,128]{1,0:T(8,128)S(1)} %get-tuple-element.31), channel_id=1, source_target_pairs={{0,28},{4,24},{8,20},{12,16},{16,12},{20,8},{24,4},{28,0},{1,29},{... | collective-permute-start | bytes 294920 | tf_op jit(solution)/shard_map/ppermute | solution.py:402
  35.6 0.4 gram.4.rest_8_
  36.1 0.3 gram.5.rest_7_
  36.4 0.0 collective-permute-done.3.rest_4_.rest_12_
  36.4 0.3 collective-permute-done.4.rest_5_.rest_13_
  36.7 0.0 collective-permute-done.rest_1_.rest_9_
  36.7 0.3 collective-permute-done.5.rest_6_.rest_14_
  37.0 0.3 gram.6.rest_8_
  37.3 3.6 %collective-permute-done.6.rest_7_.rest_15_ = f32[192,128]{1,0:T(8,128)S(1)} collective-permute-done((f32[192,128]{1,0:T(8,128)S(1)}, f32[192,128]{1,0:T(8,128)S(1)}, u32[]{:S(2)}, u32[]{:S(2)}) %collective-permute-start.6) | collective-permute-done | bytes 98336 | tf_op jit(solution)/shard_map/ppermute | solution.py:402
  40.9 0.2 gram.7
  41.0 11.9 %all_to_all.5.sums = f32[32,1,128]{2,1,0:T(1,128)S(1)} all-to-all(f32[32,1,128]{2,1,0:T(1,128)S(1)} %gram.7), channel_id=1, replica_groups=mesh['dp'=8,'chan'=4] {'dp','chan'}, dimensions={0} | all-to-all | bytes 32768 | tf_op jit(solution)/shard_map/all_to_all | solution.py:463
  53.0 0.0 copy-done
  53.0 0.0 copy-done.1
  53.0 1.2 %final.1 = (f32[576,128]{1,0:T(8,128)}, f32[576,128]{1,0:T(8,128)}) custom-call(s32[1]{0:T(128)} %bitcast.me_ref, f32[32,1,128]{2,1,0:T(1,128)S(1)} %all_to_all.5.sums, f32[576,128]{1,0:T(8,128)S(1)} %bitcast.13, f32[576,128]{1,0:T(8,128)S(1)} %bitcast.14, f32[384,128]{1,0:T(8,128)S(1)} %get-tuple-element.32.rest_0_, ...), custom_call_target="tpu_custom_call" | custom-call | flops 1179648 | bytes 3538944 | tf_op jit(solution)/shard_map/final/pallas_call | solution.py:384
Async XLA Ops:
  7.5 14.1 %collective-permute-start.8 = (f32[384,128]{1,0:T(8,128)S(1)}, f32[384,128]{1,0:T(8,128)S(1)}, u32[]{:S(2)}, u32[]{:S(2)}) collective-permute-start(f32[384,128]{1,0:T(8,128)S(1)} %get-tuple-element.34), channel_id=1, source_target_pairs={{0,8},{4,20},{8,0},{12,28},{16,24},{20,4},{24,16},{28,12},{1,9},{5... | collective-permute-start | bytes 589832 | tf_op jit(solution)/shard_map/ppermute | solution.py:402
  10.6 12.7 %collective-permute-start.9 = (f32[384,128]{1,0:T(8,128)S(1)}, f32[384,128]{1,0:T(8,128)S(1)}, u32[]{:S(2)}, u32[]{:S(2)}) collective-permute-start(f32[384,128]{1,0:T(8,128)S(1)} %get-tuple-element.35), channel_id=1, source_target_pairs={{0,12},{4,16},{8,4},{12,24},{16,28},{20,0},{24,20},{28,8},{1,13},{... | collective-permute-start | bytes 589832 | tf_op jit(solution)/shard_map/ppermute | solution.py:402
  11.3 14.6 %collective-permute-start.10 = (f32[384,128]{1,0:T(8,128)S(1)}, f32[384,128]{1,0:T(8,128)S(1)}, u32[]{:S(2)}, u32[]{:S(2)}) collective-permute-start(f32[384,128]{1,0:T(8,128)S(1)} %get-tuple-element.36), channel_id=1, source_target_pairs={{0,16},{4,12},{8,24},{12,4},{16,0},{20,28},{24,8},{28,20},{1,17},{... | collective-permute-start | bytes 589832 | tf_op jit(solution)/shard_map/ppermute | solution.py:402
  14.1 5.4 %collective-permute-start.1 = (f32[192,128]{1,0:T(8,128)S(1)}, f32[192,128]{1,0:T(8,128)S(1)}, u32[]{:S(2)}, u32[]{:S(2)}) collective-permute-start(f32[192,128]{1,0:T(8,128)S(1)} %get-tuple-element.26), channel_id=1, source_target_pairs={{0,8},{4,20},{8,0},{12,28},{16,24},{20,4},{24,16},{28,12},{1,9},{5... | collective-permute-start | bytes 294920 | tf_op jit(solution)/shard_map/ppermute | solution.py:402
  14.6 5.5 %collective-permute-start.2 = (f32[192,128]{1,0:T(8,128)S(1)}, f32[192,128]{1,0:T(8,128)S(1)}, u32[]{:S(2)}, u32[]{:S(2)}) collective-permute-start(f32[192,128]{1,0:T(8,128)S(1)} %get-tuple-element.27), channel_id=1, source_target_pairs={{0,12},{4,16},{8,4},{12,24},{16,28},{20,0},{24,20},{28,8},{1,13},{... | collective-permute-start | bytes 294920 | tf_op jit(solution)/shard_map/ppermute | solution.py:402
  19.5 7.9 %collective-permute-start.11 = (f32[384,128]{1,0:T(8,128)S(1)}, f32[384,128]{1,0:T(8,128)S(1)}, u32[]{:S(2)}, u32[]{:S(2)}) collective-permute-start(f32[384,128]{1,0:T(8,128)S(1)} %get-tuple-element.37), channel_id=1, source_target_pairs={{0,20},{4,8},{8,28},{12,0},{16,4},{20,24},{24,12},{28,16},{1,21},{... | collective-permute-start | bytes 589832 | tf_op jit(solution)/shard_map/ppermute | solution.py:402
  20.1 8.1 %collective-permute-start.7 = (f32[384,128]{1,0:T(8,128)S(1)}, f32[384,128]{1,0:T(8,128)S(1)}, u32[]{:S(2)}, u32[]{:S(2)}) collective-permute-start(f32[384,128]{1,0:T(8,128)S(1)} %get-tuple-element.33), channel_id=1, source_target_pairs={{0,4},{4,0},{8,12},{12,8},{16,20},{20,16},{24,28},{28,24},{1,5},{5... | collective-permute-start | bytes 589832 | tf_op jit(solution)/shard_map/ppermute | solution.py:402
  21.6 8.8 %collective-permute-start.12 = (f32[384,128]{1,0:T(8,128)S(1)}, f32[384,128]{1,0:T(8,128)S(1)}, u32[]{:S(2)}, u32[]{:S(2)}) collective-permute-start(f32[384,128]{1,0:T(8,128)S(1)} %get-tuple-element.38), channel_id=1, source_target_pairs={{0,24},{4,28},{8,16},{12,20},{16,8},{20,12},{24,0},{28,4},{1,25},{... | collective-permute-start | bytes 589832 | tf_op jit(solution)/shard_map/ppermute | solution.py:402
  23.3 29.7 %copy-start = (f32[64,3,3,128]{3,0,2,1:T(8,128)S(1)}, f32[64,3,3,128]{3,0,2,1:T(8,128)}, u32[]{:S(2)}) copy-start(f32[64,3,3,128]{3,0,2,1:T(8,128)} %param.6) | copy-start | bytes 884740
  23.3 29.7 %copy-start.1 = (f32[64,3,3,128]{3,0,2,1:T(8,128)S(1)}, f32[64,3,3,128]{3,0,2,1:T(8,128)}, u32[]{:S(2)}) copy-start(f32[64,3,3,128]{3,0,2,1:T(8,128)} %param.7) | copy-start | bytes 884740
  23.3 11.3 %collective-permute-start.13 = (f32[384,128]{1,0:T(8,128)S(1)}, f32[384,128]{1,0:T(8,128)S(1)}, u32[]{:S(2)}, u32[]{:S(2)}) collective-permute-start(f32[384,128]{1,0:T(8,128)S(1)} %get-tuple-element.39), channel_id=1, source_target_pairs={{0,28},{4,24},{8,20},{12,16},{16,12},{20,8},{24,4},{28,0},{1,29},{... | collective-permute-start | bytes 589832 | tf_op jit(solution)/shard_map/ppermute | solution.py:402
  25.9 10.6 %collective-permute-start.3 = (f32[192,128]{1,0:T(8,128)S(1)}, f32[192,128]{1,0:T(8,128)S(1)}, u32[]{:S(2)}, u32[]{:S(2)}) collective-permute-start(f32[192,128]{1,0:T(8,128)S(1)} %get-tuple-element.28), channel_id=1, source_target_pairs={{0,16},{4,12},{8,24},{12,4},{16,0},{20,28},{24,8},{28,20},{1,17},{... | collective-permute-start | bytes 294920 | tf_op jit(solution)/shard_map/ppermute | solution.py:402
  27.4 9.3 %collective-permute-start.4 = (f32[192,128]{1,0:T(8,128)S(1)}, f32[192,128]{1,0:T(8,128)S(1)}, u32[]{:S(2)}, u32[]{:S(2)}) collective-permute-start(f32[192,128]{1,0:T(8,128)S(1)} %get-tuple-element.29), channel_id=1, source_target_pairs={{0,20},{4,8},{8,28},{12,0},{16,4},{20,24},{24,12},{28,16},{1,21},{... | collective-permute-start | bytes 294920 | tf_op jit(solution)/shard_map/ppermute | solution.py:402
  28.2 8.5 %collective-permute-start = (f32[192,128]{1,0:T(8,128)S(1)}, f32[192,128]{1,0:T(8,128)S(1)}, u32[]{:S(2)}, u32[]{:S(2)}) collective-permute-start(f32[192,128]{1,0:T(8,128)S(1)} %get-tuple-element.25), channel_id=1, source_target_pairs={{0,4},{4,0},{8,12},{12,8},{16,20},{20,16},{24,28},{28,24},{1,5},{5... | collective-permute-start | bytes 294920 | tf_op jit(solution)/shard_map/ppermute | solution.py:402
  30.4 6.6 %collective-permute-start.5 = (f32[192,128]{1,0:T(8,128)S(1)}, f32[192,128]{1,0:T(8,128)S(1)}, u32[]{:S(2)}, u32[]{:S(2)}) collective-permute-start(f32[192,128]{1,0:T(8,128)S(1)} %get-tuple-element.30), channel_id=1, source_target_pairs={{0,24},{4,28},{8,16},{12,20},{16,8},{20,12},{24,0},{28,4},{1,25},{... | collective-permute-start | bytes 294920 | tf_op jit(solution)/shard_map/ppermute | solution.py:402
  34.6 6.3 %collective-permute-start.6 = (f32[192,128]{1,0:T(8,128)S(1)}, f32[192,128]{1,0:T(8,128)S(1)}, u32[]{:S(2)}, u32[]{:S(2)}) collective-permute-start(f32[192,128]{1,0:T(8,128)S(1)} %get-tuple-element.31), channel_id=1, source_target_pairs={{0,28},{4,24},{8,20},{12,16},{16,12},{20,8},{24,4},{28,0},{1,29},{... | collective-permute-start | bytes 294920 | tf_op jit(solution)/shard_map/ppermute | solution.py:402

commit v7 on v6

--- a/solution.py
+++ b/solution.py
@@ -434,10 +434,10 @@
     near = near_out(near)
     far = held_blocks(av, gt, me, False, (0, 1))
     own, far = far_out(far)
+    tail = held_blocks(av, gt, me, False, (2,))
+    tail_own, tail = far_out(tail)
     rest = held_blocks(av, gt, me, True, (2,))
     rest = near_out(rest)
-    tail = held_blocks(av, gt, me, False, (2,))
-    tail_own, tail = far_out(tail)
     flips = [(0, 0), (1, 1), (2, 4), (5, 3), (4, 2), (3, 5), (6, 6), (7, 7)]
     arrays = own + near + far + tail_own + rest + tail
     split = near[0].shape[0]
@@ -449,8 +449,9 @@
 
     sums = gram([(0, split, pairs(0, 6))], pieces, arrays, [], me, flips, 0)
     sums = gram([(0, split, pairs(6, 8))], pieces, arrays, [sums], me, flips, 0)
-    sums = gram([(split, whole, pairs(0, 7))], pieces, arrays, [sums], me, flips, 0)
-    sums = gram([(split, whole, pairs(7, 8))], pieces, arrays, [sums], me, flips, devices)
+    late = [pair for pair in pairs(0, 8) if 4 in pair or 5 in pair]
+    sums = gram([(split, whole, [pair for pair in pairs(0, 8) if pair not in late])], pieces, arrays, [sums], me, flips, 0)
+    sums = gram([(split, whole, late)], pieces, arrays, [sums], me, flips, devices)
     return sums, pieces, arrays, flips
 
 

time: 54.3 us -> 54.4 us (level)
  waiting for transfers between devices: 9.01 us -> 7.72 us
  blocking collectives: 11.9 us -> 12.8 us
    ppermute x14, waiting for transfers between devices: 9.01 us -> 7.72 us  [send(): lax.ppermute(block, 'dp', [(r, r ^ flips[r % 2]) for r in range(parts)])]
    all_to_all x1, blocking collectives: 11.9 us -> 12.8 us  [shards(): lax.all_to_all(sums, ('dp', 'chan'), split_axis=0, concat_axis=0, tiled=T...]
  transfers between devices with their start and end apart: 14 -> 14, of which waited for: 7 -> 8; matrix products, arithmetic and copies ran while one was open for 0% -> 0% of each run, Pallas kernels for 16% -> 16%
where the time goes in v7:
time: 54.4 us; the launch traced here: 54.2 us
  Pallas kernels  16.8 us (31%)
  starting transfers between devices  16.2 us (30%)
  blocking collectives  12.8 us (24%)
  waiting for transfers between devices  7.72 us (14%)
  between operations  0.69 us (1%)
    ppermute x14, starting transfers between devices, send(): lax.ppermute(block, 'dp', [(r, r ^ flips[r % 2]) for r in range(parts)])  16.2 us
    all_to_all x1, blocking collectives, shards(): lax.all_to_all(sums, ('dp', 'chan'), split_axis=0, concat_axis=0, tiled=T...  12.8 us
    ppermute x14, waiting for transfers between devices, send(): lax.ppermute(block, 'dp', [(r, r ^ flips[r % 2]) for r in range(parts)])  7.72 us
    pallas_call x3, Pallas kernels, held_blocks(): pl.pallas_call(functools.partial(held_kernel, near, taps), out_shape=[blo...  7.39 us
    pallas_call x1, Pallas kernels, near_blocks(): pl.pallas_call(functools.partial(near_kernel, [height * n // 32 for n in...  6.91 us
    pallas_call x4, Pallas kernels, gram(): pl.pallas_call(functools.partial(gram_kernel, jobs, near, flips, devices)...  1.31 us
    pallas_call x1, Pallas kernels, finish(): pl.pallas_call(functools.partial(final_kernel, pieces, flips), out_shape=...  1.18 us
  transfers between devices with their start and end apart: 14, of which 8 were waited for; matrix products, arithmetic and copies ran while one was open for 0% of the time, Pallas kernels for 16%

profile of v7, /device:TPU:0, one launch (start us, length us, event | category | flops | bytes accessed | tf_op | source)
XLA Modules:
  0.0 54.2 jit_solution(1898317395696757117)
XLA Ops:
  0.6 6.9 %conv_near.1 = (f32[384,128]{1,0:T(8,128)S(1)}, f32[384,128]{1,0:T(8,128)S(1)}, f32[384,128]{1,0:T(8,128)S(1)}, f32[384,128]{1,0:T(8,128)S(1)}, bf16[32,8,32,512...) custom-call(s32[1]{0:T(128)} %bitcast.me_ref, bf16[8,32,32,128]{3,2,1,0:T(8,128)(2,1)} %g_hbm.1, ...), custom_call_target="tpu_custom_call" | custom-call | flops 3221225472 | bytes 10485760 | tf_op jit(solution)/shard_map/conv_near/pallas_call | solution.py:223
  7.5 3.0 %collective-permute-start.8 = (f32[384,128]{1,0:T(8,128)S(1)}, f32[384,128]{1,0:T(8,128)S(1)}, u32[]{:S(2)}, u32[]{:S(2)}) collective-permute-start(f32[384,128]{1,0:T(8,128)S(1)} %get-tuple-element.34), channel_id=1, source_target_pairs={{0,8},{4,20},{8,0},{12,28},{16,24},{20,4},{24,16},{28,12},{1,9},{5... | collective-permute-start | bytes 589832 | tf_op jit(solution)/shard_map/ppermute | solution.py:402
  10.6 0.7 %collective-permute-start.9 = (f32[384,128]{1,0:T(8,128)S(1)}, f32[384,128]{1,0:T(8,128)S(1)}, u32[]{:S(2)}, u32[]{:S(2)}) collective-permute-start(f32[384,128]{1,0:T(8,128)S(1)} %get-tuple-element.35), channel_id=1, source_target_pairs={{0,12},{4,16},{8,4},{12,24},{16,28},{20,0},{24,20},{28,8},{1,13},{... | collective-permute-start | bytes 589832 | tf_op jit(solution)/shard_map/ppermute | solution.py:402
  11.3 0.9 %collective-permute-start.10 = (f32[384,128]{1,0:T(8,128)S(1)}, f32[384,128]{1,0:T(8,128)S(1)}, u32[]{:S(2)}, u32[]{:S(2)}) collective-permute-start(f32[384,128]{1,0:T(8,128)S(1)} %get-tuple-element.36), channel_id=1, source_target_pairs={{0,16},{4,12},{8,24},{12,4},{16,0},{20,28},{24,8},{28,20},{1,17},{... | collective-permute-start | bytes 589832 | tf_op jit(solution)/shard_map/ppermute | solution.py:402
  12.1 1.9 %conv_near_rest.1 = (f32[192,128]{1,0:T(8,128)S(1)}, f32[192,128]{1,0:T(8,128)S(1)}, f32[192,128]{1,0:T(8,128)S(1)}, f32[192,128]{1,0:T(8,128)S(1)}) custom-call(s32[1]{0:T(128)} %bitcast.me_ref, bf16[384,8704]{1,0:T(8,128)(2,1)S(1)} %get-tuple-element.22.gt, bf16[32,8,32,512]{3,2,1,0:T(8,128)(2,1)S(1)} %get-tuple-element.23.av), custom_call_target="tpu_custom_call" | custom-call | flops 1610612736 | bytes 393216 | tf_op jit(solution)/shard_map/conv_near_rest/pallas_call | solution.py:246
  14.1 0.6 %collective-permute-start.1 = (f32[192,128]{1,0:T(8,128)S(1)}, f32[192,128]{1,0:T(8,128)S(1)}, u32[]{:S(2)}, u32[]{:S(2)}) collective-permute-start(f32[192,128]{1,0:T(8,128)S(1)} %get-tuple-element.26), channel_id=1, source_target_pairs={{0,8},{4,20},{8,0},{12,28},{16,24},{20,4},{24,16},{28,12},{1,9},{5... | collective-permute-start | bytes 294920 | tf_op jit(solution)/shard_map/ppermute | solution.py:402
  14.6 1.2 %collective-permute-start.2 = (f32[192,128]{1,0:T(8,128)S(1)}, f32[192,128]{1,0:T(8,128)S(1)}, u32[]{:S(2)}, u32[]{:S(2)}) collective-permute-start(f32[192,128]{1,0:T(8,128)S(1)} %get-tuple-element.27), channel_id=1, source_target_pairs={{0,12},{4,16},{8,4},{12,24},{16,28},{20,0},{24,20},{28,8},{1,13},{... | collective-permute-start | bytes 294920 | tf_op jit(solution)/shard_map/ppermute | solution.py:402
  15.8 3.6 %conv_far.3 = (f32[384,128]{1,0:T(8,128)S(1)}, f32[384,128]{1,0:T(8,128)S(1)}, f32[384,128]{1,0:T(8,128)S(1)}, f32[384,128]{1,0:T(8,128)S(1)}) custom-call(s32[1]{0:T(128)} %bitcast.me_ref, bf16[384,8704]{1,0:T(8,128)(2,1)S(1)} %get-tuple-element.22.gt, bf16[32,8,32,512]{3,2,1,0:T(8,128)(2,1)S(1)} %get-tuple-element.23.av), custom_call_target="tpu_custom_call" | custom-call | flops 3221225472 | bytes 786432 | tf_op jit(solution)/shard_map/conv_far/pallas_call | solution.py:246
  19.4 0.1 collective-permute-done.1.rest_2_.rest_10_
  19.5 0.5 collective-permute-start.11
  20.0 0.1 collective-permute-done.2.rest_3_.rest_11_
  20.1 1.5 %collective-permute-start.7 = (f32[384,128]{1,0:T(8,128)S(1)}, f32[384,128]{1,0:T(8,128)S(1)}, u32[]{:S(2)}, u32[]{:S(2)}) collective-permute-start(f32[384,128]{1,0:T(8,128)S(1)} %get-tuple-element.33), channel_id=1, source_target_pairs={{0,4},{4,0},{8,12},{12,8},{16,20},{20,16},{24,28},{28,24},{1,5},{5... | collective-permute-start | bytes 589832 | tf_op jit(solution)/shard_map/ppermute | solution.py:402
  21.6 0.0 collective-permute-done.8.rest_2_
  21.6 1.6 %collective-permute-start.12 = (f32[384,128]{1,0:T(8,128)S(1)}, f32[384,128]{1,0:T(8,128)S(1)}, u32[]{:S(2)}, u32[]{:S(2)}) collective-permute-start(f32[384,128]{1,0:T(8,128)S(1)} %get-tuple-element.38), channel_id=1, source_target_pairs={{0,24},{4,28},{8,16},{12,20},{16,8},{20,12},{24,0},{28,4},{1,25},{... | collective-permute-start | bytes 589832 | tf_op jit(solution)/shard_map/ppermute | solution.py:402
  23.3 0.0 collective-permute-done.9.rest_3_
  23.3 0.0 copy-start
  23.3 0.0 copy-start.1
  23.3 0.7 %collective-permute-start.13 = (f32[384,128]{1,0:T(8,128)S(1)}, f32[384,128]{1,0:T(8,128)S(1)}, u32[]{:S(2)}, u32[]{:S(2)}) collective-permute-start(f32[384,128]{1,0:T(8,128)S(1)} %get-tuple-element.39), channel_id=1, source_target_pairs={{0,28},{4,24},{8,20},{12,16},{16,12},{20,8},{24,4},{28,0},{1,29},{... | collective-permute-start | bytes 589832 | tf_op jit(solution)/shard_map/ppermute | solution.py:402
  24.0 1.9 %conv_far.2 = (f32[192,128]{1,0:T(8,128)S(1)}, f32[192,128]{1,0:T(8,128)S(1)}, f32[192,128]{1,0:T(8,128)S(1)}, f32[192,128]{1,0:T(8,128)S(1)}) custom-call(s32[1]{0:T(128)} %bitcast.me_ref, bf16[384,8704]{1,0:T(8,128)(2,1)S(1)} %get-tuple-element.22.gt, bf16[32,8,32,512]{3,2,1,0:T(8,128)(2,1)S(1)} %get-tuple-element.23.av), custom_call_target="tpu_custom_call" | custom-call | flops 1610612736 | bytes 393216 | tf_op jit(solution)/shard_map/conv_far/pallas_call | solution.py:246
  25.9 0.0 collective-permute-done.10.rest_4_
  25.9 0.8 %collective-permute-start = (f32[192,128]{1,0:T(8,128)S(1)}, f32[192,128]{1,0:T(8,128)S(1)}, u32[]{:S(2)}, u32[]{:S(2)}) collective-permute-start(f32[192,128]{1,0:T(8,128)S(1)} %get-tuple-element.25), channel_id=1, source_target_pairs={{0,4},{4,0},{8,12},{12,8},{16,20},{20,16},{24,28},{28,24},{1,5},{5... | collective-permute-start | bytes 294920 | tf_op jit(solution)/shard_map/ppermute | solution.py:402
  26.7 0.0 collective-permute-done.11.rest_5_
  26.7 1.7 %collective-permute-start.5 = (f32[192,128]{1,0:T(8,128)S(1)}, f32[192,128]{1,0:T(8,128)S(1)}, u32[]{:S(2)}, u32[]{:S(2)}) collective-permute-start(f32[192,128]{1,0:T(8,128)S(1)} %get-tuple-element.30), channel_id=1, source_target_pairs={{0,24},{4,28},{8,16},{12,20},{16,8},{20,12},{24,0},{28,4},{1,25},{... | collective-permute-start | bytes 294920 | tf_op jit(solution)/shard_map/ppermute | solution.py:402
  28.3 0.0 collective-permute-done.7.rest_1_
  28.3 0.7 %collective-permute-start.6 = (f32[192,128]{1,0:T(8,128)S(1)}, f32[192,128]{1,0:T(8,128)S(1)}, u32[]{:S(2)}, u32[]{:S(2)}) collective-permute-start(f32[192,128]{1,0:T(8,128)S(1)} %get-tuple-element.31), channel_id=1, source_target_pairs={{0,28},{4,24},{8,20},{12,16},{16,12},{20,8},{24,4},{28,0},{1,29},{... | collective-permute-start | bytes 294920 | tf_op jit(solution)/shard_map/ppermute | solution.py:402
  29.0 1.3 %collective-permute-done.12.rest_6_ = f32[384,128]{1,0:T(8,128)S(1)} collective-permute-done((f32[384,128]{1,0:T(8,128)S(1)}, f32[384,128]{1,0:T(8,128)S(1)}, u32[]{:S(2)}, u32[]{:S(2)}) %collective-permute-start.12) | collective-permute-done | bytes 196640 | tf_op jit(solution)/shard_map/ppermute | solution.py:402
  30.3 1.5 %collective-permute-start.3 = (f32[192,128]{1,0:T(8,128)S(1)}, f32[192,128]{1,0:T(8,128)S(1)}, u32[]{:S(2)}, u32[]{:S(2)}) collective-permute-start(f32[192,128]{1,0:T(8,128)S(1)} %get-tuple-element.28), channel_id=1, source_target_pairs={{0,16},{4,12},{8,24},{12,4},{16,0},{20,28},{24,8},{28,20},{1,17},{... | collective-permute-start | bytes 294920 | tf_op jit(solution)/shard_map/ppermute | solution.py:402
  31.8 2.8 %collective-permute-done.13.rest_7_ = f32[384,128]{1,0:T(8,128)S(1)} collective-permute-done((f32[384,128]{1,0:T(8,128)S(1)}, f32[384,128]{1,0:T(8,128)S(1)}, u32[]{:S(2)}, u32[]{:S(2)}) %collective-permute-start.13) | collective-permute-done | bytes 196640 | tf_op jit(solution)/shard_map/ppermute | solution.py:402
  34.5 0.9 %collective-permute-start.4 = (f32[192,128]{1,0:T(8,128)S(1)}, f32[192,128]{1,0:T(8,128)S(1)}, u32[]{:S(2)}, u32[]{:S(2)}) collective-permute-start(f32[192,128]{1,0:T(8,128)S(1)} %get-tuple-element.29), channel_id=1, source_target_pairs={{0,20},{4,8},{8,28},{12,0},{16,4},{20,24},{24,12},{28,16},{1,21},{... | collective-permute-start | bytes 294920 | tf_op jit(solution)/shard_map/ppermute | solution.py:402
  35.5 0.4 gram.4.rest_8_
  35.9 0.3 gram.5.rest_6_
  36.3 0.0 collective-permute-done.rest_1_.rest_9_
  36.3 0.5 collective-permute-done.5.rest_4_.rest_6_.rest_14_
  36.7 2.1 %collective-permute-done.6.rest_5_.rest_7_.rest_15_ = f32[192,128]{1,0:T(8,128)S(1)} collective-permute-done((f32[192,128]{1,0:T(8,128)S(1)}, f32[192,128]{1,0:T(8,128)S(1)}, u32[]{:S(2)}, u32[]{:S(2)}) %collective-permute-start.6) | collective-permute-done | bytes 98336 | tf_op jit(solution)/shard_map/ppermute | solution.py:402
  38.8 0.3 gram.6.rest_8_
  39.1 0.7 %collective-permute-done.3.rest_4_.rest_12_ = f32[192,128]{1,0:T(8,128)S(1)} collective-permute-done((f32[192,128]{1,0:T(8,128)S(1)}, f32[192,128]{1,0:T(8,128)S(1)}, u32[]{:S(2)}, u32[]{:S(2)}) %collective-permute-start.3) | collective-permute-done | bytes 98336 | tf_op jit(solution)/shard_map/ppermute | solution.py:402
  39.8 0.2 collective-permute-done.4.rest_5_.rest_13_
  40.0 0.2 gram.7
  40.2 12.8 %all_to_all.5.sums = f32[32,1,128]{2,1,0:T(1,128)S(1)} all-to-all(f32[32,1,128]{2,1,0:T(1,128)S(1)} %gram.7), channel_id=1, replica_groups=mesh['dp'=8,'chan'=4] {'dp','chan'}, dimensions={0} | all-to-all | bytes 32768 | tf_op jit(solution)/shard_map/all_to_all | solution.py:464
  53.0 0.0 copy-done
  53.0 0.0 copy-done.1
  53.0 1.2 %final.1 = (f32[576,128]{1,0:T(8,128)}, f32[576,128]{1,0:T(8,128)}) custom-call(s32[1]{0:T(128)} %bitcast.me_ref, f32[32,1,128]{2,1,0:T(1,128)S(1)} %all_to_all.5.sums, f32[576,128]{1,0:T(8,128)S(1)} %bitcast.13, f32[576,128]{1,0:T(8,128)S(1)} %bitcast.14, f32[384,128]{1,0:T(8,128)S(1)} %get-tuple-element.32.rest_0_, ...), custom_call_target="tpu_custom_call" | custom-call | flops 1179648 | bytes 3538944 | tf_op jit(solution)/shard_map/final/pallas_call | solution.py:384
Async XLA Ops:
  7.5 14.1 %collective-permute-start.8 = (f32[384,128]{1,0:T(8,128)S(1)}, f32[384,128]{1,0:T(8,128)S(1)}, u32[]{:S(2)}, u32[]{:S(2)}) collective-permute-start(f32[384,128]{1,0:T(8,128)S(1)} %get-tuple-element.34), channel_id=1, source_target_pairs={{0,8},{4,20},{8,0},{12,28},{16,24},{20,4},{24,16},{28,12},{1,9},{5... | collective-permute-start | bytes 589832 | tf_op jit(solution)/shard_map/ppermute | solution.py:402
  10.6 12.7 %collective-permute-start.9 = (f32[384,128]{1,0:T(8,128)S(1)}, f32[384,128]{1,0:T(8,128)S(1)}, u32[]{:S(2)}, u32[]{:S(2)}) collective-permute-start(f32[384,128]{1,0:T(8,128)S(1)} %get-tuple-element.35), channel_id=1, source_target_pairs={{0,12},{4,16},{8,4},{12,24},{16,28},{20,0},{24,20},{28,8},{1,13},{... | collective-permute-start | bytes 589832 | tf_op jit(solution)/shard_map/ppermute | solution.py:402
  11.3 14.6 %collective-permute-start.10 = (f32[384,128]{1,0:T(8,128)S(1)}, f32[384,128]{1,0:T(8,128)S(1)}, u32[]{:S(2)}, u32[]{:S(2)}) collective-permute-start(f32[384,128]{1,0:T(8,128)S(1)} %get-tuple-element.36), channel_id=1, source_target_pairs={{0,16},{4,12},{8,24},{12,4},{16,0},{20,28},{24,8},{28,20},{1,17},{... | collective-permute-start | bytes 589832 | tf_op jit(solution)/shard_map/ppermute | solution.py:402
  14.1 5.4 %collective-permute-start.1 = (f32[192,128]{1,0:T(8,128)S(1)}, f32[192,128]{1,0:T(8,128)S(1)}, u32[]{:S(2)}, u32[]{:S(2)}) collective-permute-start(f32[192,128]{1,0:T(8,128)S(1)} %get-tuple-element.26), channel_id=1, source_target_pairs={{0,8},{4,20},{8,0},{12,28},{16,24},{20,4},{24,16},{28,12},{1,9},{5... | collective-permute-start | bytes 294920 | tf_op jit(solution)/shard_map/ppermute | solution.py:402
  14.6 5.5 %collective-permute-start.2 = (f32[192,128]{1,0:T(8,128)S(1)}, f32[192,128]{1,0:T(8,128)S(1)}, u32[]{:S(2)}, u32[]{:S(2)}) collective-permute-start(f32[192,128]{1,0:T(8,128)S(1)} %get-tuple-element.27), channel_id=1, source_target_pairs={{0,12},{4,16},{8,4},{12,24},{16,28},{20,0},{24,20},{28,8},{1,13},{... | collective-permute-start | bytes 294920 | tf_op jit(solution)/shard_map/ppermute | solution.py:402
  19.5 7.2 %collective-permute-start.11 = (f32[384,128]{1,0:T(8,128)S(1)}, f32[384,128]{1,0:T(8,128)S(1)}, u32[]{:S(2)}, u32[]{:S(2)}) collective-permute-start(f32[384,128]{1,0:T(8,128)S(1)} %get-tuple-element.37), channel_id=1, source_target_pairs={{0,20},{4,8},{8,28},{12,0},{16,4},{20,24},{24,12},{28,16},{1,21},{... | collective-permute-start | bytes 589832 | tf_op jit(solution)/shard_map/ppermute | solution.py:402
  20.1 8.2 %collective-permute-start.7 = (f32[384,128]{1,0:T(8,128)S(1)}, f32[384,128]{1,0:T(8,128)S(1)}, u32[]{:S(2)}, u32[]{:S(2)}) collective-permute-start(f32[384,128]{1,0:T(8,128)S(1)} %get-tuple-element.33), channel_id=1, source_target_pairs={{0,4},{4,0},{8,12},{12,8},{16,20},{20,16},{24,28},{28,24},{1,5},{5... | collective-permute-start | bytes 589832 | tf_op jit(solution)/shard_map/ppermute | solution.py:402
  21.6 8.7 %collective-permute-start.12 = (f32[384,128]{1,0:T(8,128)S(1)}, f32[384,128]{1,0:T(8,128)S(1)}, u32[]{:S(2)}, u32[]{:S(2)}) collective-permute-start(f32[384,128]{1,0:T(8,128)S(1)} %get-tuple-element.38), channel_id=1, source_target_pairs={{0,24},{4,28},{8,16},{12,20},{16,8},{20,12},{24,0},{28,4},{1,25},{... | collective-permute-start | bytes 589832 | tf_op jit(solution)/shard_map/ppermute | solution.py:402
  23.3 29.7 %copy-start = (f32[64,3,3,128]{3,0,2,1:T(8,128)S(1)}, f32[64,3,3,128]{3,0,2,1:T(8,128)}, u32[]{:S(2)}) copy-start(f32[64,3,3,128]{3,0,2,1:T(8,128)} %param.6) | copy-start | bytes 884740
  23.3 29.7 %copy-start.1 = (f32[64,3,3,128]{3,0,2,1:T(8,128)S(1)}, f32[64,3,3,128]{3,0,2,1:T(8,128)}, u32[]{:S(2)}) copy-start(f32[64,3,3,128]{3,0,2,1:T(8,128)} %param.7) | copy-start | bytes 884740
  23.3 11.2 %collective-permute-start.13 = (f32[384,128]{1,0:T(8,128)S(1)}, f32[384,128]{1,0:T(8,128)S(1)}, u32[]{:S(2)}, u32[]{:S(2)}) collective-permute-start(f32[384,128]{1,0:T(8,128)S(1)} %get-tuple-element.39), channel_id=1, source_target_pairs={{0,28},{4,24},{8,20},{12,16},{16,12},{20,8},{24,4},{28,0},{1,29},{... | collective-permute-start | bytes 589832 | tf_op jit(solution)/shard_map/ppermute | solution.py:402
  25.9 10.4 %collective-permute-start = (f32[192,128]{1,0:T(8,128)S(1)}, f32[192,128]{1,0:T(8,128)S(1)}, u32[]{:S(2)}, u32[]{:S(2)}) collective-permute-start(f32[192,128]{1,0:T(8,128)S(1)} %get-tuple-element.25), channel_id=1, source_target_pairs={{0,4},{4,0},{8,12},{12,8},{16,20},{20,16},{24,28},{28,24},{1,5},{5... | collective-permute-start | bytes 294920 | tf_op jit(solution)/shard_map/ppermute | solution.py:402
  26.7 10.1 %collective-permute-start.5 = (f32[192,128]{1,0:T(8,128)S(1)}, f32[192,128]{1,0:T(8,128)S(1)}, u32[]{:S(2)}, u32[]{:S(2)}) collective-permute-start(f32[192,128]{1,0:T(8,128)S(1)} %get-tuple-element.30), channel_id=1, source_target_pairs={{0,24},{4,28},{8,16},{12,20},{16,8},{20,12},{24,0},{28,4},{1,25},{... | collective-permute-start | bytes 294920 | tf_op jit(solution)/shard_map/ppermute | solution.py:402
  28.3 10.5 %collective-permute-start.6 = (f32[192,128]{1,0:T(8,128)S(1)}, f32[192,128]{1,0:T(8,128)S(1)}, u32[]{:S(2)}, u32[]{:S(2)}) collective-permute-start(f32[192,128]{1,0:T(8,128)S(1)} %get-tuple-element.31), channel_id=1, source_target_pairs={{0,28},{4,24},{8,20},{12,16},{16,12},{20,8},{24,4},{28,0},{1,29},{... | collective-permute-start | bytes 294920 | tf_op jit(solution)/shard_map/ppermute | solution.py:402
  30.3 9.5 %collective-permute-start.3 = (f32[192,128]{1,0:T(8,128)S(1)}, f32[192,128]{1,0:T(8,128)S(1)}, u32[]{:S(2)}, u32[]{:S(2)}) collective-permute-start(f32[192,128]{1,0:T(8,128)S(1)} %get-tuple-element.28), channel_id=1, source_target_pairs={{0,16},{4,12},{8,24},{12,4},{16,0},{20,28},{24,8},{28,20},{1,17},{... | collective-permute-start | bytes 294920 | tf_op jit(solution)/shard_map/ppermute | solution.py:402
  34.5 5.4 %collective-permute-start.4 = (f32[192,128]{1,0:T(8,128)S(1)}, f32[192,128]{1,0:T(8,128)S(1)}, u32[]{:S(2)}, u32[]{:S(2)}) collective-permute-start(f32[192,128]{1,0:T(8,128)S(1)} %get-tuple-element.29), channel_id=1, source_target_pairs={{0,20},{4,8},{8,28},{12,0},{16,4},{20,24},{24,12},{28,16},{1,21},{... | collective-permute-start | bytes 294920 | tf_op jit(solution)/shard_map/ppermute | solution.py:402
